TPU v7x, 32 devices: a whole 2x2x4 slice. The times are simulated.
32 devices in a mesh: fsdp: 8 (over z, y), tp: 4 (over x, core).
Axes of the slice: x: 2, y: 2, z: 4, core: 2. Of those that a mesh axis runs over, the one named last changes fastest.
Arguments:
- hidden_in: bfloat16 [10240, 4096], P(('fsdp', 'tp')), may hold values from -6 to 6
- segment_ids: int32 [8, 1280], P('fsdp'), may hold values from 0 to 9, never falling along the last dimension, each value on 1 to 640 neighbouring positions
- qkv_weight: bfloat16 [4096, 3, 4096], P('fsdp', None, 'tp'), may hold values from -0.5 to 0.5
- out_weight: bfloat16 [4096, 4096], P('tp', 'fsdp'), may hold values from -0.375 to 0.375
- up_weight: bfloat16 [4096, 16384], P('fsdp', 'tp'), may hold values from -0.09375 to 0.09375
- down_weight: bfloat16 [16384, 4096], P('tp', 'fsdp'), may hold values from -0.046875 to 0.046875
- norm1_gain: bfloat16 [4096], P('fsdp'), may hold values from 0.25 to 1.75
- norm2_gain: bfloat16 [4096], P('fsdp'), may hold values from 0.25 to 1.75
- out_cotangent: bfloat16 [10240, 4096], P(('fsdp', 'tp')), may hold values from -6 to 6
Outputs:
- block_out: bfloat16 [10240, 4096], P(('fsdp', 'tp'))
- grad_in: float32 [10240, 4096], P(('fsdp', 'tp'))
- grad_norm1: float32 [4096], P(('fsdp', 'tp'))
- grad_norm2: float32 [4096], P(('fsdp', 'tp'))
- grad_qkv: float32 [4096, 3, 4096], P('fsdp', None, 'tp')
- grad_outproj: float32 [4096, 4096], P('tp', 'fsdp')
- grad_up: float32 [4096, 16384], P('fsdp', 'tp')
- grad_down: float32 [16384, 4096], P('tp', 'fsdp')
Inputs may be any that keep to these rules, and one draw needn't show every extreme that they name: `segment_ids`: along each sequence the numbers never fall; equal numbers mark one document of 1 to 640 positions, and one document of every sequence has 640.
All inputs are finite; a program needn't handle non-finite values.
Results may differ from a plain program's by a relative error of at most 0.015.
Values may be sent and summed in bfloat16 or wider, within the bound.
No kernel may reach another device: no remote copies, remote signals or barrier semaphores. Data moves between devices by JAX's collectives and lax.ppermute only.
A program may use at most 512 MiB of HBM per device.

v0:
```python
import math

import jax
import jax.numpy as jnp
from jax import lax
from jax.sharding import PartitionSpec as P

D = 4096
H = 32


NORM_EPSILON = 1e-05
SQRT_HALF = 0.7071067811865476
INV_ROOT_TWO_PI = 0.3989422804014327


def norm_forward(values_in):
    row_mean = jnp.mean(values_in, axis=-1, keepdims=True)
    centred = values_in - row_mean
    row_variance = jnp.mean(centred * centred, axis=-1, keepdims=True)
    inverse = lax.rsqrt(row_variance + NORM_EPSILON)
    return (centred * inverse, inverse)


def norm_backward(grad_out, normed, inverse, gain):
    grad_gain = jnp.sum(grad_out * normed, axis=0)
    scaled = grad_out * gain
    mean_one = jnp.mean(scaled, axis=-1, keepdims=True)
    mean_two = jnp.mean(scaled * normed, axis=-1, keepdims=True)
    return (inverse * (scaled - mean_one - normed * mean_two), grad_gain)


def gelu_value(pre_act):
    return 0.5 * pre_act * (1.0 + jax.scipy.special.erf(pre_act * SQRT_HALF))


def gelu_slope(pre_act):
    return (
        0.5 * (1.0 + jax.scipy.special.erf(pre_act * SQRT_HALF))
        + pre_act * jnp.exp(-0.5 * pre_act * pre_act) * INV_ROOT_TWO_PI
    )


def contract_rows(left, right):
    return lax.dot_general(
        left, right, (((0,), (0,)), ((), ())), preferred_element_type=jnp.float32
    )


def contract_columns(left, right):
    return lax.dot_general(
        left, right, (((1,), (1,)), ((), ())), preferred_element_type=jnp.float32
    )


def block_scores(
    query_block, keys_all, slopes, query_pos, key_pos, query_doc, key_doc, score_scale
):
    scores = jnp.einsum("qhd,khd->hqk", query_block, keys_all, preferred_element_type=jnp.float32)
    distance = (query_pos[:, None] - key_pos[None, :]).astype(jnp.float32)
    scores = scores * score_scale - slopes[:, None, None] * distance[None]
    allowed = (key_pos[None, :] <= query_pos[:, None]) & (query_doc[:, None] == key_doc[None, :])
    return jnp.where(allowed[None], scores, -1e30)


def unpack(group, local_width):
    w_qkv, w_out, w_up, w_down, gain_one, gain_two = group
    return (
        w_qkv.reshape(D, 3 * local_width),
        w_out,
        w_up,
        w_down,
        gain_one.astype(jnp.float32),
        gain_two.astype(jnp.float32),
    )


def on_device(
    hidden_in,
    segment_ids,
    qkv_weight,
    out_weight,
    up_weight,
    down_weight,
    norm1_gain,
    norm2_gain,
    out_cotangent,
):
    split_count = lax.axis_size("tp")
    split_index = lax.axis_index("tp")
    tok_rows = hidden_in.shape[0]
    sequence = tok_rows * split_count
    local_heads = H // split_count
    head_width = D // H
    local_width = local_heads * head_width
    blocks = max(1, sequence // 512)
    block_rows = sequence // blocks
    score_scale = 1.0 / math.sqrt(head_width)
    slopes = 2.0 ** (
        -8.0 * (split_index * local_heads + jnp.arange(local_heads) + 1).astype(jnp.float32) / H
    )
    positions = jnp.arange(sequence)
    document = segment_ids[0]
    gathered = (
        lax.all_gather(qkv_weight, "fsdp", axis=0, tiled=True),
        lax.all_gather(out_weight, "fsdp", axis=1, tiled=True),
        lax.all_gather(up_weight, "fsdp", axis=0, tiled=True),
        lax.all_gather(down_weight, "fsdp", axis=1, tiled=True),
        lax.all_gather(norm1_gain, "fsdp", axis=0, tiled=True),
        lax.all_gather(norm2_gain, "fsdp", axis=0, tiled=True),
    )
    w_qkv, w_out, w_up, w_down, gain_one, gain_two = unpack(gathered, local_width)
    hidden_f = hidden_in.astype(jnp.float32)
    normed_one, inverse_one = norm_forward(hidden_f)
    input_one = (normed_one * gain_one).astype(jnp.bfloat16)
    rows_one = lax.all_gather(input_one, "tp", axis=0, tiled=True)
    projected = jnp.dot(rows_one, w_qkv, preferred_element_type=jnp.float32).astype(jnp.bfloat16)
    projected = projected.reshape(sequence, 3, local_heads, head_width)
    queries = projected[:, 0]
    keys_all = projected[:, 1]
    values_all = projected[:, 2]
    out_blocks = []
    total_blocks = []
    for block_number in range(blocks):
        first = block_number * block_rows
        query_block = queries[first : first + block_rows]
        scores = block_scores(
            query_block,
            keys_all,
            slopes,
            positions[first : first + block_rows],
            positions,
            document[first : first + block_rows],
            document,
            score_scale,
        )
        row_peak = jnp.max(scores, axis=-1, keepdims=True)
        log_total = row_peak + jnp.log(jnp.sum(jnp.exp(scores - row_peak), axis=-1, keepdims=True))
        attn_probs = jnp.exp(scores - log_total).astype(jnp.bfloat16)
        out_blocks.append(
            jnp.einsum(
                "hqk,khd->qhd", attn_probs, values_all, preferred_element_type=jnp.float32
            ).astype(jnp.bfloat16)
        )
        total_blocks.append(log_total)
    attended = jnp.concatenate(out_blocks, axis=0).reshape(sequence, local_width)
    resid_one = hidden_f + lax.psum_scatter(
        jnp.dot(attended, w_out, preferred_element_type=jnp.float32),
        "tp",
        scatter_dimension=0,
        tiled=True,
    )
    normed_two, inverse_two = norm_forward(resid_one)
    input_two = (normed_two * gain_two).astype(jnp.bfloat16)
    rows_two = lax.all_gather(input_two, "tp", axis=0, tiled=True)
    pre_act = jnp.dot(rows_two, w_up, preferred_element_type=jnp.float32)
    activated = gelu_value(pre_act).astype(jnp.bfloat16)
    block_out = (
        resid_one
        + lax.psum_scatter(
            jnp.dot(activated, w_down, preferred_element_type=jnp.float32).astype(jnp.bfloat16),
            "tp",
            scatter_dimension=0,
            tiled=True,
        ).astype(jnp.float32)
    ).astype(jnp.bfloat16)
    again = (
        lax.all_gather(qkv_weight, "fsdp", axis=0, tiled=True),
        lax.all_gather(out_weight, "fsdp", axis=1, tiled=True),
        lax.all_gather(up_weight, "fsdp", axis=0, tiled=True),
        lax.all_gather(down_weight, "fsdp", axis=1, tiled=True),
        lax.all_gather(norm1_gain, "fsdp", axis=0, tiled=True),
        lax.all_gather(norm2_gain, "fsdp", axis=0, tiled=True),
    )
    w_qkv, w_out, w_up, w_down, gain_one, gain_two = unpack(again, local_width)
    cot_rows = lax.all_gather(out_cotangent, "tp", axis=0, tiled=True)
    grad_down = lax.psum_scatter(
        contract_rows(activated, cot_rows).astype(jnp.bfloat16),
        "fsdp",
        scatter_dimension=1,
        tiled=True,
    ).astype(jnp.float32)
    grad_act = contract_columns(cot_rows, w_down)
    grad_pre = (grad_act * gelu_slope(pre_act)).astype(jnp.bfloat16)
    grad_up = lax.psum_scatter(
        contract_rows(rows_two, grad_pre).astype(jnp.bfloat16),
        "fsdp",
        scatter_dimension=0,
        tiled=True,
    ).astype(jnp.float32)
    grad_in_two = lax.psum_scatter(
        contract_columns(grad_pre, w_up), "tp", scatter_dimension=0, tiled=True
    )
    grad_resid_part, grad_gain_two = norm_backward(grad_in_two, normed_two, inverse_two, gain_two)
    grad_resid = out_cotangent.astype(jnp.float32) + grad_resid_part
    grad_attn_rows = lax.all_gather(grad_resid.astype(jnp.bfloat16), "tp", axis=0, tiled=True)
    grad_out_part = contract_rows(attended, grad_attn_rows)
    grad_attended = contract_columns(grad_attn_rows, w_out).astype(jnp.bfloat16)
    grad_attended = grad_attended.reshape(sequence, local_heads, head_width)
    key_sum = jnp.zeros((sequence, local_heads, head_width), jnp.float32)
    value_sum = jnp.zeros((sequence, local_heads, head_width), jnp.float32)
    query_grads = []
    for block_number in range(blocks):
        first = block_number * block_rows
        query_block = queries[first : first + block_rows]
        grad_block = grad_attended[first : first + block_rows]
        scores = block_scores(
            query_block,
            keys_all,
            slopes,
            positions[first : first + block_rows],
            positions,
            document[first : first + block_rows],
            document,
            score_scale,
        )
        prob_full = jnp.exp(scores - total_blocks[block_number])
        attn_probs = prob_full.astype(jnp.bfloat16)
        grad_probs = jnp.einsum(
            "qhd,khd->hqk", grad_block, values_all, preferred_element_type=jnp.float32
        )
        row_dot = jnp.sum(prob_full * grad_probs, axis=-1, keepdims=True)
        grad_scores = (prob_full * (grad_probs - row_dot) * score_scale).astype(jnp.bfloat16)
        query_grads.append(
            jnp.einsum(
                "hqk,khd->qhd", grad_scores, keys_all, preferred_element_type=jnp.float32
            ).astype(jnp.bfloat16)
        )
        key_sum = key_sum + jnp.einsum(
            "hqk,qhd->khd", grad_scores, query_block, preferred_element_type=jnp.float32
        )
        value_sum = value_sum + jnp.einsum(
            "hqk,qhd->khd", attn_probs, grad_block, preferred_element_type=jnp.float32
        )
    grad_proj = jnp.stack(
        [
            jnp.concatenate(query_grads, axis=0),
            key_sum.astype(jnp.bfloat16),
            value_sum.astype(jnp.bfloat16),
        ],
        axis=1,
    ).reshape(sequence, 3 * local_width)
    grad_qkv_part = contract_rows(rows_one, grad_proj).reshape(D, 3, local_width)
    grad_qkv, grad_outproj = (
        lax.psum_scatter(
            grad_qkv_part.astype(jnp.bfloat16), "fsdp", scatter_dimension=0, tiled=True
        ).astype(jnp.float32),
        lax.psum_scatter(
            grad_out_part.astype(jnp.bfloat16), "fsdp", scatter_dimension=1, tiled=True
        ).astype(jnp.float32),
    )
    grad_in_one = lax.psum_scatter(
        contract_columns(grad_proj, w_qkv).astype(jnp.bfloat16),
        "tp",
        scatter_dimension=0,
        tiled=True,
    ).astype(jnp.float32)
    grad_hidden_part, grad_gain_one = norm_backward(grad_in_one, normed_one, inverse_one, gain_one)
    grad_in = grad_resid + grad_hidden_part
    grad_norm1, grad_norm2 = (
        lax.psum_scatter(grad_gain_one, ("fsdp", "tp"), scatter_dimension=0, tiled=True),
        lax.psum_scatter(grad_gain_two, ("fsdp", "tp"), scatter_dimension=0, tiled=True),
    )
    return (block_out, grad_in, grad_norm1, grad_norm2, grad_qkv, grad_outproj, grad_up, grad_down)


def solution(mesh):
    return jax.shard_map(
        on_device,
        mesh=mesh,
        in_specs=(
            P(("fsdp", "tp"), None),
            P("fsdp", None),
            P("fsdp", None, "tp"),
            P("tp", "fsdp"),
            P("fsdp", "tp"),
            P("tp", "fsdp"),
            P("fsdp"),
            P("fsdp"),
            P(("fsdp", "tp"), None),
        ),
        out_specs=(
            P(("fsdp", "tp"), None),
            P(("fsdp", "tp"), None),
            P(("fsdp", "tp")),
            P(("fsdp", "tp")),
            P("fsdp", None, "tp"),
            P("tp", "fsdp"),
            P("fsdp", "tp"),
            P("tp", "fsdp"),
        ),
        check_vma=False,
    )
```

profile of v0, /device:TPU:0, one launch (start us, length us, event | category | flops | bytes accessed | tf_op | source)
XLA Modules:
  0.0 4507.4 jit_solution(14487988804248074573)
XLA Ops:
  56.2 59.4 %all-gather.11.cloned.1.call-done = bf16[1280,4096]{1,0:T(8,128)(2,1)} async-done(((bf16[320,4096]{1,0:T(8,128)(2,1)}), bf16[1280,4096]{1,0:T(8,128)(2,1)}) %all-gather.11.cloned.1.call-update) | async-done | bytes 10485776 | tf_op jit(solution)/shard_map/all_gather | solution.py:116
  115.6 482.6 %all-gather.13.cloned.1.call-done = bf16[4096,3,1024]{0,2,1:T(8,128)(2,1)} async-done(((bf16[512,3,1024]{0,2,1:T(8,128)(2,1)}), bf16[4096,3,1024]{0,2,1:T(8,128)(2,1)}) %all-gather.13.cloned.1.call-update) | async-done | bytes 25165840 | tf_op jit(solution)/shard_map/all_gather | solution.py:105
  772.7 126.4 %reduce-scatter.9.cloned.1.call-done = f32[320,4096]{1,0:T(8,128)} async-done(((f32[1280,4096]{1,0:T(8,128)}), f32[320,4096]{1,0:T(8,128)}) %reduce-scatter.9.cloned.1.call-update) | async-done | bytes 5242896 | tf_op jit(solution)/shard_map/reduce_scatter | solution.py:147
  908.7 629.6 %all-gather.19.cloned.1.call-done = bf16[4096,4096]{1,0:T(8,128)(2,1)} async-done(((bf16[512,4096]{1,0:T(8,128)(2,1)}), bf16[4096,4096]{1,0:T(8,128)(2,1)}) %all-gather.19.cloned.1.call-update) | async-done | bytes 33554448 | tf_op jit(solution)/shard_map/all_gather | solution.py:107
  1538.3 72.3 %all-gather.17.cloned.1.call-done = bf16[1280,4096]{1,0:T(8,128)(2,1)} async-done(((bf16[320,4096]{1,0:T(8,128)(2,1)}), bf16[1280,4096]{1,0:T(8,128)(2,1)}) %all-gather.17.cloned.1.call-update) | async-done | bytes 10485776 | tf_op jit(solution)/shard_map/all_gather | solution.py:155
  1610.6 54.2 %multiply_convert_fusion.2 = (bf16[1280,4096]{1,0:T(8,128)(2,1)}, f32[1280,4096]{1,0:T(8,128)}) fusion(bf16[1280,4096]{1,0:T(8,128)(2,1)} %all-gather.17.cloned.1.call-done, bf16[4096,4096]{1,0:T(8,128)(2,1)} %all-gather.19.cloned.1.call-done), kind=kOutput, calls=%fused_computation.23 | convolution fusion | flops 42975887360 | bytes 75497472 | tf_op jit(solution)/shard_map/dot_general | solution.py:156
  1682.4 639.4 %all-gather.21.cloned.1.call-done = bf16[4096,4096]{1,0:T(8,128)(2,1)} async-done(((bf16[4096,512]{1,0:T(8,128)(2,1)}), bf16[4096,4096]{1,0:T(8,128)(2,1)}) %all-gather.21.cloned.1.call-update) | async-done | bytes 33554448 | tf_op jit(solution)/shard_map/all_gather | solution.py:108
  2321.8 58.6 %fusion.13 = bf16[1280,4096]{1,0:T(8,128)(2,1)} fusion(f32[1280,4096]{1,0:T(8,128)} %get-tuple-element.36, bf16[1280,4096]{1,0:T(8,128)(2,1)} %all-gather.23.cloned.1.call-done, bf16[4096,4096]{1,0:T(8,128)(2,1)} %all-gather.21.cloned.1.call-done), kind=kOutput, calls=%fused_computation.22 | convolution fusion | flops 43002101760 | bytes 75497472 | tf_op jit(solution)/shard_map/dot_general | solution.py:51
  2380.5 53.2 %fusion.117 = f32[1280,4096]{1,0:T(8,128)} fusion(bf16[1280,4096]{1,0:T(8,128)(2,1)} %fusion.13, bf16[4096,4096]{1,0:T(8,128)(2,1)} %all-gather.19.cloned.1.call-done), kind=kOutput, calls=%fused_computation.132 | convolution fusion | flops 42949672960 | bytes 65011712 | tf_op jit(solution)/shard_map/dot_general | solution.py:51
  2433.8 52.0 %convolution_convert_fusion.3 = bf16[1280,4096]{1,0:T(8,128)(2,1)} fusion(bf16[1280,4096]{1,0:T(8,128)(2,1)} %get-tuple-element.35, bf16[4096,4096]{1,0:T(8,128)(2,1)} %all-gather.21.cloned.1.call-done), kind=kOutput, calls=%fused_computation.28 | convolution fusion | flops 42954915840 | bytes 54525952 | tf_op jit(solution)/shard_map/dot_general | solution.py:161
  2485.8 101.1 %reduce-scatter.13.cloned.1.call-done = f32[320,4096]{1,0:T(8,128)} async-done(((f32[1280,4096]{1,0:T(8,128)}), f32[320,4096]{1,0:T(8,128)}) %reduce-scatter.13.cloned.1.call-update) | async-done | bytes 5242896 | tf_op jit(solution)/shard_map/reduce_scatter | solution.py:191
  2593.5 81.3 %reduce-scatter.11.cloned.1.call-done = bf16[320,4096]{1,0:T(8,128)(2,1)} async-done(((bf16[1280,4096]{1,0:T(8,128)(2,1)}), bf16[320,4096]{1,0:T(8,128)(2,1)}) %reduce-scatter.11.cloned.1.call-update) | async-done | bytes 2621456 | tf_op jit(solution)/shard_map/reduce_scatter | solution.py:160
  2683.4 52.9 %convolution_convert_fusion.1 = bf16[4096,4096]{1,0:T(8,128)(2,1)} fusion(bf16[1280,4096]{1,0:T(8,128)(2,1)} %all-gather.17.cloned.1.call-done, bf16[1280,4096]{1,0:T(8,128)(2,1)} %fusion.13), kind=kOutput, calls=%fused_computation.4 | convolution fusion | flops 42966450176 | bytes 54525952 | tf_op jit(solution)/shard_map/dot_general | solution.py:45
  2736.4 53.1 %convolution_convert_fusion = bf16[4096,4096]{1,0:T(8,128)(2,1)} fusion(bf16[1280,4096]{1,0:T(8,128)(2,1)} %get-tuple-element.35, bf16[1280,4096]{1,0:T(8,128)(2,1)} %all-gather.23.cloned.1.call-done), kind=kOutput, calls=%fused_computation.3 | convolution fusion | flops 42966450176 | bytes 54525952 | tf_op jit(solution)/shard_map/dot_general | solution.py:45
  2838.7 46.9 %fusion.88 = bf16[640,8,128]{0,2,1:T(8,128)(2,1)} fusion(f32[8,640,1280]{2,1,0:T(8,128)} %fusion.63, f32[8,640,1280]{2,1,0:T(8,128)} %get-tuple-element.32, f32[8,640]{1,0:T(8,128)S(1)} %copy-done.25, bf16[1280,1,8,128]{3,2,1,0:T(8,128)(2,1)} %get-tuple-element.25), kind=kOutput, calls=%fused_computation.96 | convolution fusion | flops 1724258560 | bytes 56381440 | tf_op jit(solution)/shard_map/hqk,khd->qhd/dot_general | solution.py:225
  2897.9 46.8 %fusion.85 = bf16[640,8,128]{0,2,1:T(8,128)(2,1)} fusion(f32[8,640,1280]{2,1,0:T(8,128)} %fusion.65, f32[8,640,1280]{2,1,0:T(8,128)} %get-tuple-element.34, f32[8,640]{1,0:T(8,128)S(1)} %copy-done.27, bf16[1280,1,8,128]{3,2,1,0:T(8,128)(2,1)} %get-tuple-element.25), kind=kOutput, calls=%fused_computation.95 | convolution fusion | flops 1724258560 | bytes 56381440 | tf_op jit(solution)/shard_map/hqk,khd->qhd/dot_general | solution.py:225
  2947.8 53.2 %fusion.19 = f32[8,128,1280]{2,1,0:T(8,128)} fusion(f32[8,640,1280]{2,1,0:T(8,128)} %fusion.65, f32[8,640,1280]{2,1,0:T(8,128)} %get-tuple-element.34, f32[8,640]{1,0:T(8,128)S(1)} %copy-done.27, bf16[640,1,8,128]{3,2,1,0:T(8,128)(2,1)S(1)} %copy-done.18), kind=kOutput, calls=%fused_computation.33 | convolution fusion | flops 1723603200 | bytes 59002880 | tf_op jit(solution)/shard_map/hqk,qhd->khd/dot_general | solution.py:229
  3001.1 54.9 %fusion.60 = bf16[1280,1,8,128]{0,3,2,1:T(8,128)(2,1)} fusion(f32[8,128,1280]{2,1,0:T(8,128)} %fusion.19, f32[8,640,1280]{2,1,0:T(8,128)} %fusion.63, f32[8,640,1280]{2,1,0:T(8,128)} %get-tuple-element.32, f32[8,640]{1,0:T(8,128)S(1)} %copy-done.25, bf16[640,1,8,128]{3,2,1,0:T(8,128)(2,1)S(1)} %copy-done.16), kind=kOutput, calls=%fused_computation.81 | convolution fusion | flops 1726224640 | bytes 61624320 | tf_op jit(solution)/shard_map/hqk,qhd->khd/dot_general | solution.py:229
  3164.7 136.0 %reduce-scatter.21.cloned.1.call-done = bf16[512,4096]{1,0:T(8,128)(2,1)} async-done(((bf16[4096,4096]{1,0:T(8,128)(2,1)}), bf16[512,4096]{1,0:T(8,128)(2,1)}) %reduce-scatter.21.cloned.1.call-update) | async-done | bytes 4194320 | tf_op jit(solution)/shard_map/reduce_scatter | solution.py:185
  3307.5 539.1 %reduce-scatter.23.cloned.1.call-done = bf16[4096,512]{1,0:T(8,128)(2,1)} async-done(((bf16[4096,4096]{1,0:T(8,128)(2,1)}), bf16[4096,512]{1,0:T(8,128)(2,1)}) %reduce-scatter.23.cloned.1.call-update) | async-done | bytes 4194320 | tf_op jit(solution)/shard_map/reduce_scatter | solution.py:177
  3853.4 145.3 %reduce-scatter.19.cloned.1.call-done = bf16[1024,512]{1,0:T(8,128)(2,1)} async-done(((bf16[1024,4096]{1,0:T(8,128)(2,1)}), bf16[1024,512]{1,0:T(8,128)(2,1)}) %reduce-scatter.19.cloned.1.call-update) | async-done | bytes 1048592 | tf_op jit(solution)/shard_map/reduce_scatter | solution.py:248
  4001.5 84.1 %reduce-scatter.15.cloned.1.call-done = bf16[320,4096]{1,0:T(8,128)(2,1)} async-done(((bf16[1280,4096]{1,0:T(8,128)(2,1)}), bf16[320,4096]{1,0:T(8,128)(2,1)}) %reduce-scatter.15.cloned.1.call-update) | async-done | bytes 2621456 | tf_op jit(solution)/shard_map/reduce_scatter | solution.py:252
  4089.7 43.8 all-reduce.2
  4140.7 354.6 %reduce-scatter.17.cloned.1.call-done = bf16[512,3,1024]{2,0,1:T(8,128)(2,1)} async-done(((bf16[4096,3,1024]{2,0,1:T(8,128)(2,1)}), bf16[512,3,1024]{2,0,1:T(8,128)(2,1)}) %reduce-scatter.17.cloned.1.call-update) | async-done | bytes 3145744 | tf_op jit(solution)/shard_map/reduce_scatter | solution.py:245
  (177 shorter events, 471.8 us)
Async XLA Ops:
  7.2 108.4 %all-gather.11.cloned.1.call-start = ((), (), s32[]{:S(2)}) async-start(), calls=%async_computation.8 | async-start | bytes 13107200 | tf_op jit(solution)/shard_map/all_gather | solution.py:116
  45.8 552.4 %all-gather.13.cloned.1.call-start = ((), (), s32[]{:S(2)}) async-start(), calls=%async_computation.9 | async-start | bytes 28311552 | tf_op jit(solution)/shard_map/all_gather | solution.py:105
  48.8 678.6 %all-gather.15.cloned.1.call-start = ((), (), s32[]{:S(2)}) async-start(), calls=%async_computation.10 | async-start | bytes 9437184 | tf_op jit(solution)/shard_map/all_gather | solution.py:106
  49.6 849.5 %reduce-scatter.9.cloned.1.call-start = ((), (), s32[]{:S(2)}) async-start(), calls=%async_computation.11 | async-start | bytes 26214400 | tf_op jit(solution)/shard_map/reduce_scatter | solution.py:147
  745.8 153.3 %copy-start.1 = (bf16[320,4096]{1,0:T(8,128)(2,1)S(1)}, bf16[320,4096]{1,0:T(8,128)(2,1)}, u32[]{:S(2)}) copy-start(bf16[320,4096]{1,0:T(8,128)(2,1)} %param.9) | copy-start | bytes 7864324
  745.8 792.5 %all-gather.19.cloned.1.call-start = ((), (), s32[]{:S(2)}) async-start(), calls=%async_computation.13 | async-start | bytes 37748736 | tf_op jit(solution)/shard_map/all_gather | solution.py:107
  746.4 864.2 %all-gather.17.cloned.1.call-start = ((), (), s32[]{:S(2)}) async-start(), calls=%async_computation.12 | async-start | bytes 13107200 | tf_op jit(solution)/shard_map/all_gather | solution.py:155
  772.7 130.2 %copy-start.22 = (f32[8,1,512]{2,1,0:T(1,128)}, f32[8,1,512]{2,1,0:T(1,128)S(1)}, u32[]{:S(2)}) copy-start(f32[8,1,512]{2,1,0:T(1,128)S(1)} %convert_element_type.191) | copy-start | bytes 49156
  907.2 775.3 %all-gather.23.cloned.1.call-start = ((), (), s32[]{:S(2)}) async-start(), calls=%async_computation.16 | async-start | bytes 13107200 | tf_op jit(solution)/shard_map/all_gather | solution.py:176
  907.9 1413.9 %all-gather.21.cloned.1.call-start = ((), (), s32[]{:S(2)}) async-start(), calls=%async_computation.14 | async-start | bytes 37748736 | tf_op jit(solution)/shard_map/all_gather | solution.py:108
  908.7 1678.3 %reduce-scatter.13.cloned.1.call-start = ((), (), s32[]{:S(2)}) async-start(), calls=%async_computation.17 | async-start | bytes 26214400 | tf_op jit(solution)/shard_map/reduce_scatter | solution.py:191
  2433.7 241.0 %reduce-scatter.11.cloned.1.call-start = ((), (), s32[]{:S(2)}) async-start(), calls=%async_computation.15 | async-start | bytes 13107200 | tf_op jit(solution)/shard_map/reduce_scatter | solution.py:160
  2485.8 189.0 %copy-start.8 = (bf16[320,4096]{1,0:T(8,128)(2,1)S(1)}, bf16[320,4096]{1,0:T(8,128)(2,1)}, u32[]{:S(2)}) copy-start(bf16[320,4096]{1,0:T(8,128)(2,1)} %param.17) | copy-start | bytes 7864324
  2485.8 303.7 %all-gather.25.cloned.1.call-start = ((), (), s32[]{:S(2)}) async-start(), calls=%async_computation.18 | async-start | bytes 13107200 | tf_op jit(solution)/shard_map/all_gather | solution.py:196
  2683.3 617.4 %reduce-scatter.21.cloned.1.call-start = ((), (), s32[]{:S(2)}) async-start(), calls=%async_computation.22 | async-start | bytes 37748736 | tf_op jit(solution)/shard_map/reduce_scatter | solution.py:185
  2736.3 1110.3 %reduce-scatter.23.cloned.1.call-start = ((), (), s32[]{:S(2)}) async-start(), calls=%async_computation.23 | async-start | bytes 37748736 | tf_op jit(solution)/shard_map/reduce_scatter | solution.py:177
  2789.4 1209.2 %reduce-scatter.19.cloned.1.call-start = ((), (), s32[]{:S(2)}) async-start(), calls=%async_computation.21 | async-start | bytes 9437184 | tf_op jit(solution)/shard_map/reduce_scatter | solution.py:248
  2808.7 1276.9 %reduce-scatter.15.cloned.1.call-start = ((), (), s32[]{:S(2)}) async-start(), calls=%async_computation.19 | async-start | bytes 13107200 | tf_op jit(solution)/shard_map/reduce_scatter | solution.py:252
  3124.3 1371.0 %reduce-scatter.17.cloned.1.call-start = ((), (), s32[]{:S(2)}) async-start(), calls=%async_computation.20 | async-start | bytes 28311552 | tf_op jit(solution)/shard_map/reduce_scatter | solution.py:245
  3307.4 778.2 %copy-start.2 = (bf16[320,4096]{1,0:T(8,128)(2,1)S(1)}, bf16[320,4096]{1,0:T(8,128)(2,1)}, u32[]{:S(2)}) copy-start(bf16[320,4096]{1,0:T(8,128)(2,1)} %param.9) | copy-start | bytes 7864324
  3307.4 778.2 %copy-start.21 = (f32[8,1,512]{2,1,0:T(1,128)S(1)}, f32[8,1,512]{2,1,0:T(1,128)}, u32[]{:S(2)}) copy-start(f32[8,1,512]{2,1,0:T(1,128)} %copy-done.20) | copy-start | bytes 49156
  3307.4 778.2 %copy-start.30 = (f32[320]{0:T(512)S(1)}, f32[320]{0:T(512)}, u32[]{:S(2)}) copy-start(f32[320]{0:T(512)} %copy-done.29) | copy-start | bytes 3844
  3307.4 778.2 %copy-start.34 = (f32[320]{0:T(512)S(1)}, f32[320]{0:T(512)}, u32[]{:S(2)}) copy-start(f32[320]{0:T(512)} %copy-done.33) | copy-start | bytes 3844
  3307.5 782.3 %copy-start.28 = (f32[4096]{0:T(1024)S(1)}, f32[4096]{0:T(1024)}, u32[]{:S(2)}) copy-start(f32[4096]{0:T(1024)} %get-tuple-element.8) | copy-start | bytes 49156
  (31 other events, 742.7 us)
Sparse Core Ops, SparseCore 0:
  45.9 69.6 all-gather.10
  117.7 480.4 all-gather.12
  600.3 125.3 all-gather.14
  745.9 153.1 reduce-scatter.8
  900.5 637.7 all-gather.18
  1540.4 70.1 all-gather.16
  1612.2 70.1 all-gather.22
  1684.0 637.7 all-gather.20
  2433.8 153.0 reduce-scatter.12
  2589.4 85.3 reduce-scatter.10
  2683.5 70.1 all-gather.24
  2757.3 543.4 reduce-scatter.20
  3304.5 542.0 reduce-scatter.22
  3850.1 148.5 reduce-scatter.18
  4001.3 84.2 reduce-scatter.14
  4089.9 405.3 reduce-scatter.16
where the time goes:
time: 4510 us
  waiting for transfers between devices  3470 us (77%)
  matrix products  795 us (18%)
  blocking collectives  98 us (2%)
  other arithmetic  96.2 us (2%)
    all_gather x1, waiting for transfers between devices, on_device(): lax.all_gather(down_weight, 'fsdp', axis=1, tiled=True)  639 us
    all_gather x1, waiting for transfers between devices, on_device(): lax.all_gather(up_weight, 'fsdp', axis=0, tiled=True)  630 us
    reduce_scatter x1, waiting for transfers between devices, on_device(): lax.psum_scatter(contract_rows(activated, cot_rows).astype(jnp.bfloat16),...  539 us
    all_gather x1, waiting for transfers between devices, on_device(): lax.all_gather(qkv_weight, 'fsdp', axis=0, tiled=True)  483 us
    reduce_scatter x1, waiting for transfers between devices, on_device(): lax.psum_scatter(grad_qkv_part.astype(jnp.bfloat16), 'fsdp', scatter_dime...  355 us
    dot_general x4, matrix products, contract_columns(): lax.dot_general(left, right, (((1,), (1,)), ((), ())), preferred_element_...  167 us
    dot_general x4, matrix products, contract_rows(): lax.dot_general(left, right, (((0,), (0,)), ((), ())), preferred_element_...  164 us
    reduce_scatter x1, waiting for transfers between devices, on_device(): lax.psum_scatter(grad_out_part.astype(jnp.bfloat16), 'fsdp', scatter_dime...  145 us
  transfers between devices with their start and end apart: 16, of which 14 were waited for; matrix products, arithmetic and copies ran while one was open for 17% of the time, Pallas kernels for 0%

commit v1 on v0

v1 whole, which is shorter than its diff:
```python
import math

import jax
import jax.numpy as jnp
from jax import lax
from jax.experimental import pallas as pl
from jax.experimental.pallas import tpu as pltpu
from jax.sharding import PartitionSpec as P

D = 4096
H = 32
HEAD = D // H
REACH = 640
NORM_EPSILON = 1e-05
SQRT_HALF = 0.7071067811865476
INV_ROOT_TWO_PI = 0.3989422804014327
BF = jnp.bfloat16
F32 = jnp.float32


def norm_forward(values_in):
    row_mean = jnp.mean(values_in, axis=-1, keepdims=True)
    centred = values_in - row_mean
    row_variance = jnp.mean(centred * centred, axis=-1, keepdims=True)
    inverse = lax.rsqrt(row_variance + NORM_EPSILON)
    return centred * inverse, inverse


def norm_backward(grad_out, normed, inverse, gain):
    grad_gain = jnp.sum(grad_out * normed, axis=0)
    scaled = grad_out * gain
    mean_one = jnp.mean(scaled, axis=-1, keepdims=True)
    mean_two = jnp.mean(scaled * normed, axis=-1, keepdims=True)
    return inverse * (scaled - mean_one - normed * mean_two), grad_gain


def gelu_value(pre_act):
    return 0.5 * pre_act * (1.0 + jax.scipy.special.erf(pre_act * SQRT_HALF))


def gelu_slope(pre_act):
    return (
        0.5 * (1.0 + jax.scipy.special.erf(pre_act * SQRT_HALF))
        + pre_act * jnp.exp(-0.5 * pre_act * pre_act) * INV_ROOT_TWO_PI
    )


def dot(left, right, cl, cr):
    return lax.dot_general(left, right, (((cl,), (cr,)), ((), ())), preferred_element_type=F32)


QB = 256


def window(first):
    low = max(0, first - REACH)
    return low, first + QB - low


def masked_scores(q, k, start, slope, first, low, width, scale):
    scores = dot(q, k, 1, 1)
    row = first + lax.broadcasted_iota(jnp.int32, (QB, width), 0)
    col = low + lax.broadcasted_iota(jnp.int32, (QB, width), 1)
    scores = scores * scale - slope * (row - col).astype(F32)
    return jnp.where((col >= start) & (col <= row), scores, -1e30)


def load_ordered(ref, scratches, turn, piece):
    for i in range(4):
        rel = lax.bitwise_xor(jnp.int32(i), turn)
        block = ref[lax.bitwise_and(rel, 1), 0, lax.shift_right_logical(rel, 1)]
        for j, scratch in enumerate(scratches):
            scratch[i * piece : (i + 1) * piece, :] = block[:, j * HEAD : (j + 1) * HEAD]


def attention_forward(turn_ref, slope_ref, qkv_ref, start_ref, o_ref, lse_ref, q_s, k_s, v_s, o_s):
    turn = turn_ref[0]
    slope = slope_ref[pl.program_id(1)]
    sequence = q_s.shape[0]
    piece = sequence // 4
    scale = 1.0 / math.sqrt(HEAD)
    load_ordered(qkv_ref, (q_s, k_s, v_s), turn, piece)
    for first in range(0, sequence, QB):
        low, width = window(first)
        scores = masked_scores(
            q_s[first : first + QB, :],
            k_s[low : low + width, :],
            start_ref[0, first : first + QB, :],
            slope,
            first,
            low,
            width,
            scale,
        )
        peak = jnp.max(scores, axis=-1, keepdims=True)
        weights = jnp.exp(scores - peak)
        total = jnp.sum(weights, axis=-1, keepdims=True)
        lse_ref[0, 0, first : first + QB, :] = peak + jnp.log(total)
        probs = (weights * (1.0 / total)).astype(BF)
        o_s[first : first + QB, :] = dot(probs, v_s[low : low + width, :], 1, 0).astype(BF)
    for i in range(4):
        rel = lax.bitwise_xor(jnp.int32(i), turn)
        o_ref[lax.bitwise_and(rel, 1), 0, lax.shift_right_logical(rel, 1)] = o_s[
            i * piece : (i + 1) * piece, :
        ]


def attention_backward(
    turn_ref, slope_ref, qkv_ref, do_ref, start_ref, lse_ref, out_ref, q_s, k_s, v_s, do_s, dq_s, dk_s, dv_s
):
    turn = turn_ref[0]
    slope = slope_ref[pl.program_id(1)]
    sequence = q_s.shape[0]
    piece = sequence // 4
    scale = 1.0 / math.sqrt(HEAD)
    load_ordered(qkv_ref, (q_s, k_s, v_s), turn, piece)
    load_ordered(do_ref, (do_s,), turn, piece)
    dk_s[...] = jnp.zeros_like(dk_s)
    dv_s[...] = jnp.zeros_like(dv_s)
    for first in range(0, sequence, QB):
        low, width = window(first)
        keys = k_s[low : low + width, :]
        query = q_s[first : first + QB, :]
        grad = do_s[first : first + QB, :]
        scores = masked_scores(
            query, keys, start_ref[0, first : first + QB, :], slope, first, low, width, scale
        )
        probs = jnp.exp(scores - lse_ref[0, 0, first : first + QB, :])
        grad_probs = dot(grad, v_s[low : low + width, :], 1, 1)
        delta = jnp.sum(probs * grad_probs, axis=-1, keepdims=True)
        grad_scores = (probs * (grad_probs - delta) * scale).astype(BF)
        dq_s[first : first + QB, :] = dot(grad_scores, keys, 1, 0).astype(BF)
        dk_s[low : low + width, :] += dot(grad_scores, query, 0, 0)
        dv_s[low : low + width, :] += dot(probs.astype(BF), grad, 0, 0)
    for i in range(4):
        rel = lax.bitwise_xor(jnp.int32(i), turn)
        rows = slice(i * piece, (i + 1) * piece)
        at = (lax.bitwise_and(rel, 1), 0, lax.shift_right_logical(rel, 1))
        out_ref[(*at, slice(None), slice(0, HEAD))] = dq_s[rows, :]
        out_ref[(*at, slice(None), slice(HEAD, 2 * HEAD))] = dk_s[rows, :].astype(BF)
        out_ref[(*at, slice(None), slice(2 * HEAD, 3 * HEAD))] = dv_s[rows, :].astype(BF)


def on_device(
    hidden_in,
    segment_ids,
    qkv_weight,
    out_weight,
    up_weight,
    down_weight,
    norm1_gain,
    norm2_gain,
    out_cotangent,
):
    n = lax.axis_size("fsdp")
    tp = lax.axis_size("tp")
    ring = n // 4
    f = lax.axis_index("fsdp")
    t = lax.axis_index("tp")
    y, zl, zh = f & 1, (f >> 1) & 1, f >> 2
    low_half = zl == 0
    piece = hidden_in.shape[0]
    sequence = piece * tp
    heads = H // tp // 2
    width = heads * HEAD
    unit = D // n

    def over(axis, to, size):
        return lambda v: lax.ppermute(v, axis, [(i, to(i)) for i in range(size)])

    pp_core = over("tp", lambda i: i ^ 1, tp)
    pp_x = over("tp", lambda i: i ^ 2, tp)
    pp_zl = over("fsdp", lambda i: i ^ 2, n)
    pp_y = over("fsdp", lambda i: i ^ 1, n)
    pp_up = over("fsdp", lambda i: (i + 4) % n, n)
    pp_down = over("fsdp", lambda i: (i - 4) % n, n)

    def to_rel(v):
        cols = [v[..., b * unit : (b + 1) * unit] for b in range(n)]

        def pick(k, j, l):
            chosen = None
            for a in range(ring):
                both = jnp.where(y == j, cols[a * 4 + l * 2], cols[a * 4 + l * 2 + 1])
                chosen = both if chosen is None else jnp.where((zh - k) % ring == a, both, chosen)
            return chosen

        return jnp.concatenate(
            [pick(k, j, l) for k in range(ring) for j in range(2) for l in range(2)], axis=-1
        )

    def from_rel(v):
        cols = [v[..., b * unit : (b + 1) * unit] for b in range(n)]

        def pick(a, l, b):
            chosen = None
            for k in range(ring):
                both = jnp.where(y == b, cols[k * 4 + l], cols[k * 4 + 2 + l])
                chosen = both if chosen is None else jnp.where((zh - k) % ring == a, both, chosen)
            return chosen

        return jnp.concatenate(
            [pick(a, l, b) for a in range(ring) for l in range(2) for b in range(2)], axis=-1
        )

    def gather_blocks(block):
        chain = [block]
        for _ in range(ring - 1):
            chain.append(pp_up(chain[-1]))
        out = []
        for item in chain:
            out += [item, pp_y(item)]
        return out

    def gather_weight(mine, other, axis):
        blocks_mine = gather_blocks(mine)
        blocks_other = gather_blocks(pp_zl(other))
        cols = []
        for a, b in zip(blocks_mine, blocks_other):
            cols += [jnp.where(low_half, a, b), jnp.where(low_half, b, a)]
        return jnp.concatenate(cols, axis=axis)

    def reduce_weight(parts, axis):
        sums = [
            (parts[k][0].astype(F32) + pp_y(parts[k][1]).astype(F32)).astype(BF)
            for k in range(ring)
        ]
        value = sums[ring - 1]
        for k in range(ring - 2, -1, -1):
            value = (pp_down(value).astype(F32) + sums[k].astype(F32)).astype(BF)
        first, second = jnp.split(value, 2, axis=axis)
        keep = jnp.where(low_half, first, second)
        got = pp_zl(jnp.where(low_half, second, first))
        return keep, got

    def gather_rows(a):
        ax, az = pp_x(a), pp_zl(a)
        half = piece // 2
        top = pp_x(az[:half])
        bottom = pp_zl(ax[half:])
        ad = jnp.concatenate([top, bottom], axis=0)
        same = [a, ax, az, ad]
        return jnp.concatenate(same + [pp_core(v) for v in same], axis=0)

    def scatter_rows(near, far):
        e = (near + pp_core(far.astype(BF)).astype(F32)).astype(BF)
        half = piece // 2
        e00 = e[:piece]
        ex = e[piece : 2 * piece]
        ez = e[2 * piece : 3 * piece]
        ed = e[3 * piece :]
        from_x = pp_x(ed[:half])
        from_z = pp_zl(ed[half:])
        x_top = pp_x(ex[:half])
        z_bottom = pp_zl(ez[half:])
        x_bottom = pp_x((ex[half:].astype(F32) + from_z.astype(F32)).astype(BF))
        z_top = pp_zl((ez[:half].astype(F32) + from_x.astype(F32)).astype(BF))
        x_all = jnp.concatenate([x_top, x_bottom], axis=0).astype(F32)
        z_all = jnp.concatenate([z_top, z_bottom], axis=0).astype(F32)
        return e00.astype(F32) + x_all + z_all

    def rows_out(a, b, cl, cr):
        half = a.shape[0] // 2
        far = dot(a[half:], b, cl, cr)
        near = dot(a[:half], b, cl, cr)
        return scatter_rows(near, far)

    def halves(v, axis):
        first, second = jnp.split(v, 2, axis=axis)
        return jnp.where(low_half, first, second), jnp.where(low_half, second, first)

    qkv_heads = (
        qkv_weight.reshape(unit, 3, 2 * heads, HEAD)
        .transpose(0, 2, 1, 3)
        .reshape(unit, 2 * heads * 3 * HEAD)
    )
    w_qkv = gather_weight(*halves(qkv_heads, 1), 0)
    w_out = gather_weight(*halves(out_weight, 0), 1)
    w_up = gather_weight(*halves(up_weight, 1), 0)
    w_down = gather_weight(*halves(down_weight, 0), 1)

    gains = jnp.stack([norm1_gain, norm2_gain])
    gains = gather_weight(gains, gains, 1).astype(F32)
    gain_one, gain_two = gains[0], gains[1]

    documents = jnp.concatenate([segment_ids, pp_zl(segment_ids)], axis=0)
    starts = jnp.sum(
        (documents[:, None, :] < documents[:, :, None]).astype(jnp.int32), axis=-1
    )[:, :, None]
    turn = jnp.full((1,), t, jnp.int32)
    head_index = t * 2 * heads + zl * heads + jnp.arange(heads)
    slopes = 2.0 ** (-8.0 * (head_index + 1).astype(F32) / H)

    x = to_rel(hidden_in).astype(F32)
    cot = to_rel(out_cotangent)
    normed_one, inverse_one = norm_forward(x)
    rows_one = gather_rows((normed_one * gain_one).astype(BF))
    qkv = dot(rows_one, w_qkv, 1, 0).astype(BF).reshape(2, 2, 2, piece, 3 * width)

    def spec(cols):
        return pl.BlockSpec((2, 1, 2, piece, cols), lambda s, h, *_: (0, s, 0, 0, h))

    start_spec = pl.BlockSpec((1, sequence, 1), lambda s, h, *_: (s, 0, 0))
    lse_spec = pl.BlockSpec((1, 1, sequence, 1), lambda s, h, *_: (s, h, 0, 0))
    params = pltpu.CompilerParams(
        dimension_semantics=("arbitrary", "arbitrary"), vmem_limit_bytes=48 << 20
    )
    block = pltpu.VMEM((sequence, HEAD), BF)
    wide = pltpu.VMEM((sequence, HEAD), F32)
    pairs = 2 * heads
    area = sum(QB * window(i)[1] for i in range(0, sequence, QB)) * pairs
    attended, lse = pl.pallas_call(
        attention_forward,
        out_shape=(
            jax.ShapeDtypeStruct((2, 2, 2, piece, width), BF),
            jax.ShapeDtypeStruct((2, heads, sequence, 1), F32),
        ),
        grid_spec=pltpu.PrefetchScalarGridSpec(
            num_scalar_prefetch=2,
            grid=(2, heads),
            in_specs=[spec(3 * HEAD), start_spec],
            out_specs=[spec(HEAD), lse_spec],
            scratch_shapes=[block] * 4,
        ),
        compiler_params=params,
        cost_estimate=pl.CostEstimate(
            flops=4 * HEAD * area, transcendentals=area, bytes_accessed=2 * sequence * HEAD * 4 * pairs
        ),
        name="attention_forward",
    )(turn, slopes, qkv, starts)
    attended = attended.reshape(2 * sequence, width)
    resid = x + rows_out(attended, w_out, 1, 0)
    normed_two, inverse_two = norm_forward(resid)
    rows_two = gather_rows((normed_two * gain_two).astype(BF))
    pre_act = dot(rows_two, w_up, 1, 0)
    activated = gelu_value(pre_act).astype(BF)
    block_out = from_rel((resid + rows_out(activated, w_down, 1, 0)).astype(BF))

    cot_rows = gather_rows(cot)

    def grad_parts(make):
        return [[make(slice((k * 2 + j) * 2 * unit, (k * 2 + j + 1) * 2 * unit)).astype(BF) for j in range(2)] for k in range(ring)]

    keep, got = reduce_weight(grad_parts(lambda c: dot(activated, cot_rows[:, c], 0, 0)), 1)

    def joined(keep, got, axis):
        return jnp.concatenate(
            [jnp.where(low_half, keep, got), jnp.where(low_half, got, keep)], axis=axis
        ).astype(F32)

    grad_down = joined(keep, got, 0)
    grad_act = dot(cot_rows, w_down, 1, 1)
    grad_pre = (grad_act * gelu_slope(pre_act)).astype(BF)
    grad_up = joined(*reduce_weight(grad_parts(lambda c: dot(rows_two[:, c], grad_pre, 0, 0)), 0), 1)
    grad_in_two = rows_out(grad_pre, w_up, 1, 1)
    grad_part, grad_gain_two = norm_backward(grad_in_two, normed_two, inverse_two, gain_two)
    grad_resid = cot.astype(F32) + grad_part
    grad_rows = gather_rows(grad_resid.astype(BF))
    grad_attended = dot(grad_rows, w_out, 1, 1).astype(BF).reshape(2, 2, 2, piece, width)
    grad_out = joined(*reduce_weight(grad_parts(lambda c: dot(attended, grad_rows[:, c], 0, 0)), 1), 0)
    grad_proj = pl.pallas_call(
        attention_backward,
        out_shape=jax.ShapeDtypeStruct((2, 2, 2, piece, 3 * width), BF),
        grid_spec=pltpu.PrefetchScalarGridSpec(
            num_scalar_prefetch=2,
            grid=(2, heads),
            in_specs=[spec(3 * HEAD), spec(HEAD), start_spec, lse_spec],
            out_specs=spec(3 * HEAD),
            scratch_shapes=[block] * 5 + [wide] * 2,
        ),
        compiler_params=params,
        cost_estimate=pl.CostEstimate(
            flops=10 * HEAD * area, transcendentals=area, bytes_accessed=2 * sequence * HEAD * 7 * pairs
        ),
        name="attention_backward",
    )(turn, slopes, qkv, grad_attended, starts, lse)
    grad_proj = grad_proj.reshape(2 * sequence, 3 * width)
    keep, got = reduce_weight(grad_parts(lambda c: dot(rows_one[:, c], grad_proj, 0, 0)), 0)

    def parts_first(v):
        return v.reshape(unit, heads, 3, HEAD).transpose(0, 2, 1, 3).reshape(unit, 3, width)

    grad_qkv = joined(parts_first(keep), parts_first(got), 2)
    grad_in_one = rows_out(grad_proj, w_qkv, 1, 1)
    grad_part, grad_gain_one = norm_backward(grad_in_one, normed_one, inverse_one, gain_one)
    grad_in = from_rel(grad_resid + grad_part)

    def total(v):
        v = from_rel(v)
        for step in (pp_core, pp_x, pp_zl, pp_y):
            v = v + step(v)
        moving = v
        for _ in range(ring - 1):
            moving = pp_up(moving)
            v = v + moving
        size = D // (n * tp)
        return lax.dynamic_slice_in_dim(v, (f * tp + t) * size, size)

    return (
        block_out,
        grad_in,
        total(grad_gain_one),
        total(grad_gain_two),
        grad_qkv,
        grad_out,
        grad_up,
        grad_down,
    )


def solution(mesh):
    return jax.shard_map(
        on_device,
        mesh=mesh,
        in_specs=(
            P(("fsdp", "tp"), None),
            P("fsdp", None),
            P("fsdp", None, "tp"),
            P("tp", "fsdp"),
            P("fsdp", "tp"),
            P("tp", "fsdp"),
            P("fsdp"),
            P("fsdp"),
            P(("fsdp", "tp"), None),
        ),
        out_specs=(
            P(("fsdp", "tp"), None),
            P(("fsdp", "tp"), None),
            P(("fsdp", "tp")),
            P(("fsdp", "tp")),
            P("fsdp", None, "tp"),
            P("tp", "fsdp"),
            P("fsdp", "tp"),
            P("tp", "fsdp"),
        ),
        check_vma=False,
    )
```

time: 4510 us -> 2840 us (0.63)
  waiting for transfers between devices: 3470 us -> 1780 us
  matrix products: 795 us -> 552 us
  starting transfers between devices: 0.82 us -> 114 us
  other arithmetic: 96.2 us -> 209 us
  blocking collectives: 98 us -> 0 us
  local copies, waits for them, and re-layouts: 31.3 us -> 115 us
  Pallas kernels: 0 us -> 65.9 us
    all_gather x8 -> x0, waiting for transfers between devices: 1900 us -> none  [the longest x1 639 us: on_device(): lax.all_gather(down_weight, 'fsdp', axis=1, tiled=True)]
    ppermute x0 -> x122, waiting for transfers between devices: none -> 1780 us  [over(): return lambda v: lax.ppermute(v, axis, [(i, to(i)) for i in range(size)])]
    reduce_scatter x8 -> x0, waiting for transfers between devices: 1570 us -> none  [the longest x1 539 us: on_device(): lax.psum_scatter(contract_rows(activated, cot_rows).astype(jnp.bfloat16),...]
    dot_general x24 -> x28, matrix products: 795 us -> 552 us  [dot(): lax.dot_general(left, right, (((cl,), (cr,)), ((), ())), preferred_elemen...]
    ppermute x0 -> x122, starting transfers between devices: none -> 114 us  [over(): return lambda v: lax.ppermute(v, axis, [(i, to(i)) for i in range(size)])]
    unnamed x1 -> x88, other arithmetic: 0.02 us -> 95.5 us
    pallas_call x0 -> x2, Pallas kernels: none -> 65.9 us  [the longest x1 37.3 us: on_device(): pl.pallas_call(attention_backward, out_shape=jax.ShapeDtypeStruct((2, 2,...]
    all_gather x2 -> x0, blocking collectives: 54.1 us -> none  [the longest x1 27.9 us: on_device(): lax.all_gather(norm1_gain, 'fsdp', axis=0, tiled=True)]
  transfers between devices with their start and end apart: 16 -> 122, of which waited for: 14 -> 54; matrix products, arithmetic and copies ran while one was open for 17% -> 19% of each run, Pallas kernels for 0% -> 1%
where the time goes in v1:
time: 2840 us; the launch traced here: 2830 us
  waiting for transfers between devices  1780 us (63%)
  matrix products  552 us (19%)
  other arithmetic  209 us (7%)
  local copies, waits for them, and re-layouts  115 us (4%)
  starting transfers between devices  114 us (4%)
  Pallas kernels  65.9 us (2%)
    ppermute x122, waiting for transfers between devices, over(): return lambda v: lax.ppermute(v, axis, [(i, to(i)) for i in range(size)])  1780 us
    dot_general x28, matrix products, dot(): lax.dot_general(left, right, (((cl,), (cr,)), ((), ())), preferred_elemen...  552 us
    ppermute x122, starting transfers between devices, over(): return lambda v: lax.ppermute(v, axis, [(i, to(i)) for i in range(size)])  114 us
    unnamed x88, other arithmetic  95.5 us
    unnamed x176, local copies, waits for them, and re-layouts  72.5 us
  transfers between devices with their start and end apart: 122, of which 54 were waited for; matrix products, arithmetic and copies ran while one was open for 19% of the time, Pallas kernels for 1%

profile of v1, /device:TPU:0, one launch (start us, length us, event | category | flops | bytes accessed | tf_op | source)
XLA Modules:
  0.0 2833.7 jit_solution(13451492412217000416)
XLA Ops:
  70.8 40.8 %collective-permute-done.27 = bf16[512,512]{1,0:T(8,128)(2,1)S(1)} collective-permute-done((bf16[512,512]{1,0:T(8,128)(2,1)}, bf16[512,512]{1,0:T(8,128)(2,1)S(1)}, u32[]{:S(2)}, u32[]{:S(2)}) %collective-permute-start.27) | collective-permute-done | bytes 524320 | tf_op jit(solution)/shard_map/ppermute | solution.py:169
  211.2 92.9 %collective-permute-done.19 = bf16[512,1536]{1,0:T(8,128)(2,1)S(1)} collective-permute-done((bf16[512,1536]{1,0:T(8,128)(2,1)S(1)}, bf16[512,1536]{1,0:T(8,128)(2,1)S(1)}, u32[]{:S(2)}, u32[]{:S(2)}) %collective-permute-start.19) | collective-permute-done | bytes 1572896 | tf_op jit(solution)/shard_map/ppermute | solution.py:169
  314.3 30.7 %collective-permute-done.21 = bf16[512,1536]{1,0:T(8,128)(2,1)S(1)} collective-permute-done((bf16[512,1536]{1,0:T(8,128)(2,1)S(1)}, bf16[512,1536]{1,0:T(8,128)(2,1)S(1)}, u32[]{:S(2)}, u32[]{:S(2)}) %collective-permute-start.21) | collective-permute-done | bytes 1572896 | tf_op jit(solution)/shard_map/ppermute | solution.py:169
  345.1 32.7 %collective-permute-done.20 = bf16[512,1536]{1,0:T(8,128)(2,1)S(1)} collective-permute-done((bf16[512,1536]{1,0:T(8,128)(2,1)S(1)}, bf16[512,1536]{1,0:T(8,128)(2,1)S(1)}, u32[]{:S(2)}, u32[]{:S(2)}) %collective-permute-start.20) | collective-permute-done | bytes 1572896 | tf_op jit(solution)/shard_map/ppermute | solution.py:169
  386.2 40.3 %convolution_convert_fusion.4 = bf16[2560,1536]{1,0:T(8,128)(2,1)} fusion(bf16[2560,4096]{1,0:T(8,128)(2,1)} %constant_dynamic-update-slice_fusion.8, bf16[4096,1536]{1,0:T(8,128)(2,1)} %select_dynamic-update-slice_fusion.16), kind=kOutput, calls=%fused_computation.18 | convolution fusion | flops 32216186880 | bytes 41418752 | tf_op jit(solution)/shard_map/dot_general | solution.py:49
  476.3 83.9 %collective-permute-done.45 = bf16[512,2048]{1,0:T(8,128)(2,1)} collective-permute-done((bf16[512,2048]{1,0:T(8,128)(2,1)}, bf16[512,2048]{1,0:T(8,128)(2,1)}, u32[]{:S(2)}, u32[]{:S(2)}) %collective-permute-start.45) | collective-permute-done | bytes 2097184 | tf_op jit(solution)/shard_map/ppermute | solution.py:169
  571.1 44.8 %collective-permute-done.67 = bf16[320,4096]{1,0:T(8,128)(2,1)} collective-permute-done((bf16[320,4096]{1,0:T(8,128)(2,1)S(1)}, bf16[320,4096]{1,0:T(8,128)(2,1)}, u32[]{:S(2)}, u32[]{:S(2)}) %collective-permute-start.67) | collective-permute-done | bytes 2621472 | tf_op jit(solution)/shard_map/ppermute | solution.py:169
  715.6 214.4 %collective-permute-done.49 = bf16[512,2048]{1,0:T(8,128)(2,1)S(1)} collective-permute-done((bf16[512,2048]{1,0:T(8,128)(2,1)}, bf16[512,2048]{1,0:T(8,128)(2,1)S(1)}, u32[]{:S(2)}, u32[]{:S(2)}) %collective-permute-start.49) | collective-permute-done | bytes 2097184 | tf_op jit(solution)/shard_map/ppermute | solution.py:169
  991.8 37.5 %collective-permute-done.55 = bf16[2048,512]{1,0:T(8,128)(2,1)S(1)} collective-permute-done((bf16[2048,512]{1,0:T(8,128)(2,1)}, bf16[2048,512]{1,0:T(8,128)(2,1)S(1)}, u32[]{:S(2)}, u32[]{:S(2)}) %collective-permute-start.55) | collective-permute-done | bytes 2097184 | tf_op jit(solution)/shard_map/ppermute | solution.py:169
  1071.1 57.8 %collective-permute-done.51 = bf16[512,2048]{1,0:T(8,128)(2,1)S(1)} collective-permute-done((bf16[512,2048]{1,0:T(8,128)(2,1)S(1)}, bf16[512,2048]{1,0:T(8,128)(2,1)S(1)}, u32[]{:S(2)}, u32[]{:S(2)}) %collective-permute-start.51) | collective-permute-done | bytes 2097184 | tf_op jit(solution)/shard_map/ppermute | solution.py:169
  1133.9 40.0 %collective-permute-done.50 = bf16[512,2048]{1,0:T(8,128)(2,1)} collective-permute-done((bf16[512,2048]{1,0:T(8,128)(2,1)S(1)}, bf16[512,2048]{1,0:T(8,128)(2,1)}, u32[]{:S(2)}, u32[]{:S(2)}) %collective-permute-start.50) | collective-permute-done | bytes 2097184 | tf_op jit(solution)/shard_map/ppermute | solution.py:169
  1183.1 33.1 %collective-permute-done.57 = bf16[2048,512]{1,0:T(8,128)(2,1)S(1)} collective-permute-done((bf16[2048,512]{1,0:T(8,128)(2,1)S(1)}, bf16[2048,512]{1,0:T(8,128)(2,1)S(1)}, u32[]{:S(2)}, u32[]{:S(2)}) %collective-permute-start.57) | collective-permute-done | bytes 2097184 | tf_op jit(solution)/shard_map/ppermute | solution.py:169
  1259.8 55.2 %multiply_convert_fusion = (bf16[2560,2048]{1,0:T(8,128)(2,1)}, f32[2560,2048]{1,0:T(8,128)}) fusion(bf16[2560,4096]{1,0:T(8,128)(2,1)} %constant_dynamic-update-slice_fusion.17, bf16[4096,2048]{1,0:T(8,128)(2,1)} %select_dynamic-update-slice_fusion.8), kind=kOutput, calls=%fused_computation.10 | convolution fusion | flops 42975887360 | bytes 69206016 | tf_op jit(solution)/shard_map/dot_general | solution.py:49
  1362.0 63.9 %fusion.5 = bf16[2560,2048]{1,0:T(8,128)(2,1)} fusion(f32[2560,2048]{1,0:T(8,128)} %get-tuple-element.113, bf16[2560,4096]{1,0:T(8,128)(2,1)} %constant_dynamic-update-slice_fusion.34, bf16[2048,4096]{1,0:T(8,128)(2,1)} %select_dynamic-update-slice_fusion), kind=kOutput, calls=%fused_computation.6 | convolution fusion | flops 43002101760 | bytes 69206016 | tf_op jit(solution)/shard_map/dot_general | solution.py:49
  1534.8 54.9 %collective-permute-done.118 = bf16[2048,1024]{1,0:T(8,128)(2,1)S(1)} collective-permute-done((bf16[2048,1024]{1,0:T(8,128)(2,1)S(1)}, bf16[2048,1024]{1,0:T(8,128)(2,1)S(1)}, u32[]{:S(2)}, u32[]{:S(2)}) %collective-permute-start.118) | collective-permute-done | bytes 4194336 | tf_op jit(solution)/shard_map/ppermute | solution.py:169
  1592.6 87.0 %collective-permute-done.114 = bf16[1024,2048]{1,0:T(8,128)(2,1)S(1)} collective-permute-done((bf16[1024,2048]{1,0:T(8,128)(2,1)}, bf16[1024,2048]{1,0:T(8,128)(2,1)S(1)}, u32[]{:S(2)}, u32[]{:S(2)}) %collective-permute-start.114) | collective-permute-done | bytes 4194336 | tf_op jit(solution)/shard_map/ppermute | solution.py:169
  1701.8 67.8 %collective-permute-done.120 = bf16[2048,1024]{1,0:T(8,128)(2,1)} collective-permute-done((bf16[2048,1024]{1,0:T(8,128)(2,1)}, bf16[2048,1024]{1,0:T(8,128)(2,1)}, u32[]{:S(2)}, u32[]{:S(2)}) %collective-permute-start.120) | collective-permute-done | bytes 4194336 | tf_op jit(solution)/shard_map/ppermute | solution.py:169
  1784.8 79.5 %collective-permute-done.119 = bf16[2048,1024]{1,0:T(8,128)(2,1)} collective-permute-done((bf16[2048,1024]{1,0:T(8,128)(2,1)S(1)}, bf16[2048,1024]{1,0:T(8,128)(2,1)}, u32[]{:S(2)}, u32[]{:S(2)}) %collective-permute-start.119) | collective-permute-done | bytes 4194336 | tf_op jit(solution)/shard_map/ppermute | solution.py:169
  1873.7 80.5 %collective-permute-done.115 = bf16[1024,2048]{1,0:T(8,128)(2,1)} collective-permute-done((bf16[1024,2048]{1,0:T(8,128)(2,1)S(1)}, bf16[1024,2048]{1,0:T(8,128)(2,1)}, u32[]{:S(2)}, u32[]{:S(2)}) %collective-permute-start.115) | collective-permute-done | bytes 4194336 | tf_op jit(solution)/shard_map/ppermute | solution.py:169
  2232.8 54.1 %collective-permute-done.102 = f32[4096]{0:T(1024)S(1)} collective-permute-done((f32[4096]{0:T(1024)S(1)}, f32[4096]{0:T(1024)S(1)}, u32[]{:S(2)}, u32[]{:S(2)}) %collective-permute-start.102) | collective-permute-done | bytes 16416 | tf_op jit(solution)/shard_map/ppermute | solution.py:169
  2355.1 37.3 %attention_backward.1 = bf16[2,2,2,320,1536]{4,3,2,1,0:T(8,128)(2,1)} custom-call(s32[1]{0:T(128)} %bitcast.turn_ref, f32[4]{0:T(128)S(1)} %multiply_power_fusion.slope_ref, bf16[2,2,2,320,1536]{4,3,2,1,0:T(8,128)(2,1)} %bitcast.91, bf16[2,2,2,320,512]{4,3,2,1,0:T(8,128)(2,1)S(1)} %bitcast.64, s32[2,1280,1]{2,1,0:T(8,128)S(1)} %copy-done.3, ...), custom_call_target="tpu_custom_call" | custom-call | flops 8724152320 | bytes 18350080 | tf_op jit(solution)/shard_map/attention_backward/pallas_call | solution.py:361
  2520.3 35.9 %collective-permute-done.106 = bf16[1024,1536]{1,0:T(8,128)(2,1)S(1)} collective-permute-done((bf16[1024,1536]{1,0:T(8,128)(2,1)S(1)}, bf16[1024,1536]{1,0:T(8,128)(2,1)S(1)}, u32[]{:S(2)}, u32[]{:S(2)}) %collective-permute-start.106) | collective-permute-done | bytes 3145760 | tf_op jit(solution)/shard_map/ppermute | solution.py:169
  2623.2 73.9 %collective-permute-done.107 = bf16[1024,1536]{1,0:T(8,128)(2,1)} collective-permute-done((bf16[1024,1536]{1,0:T(8,128)(2,1)}, bf16[1024,1536]{1,0:T(8,128)(2,1)}, u32[]{:S(2)}, u32[]{:S(2)}) %collective-permute-start.107) | collective-permute-done | bytes 3145760 | tf_op jit(solution)/shard_map/ppermute | solution.py:169
  2710.0 40.2 %collective-permute-done.113 = bf16[512,512]{1,0:T(8,128)(2,1)S(1)} collective-permute-done((bf16[512,512]{1,0:T(8,128)(2,1)S(1)}, bf16[512,512]{1,0:T(8,128)(2,1)S(1)}, u32[]{:S(2)}, u32[]{:S(2)}) %collective-permute-start.113) | collective-permute-done | bytes 524320 | tf_op jit(solution)/shard_map/ppermute | solution.py:169
  (614 shorter events, 1352.0 us)
Async XLA Ops:
  131.5 181.0 %collective-permute-start.11 = (bf16[320,4096]{1,0:T(8,128)(2,1)S(1)}, bf16[320,4096]{1,0:T(8,128)(2,1)S(1)}, u32[]{:S(2)}, u32[]{:S(2)}) collective-permute-start(bf16[320,4096]{1,0:T(8,128)(2,1)S(1)} %get-tuple-element.62), channel_id=1, source_target_pairs={{0,1},{1,0},{2,3},{3,2},{4,5},{5,4},{6,7},{7,6},{8,9},{9,8},{10,11... | collective-permute-start | bytes 7864328 | tf_op jit(solution)/shard_map/ppermute | solution.py:169
  464.8 240.1 %collective-permute-start.30 = (bf16[1280,4096]{1,0:T(8,128)(2,1)}, bf16[1280,4096]{1,0:T(8,128)(2,1)}, u32[]{:S(2)}, u32[]{:S(2)}) collective-permute-start(bf16[1280,4096]{1,0:T(8,128)(2,1)} %convolution_convert_fusion), channel_id=1, source_target_pairs={{0,1},{1,0},{2,3},{3,2},{4,5},{5,4},{6,7},{7,6},{8,9},{9,8},{10,11... | collective-permute-start | bytes 31457288 | tf_op jit(solution)/shard_map/ppermute | solution.py:169
  473.6 142.4 %collective-permute-start.67 = (bf16[320,4096]{1,0:T(8,128)(2,1)S(1)}, bf16[320,4096]{1,0:T(8,128)(2,1)}, u32[]{:S(2)}, u32[]{:S(2)}) collective-permute-start(bf16[320,4096]{1,0:T(8,128)(2,1)S(1)} %get-tuple-element.102), channel_id=1, source_target_pairs={{0,8},{4,12},{8,0},{12,4},{16,24},{20,28},{24,16},{28,20},{1,9},{5... | collective-permute-start | bytes 7864328 | tf_op jit(solution)/shard_map/ppermute | solution.py:169
  474.8 151.5 %collective-permute-start.66 = (bf16[320,4096]{1,0:T(8,128)(2,1)S(1)}, bf16[320,4096]{1,0:T(8,128)(2,1)}, u32[]{:S(2)}, u32[]{:S(2)}) collective-permute-start(bf16[320,4096]{1,0:T(8,128)(2,1)S(1)} %get-tuple-element.102), channel_id=1, source_target_pairs={{0,2},{1,3},{2,0},{3,1},{4,6},{5,7},{6,4},{7,5},{8,10},{9,11},{10,... | collective-permute-start | bytes 7864328 | tf_op jit(solution)/shard_map/ppermute | solution.py:169
  658.0 272.6 %collective-permute-start.48 = (bf16[512,2048]{1,0:T(8,128)(2,1)}, bf16[512,2048]{1,0:T(8,128)(2,1)S(1)}, u32[]{:S(2)}, u32[]{:S(2)}) collective-permute-start(bf16[512,2048]{1,0:T(8,128)(2,1)} %get-tuple-element.50), channel_id=1, source_target_pairs={{0,16},{4,20},{8,24},{12,28},{16,0},{20,4},{24,8},{28,12},{1,17},{... | collective-permute-start | bytes 6291464 | tf_op jit(solution)/shard_map/ppermute | solution.py:169
  663.6 275.3 %collective-permute-start.53 = (bf16[2048,512]{1,0:T(8,128)(2,1)}, bf16[2048,512]{1,0:T(8,128)(2,1)}, u32[]{:S(2)}, u32[]{:S(2)}) collective-permute-start(bf16[2048,512]{1,0:T(8,128)(2,1)} %get-tuple-element.56), channel_id=1, source_target_pairs={{0,4},{4,0},{8,12},{12,8},{16,20},{20,16},{24,28},{28,24},{1,5},{5... | collective-permute-start | bytes 6291464 | tf_op jit(solution)/shard_map/ppermute | solution.py:169
  696.6 291.5 %collective-permute-start.56 = (bf16[2048,512]{1,0:T(8,128)(2,1)}, bf16[2048,512]{1,0:T(8,128)(2,1)S(1)}, u32[]{:S(2)}, u32[]{:S(2)}) collective-permute-start(bf16[2048,512]{1,0:T(8,128)(2,1)} %collective-permute-done.52), channel_id=1, source_target_pairs={{0,16},{4,20},{8,24},{12,28},{16,0},{20,4},{24,8},{28,12},{1,17},{... | collective-permute-start | bytes 6291464 | tf_op jit(solution)/shard_map/ppermute | solution.py:169
  699.2 236.4 %collective-permute-start.54 = (bf16[2048,512]{1,0:T(8,128)(2,1)}, bf16[2048,512]{1,0:T(8,128)(2,1)}, u32[]{:S(2)}, u32[]{:S(2)}) collective-permute-start(bf16[2048,512]{1,0:T(8,128)(2,1)} %collective-permute-done.52), channel_id=1, source_target_pairs={{0,4},{4,0},{8,12},{12,8},{16,20},{20,16},{24,28},{28,24},{1,5},{5... | collective-permute-start | bytes 6291464 | tf_op jit(solution)/shard_map/ppermute | solution.py:169
  705.0 225.1 %collective-permute-start.49 = (bf16[512,2048]{1,0:T(8,128)(2,1)}, bf16[512,2048]{1,0:T(8,128)(2,1)S(1)}, u32[]{:S(2)}, u32[]{:S(2)}) collective-permute-start(bf16[512,2048]{1,0:T(8,128)(2,1)} %collective-permute-done.45), channel_id=1, source_target_pairs={{0,16},{4,20},{8,24},{12,28},{16,0},{20,4},{24,8},{28,12},{1,17},{... | collective-permute-start | bytes 6291464 | tf_op jit(solution)/shard_map/ppermute | solution.py:169
  1035.4 147.7 %collective-permute-start.58 = (bf16[2048,512]{1,0:T(8,128)(2,1)S(1)}, bf16[2048,512]{1,0:T(8,128)(2,1)S(1)}, u32[]{:S(2)}, u32[]{:S(2)}) collective-permute-start(bf16[2048,512]{1,0:T(8,128)(2,1)S(1)} %collective-permute-done.56), channel_id=1, source_target_pairs={{0,4},{4,0},{8,12},{12,8},{16,20},{20,16},{24,28},{28,24},{1,5},{5... | collective-permute-start | bytes 6291464 | tf_op jit(solution)/shard_map/ppermute | solution.py:169
  1069.1 147.1 %collective-permute-start.57 = (bf16[2048,512]{1,0:T(8,128)(2,1)S(1)}, bf16[2048,512]{1,0:T(8,128)(2,1)S(1)}, u32[]{:S(2)}, u32[]{:S(2)}) collective-permute-start(bf16[2048,512]{1,0:T(8,128)(2,1)S(1)} %collective-permute-done.55), channel_id=1, source_target_pairs={{0,4},{4,0},{8,12},{12,8},{16,20},{20,16},{24,28},{28,24},{1,5},{5... | collective-permute-start | bytes 6291464 | tf_op jit(solution)/shard_map/ppermute | solution.py:169
  1069.7 148.5 %collective-permute-start.38 = (bf16[320,4096]{1,0:T(8,128)(2,1)}, bf16[320,4096]{1,0:T(8,128)(2,1)S(1)}, u32[]{:S(2)}, u32[]{:S(2)}) collective-permute-start(bf16[320,4096]{1,0:T(8,128)(2,1)} %get-tuple-element.52), channel_id=1, source_target_pairs={{0,8},{4,12},{8,0},{12,4},{16,24},{20,28},{24,16},{28,20},{1,9},{5... | collective-permute-start | bytes 7864328 | tf_op jit(solution)/shard_map/ppermute | solution.py:169
  1497.8 181.8 %collective-permute-start.114 = (bf16[1024,2048]{1,0:T(8,128)(2,1)}, bf16[1024,2048]{1,0:T(8,128)(2,1)S(1)}, u32[]{:S(2)}, u32[]{:S(2)}) collective-permute-start(bf16[1024,2048]{1,0:T(8,128)(2,1)} %fusion.55), channel_id=1, source_target_pairs={{0,4},{4,0},{8,12},{12,8},{16,20},{20,16},{24,28},{28,24},{1,5},{5... | collective-permute-start | bytes 12582920 | tf_op jit(solution)/shard_map/ppermute | solution.py:169
  1515.4 447.2 %collective-permute-start.59 = (bf16[1280,4096]{1,0:T(8,128)(2,1)}, bf16[1280,4096]{1,0:T(8,128)(2,1)}, u32[]{:S(2)}, u32[]{:S(2)}) collective-permute-start(bf16[1280,4096]{1,0:T(8,128)(2,1)} %convolution_convert_fusion.3), channel_id=1, source_target_pairs={{0,1},{1,0},{2,3},{3,2},{4,5},{5,4},{6,7},{7,6},{8,9},{9,8},{10,11... | collective-permute-start | bytes 31457288 | tf_op jit(solution)/shard_map/ppermute | solution.py:169
  1532.7 236.9 %collective-permute-start.120 = (bf16[2048,1024]{1,0:T(8,128)(2,1)}, bf16[2048,1024]{1,0:T(8,128)(2,1)}, u32[]{:S(2)}, u32[]{:S(2)}) collective-permute-start(bf16[2048,1024]{1,0:T(8,128)(2,1)} %fusion.76), channel_id=1, source_target_pairs={{0,4},{4,0},{8,12},{12,8},{16,20},{20,16},{24,28},{28,24},{1,5},{5... | collective-permute-start | bytes 12582920 | tf_op jit(solution)/shard_map/ppermute | solution.py:169
  1534.2 339.4 %collective-permute-start.116 = (bf16[1024,2048]{1,0:T(8,128)(2,1)}, bf16[1024,2048]{1,0:T(8,128)(2,1)}, u32[]{:S(2)}, u32[]{:S(2)}) collective-permute-start(bf16[1024,2048]{1,0:T(8,128)(2,1)} %fusion.58), channel_id=1, source_target_pairs={{0,4},{4,0},{8,12},{12,8},{16,20},{20,16},{24,28},{28,24},{1,5},{5... | collective-permute-start | bytes 12582920 | tf_op jit(solution)/shard_map/ppermute | solution.py:169
  1591.8 272.5 %collective-permute-start.119 = (bf16[2048,1024]{1,0:T(8,128)(2,1)S(1)}, bf16[2048,1024]{1,0:T(8,128)(2,1)}, u32[]{:S(2)}, u32[]{:S(2)}) collective-permute-start(bf16[2048,1024]{1,0:T(8,128)(2,1)S(1)} %add_convert_fusion.6), channel_id=1, source_target_pairs={{0,16},{4,20},{8,24},{12,28},{16,0},{20,4},{24,8},{28,12},{1,17},{... | collective-permute-start | bytes 12582920 | tf_op jit(solution)/shard_map/ppermute | solution.py:169
  1683.9 270.3 %collective-permute-start.115 = (bf16[1024,2048]{1,0:T(8,128)(2,1)S(1)}, bf16[1024,2048]{1,0:T(8,128)(2,1)}, u32[]{:S(2)}, u32[]{:S(2)}) collective-permute-start(bf16[1024,2048]{1,0:T(8,128)(2,1)S(1)} %add_convert_fusion.9), channel_id=1, source_target_pairs={{0,16},{4,20},{8,24},{12,28},{16,0},{20,4},{24,8},{28,12},{1,17},{... | collective-permute-start | bytes 12582920 | tf_op jit(solution)/shard_map/ppermute | solution.py:169
  1769.6 228.9 %collective-permute-start.74 = (bf16[1280,4096]{1,0:T(8,128)(2,1)}, bf16[1280,4096]{1,0:T(8,128)(2,1)}, u32[]{:S(2)}, u32[]{:S(2)}) collective-permute-start(bf16[1280,4096]{1,0:T(8,128)(2,1)} %convolution_convert_fusion.2), channel_id=1, source_target_pairs={{0,1},{1,0},{2,3},{3,2},{4,5},{5,4},{6,7},{7,6},{8,9},{9,8},{10,11... | collective-permute-start | bytes 31457288 | tf_op jit(solution)/shard_map/ppermute | solution.py:169
  1873.6 159.7 %collective-permute-start.121 = (bf16[2048,512]{1,0:T(8,128)(2,1)}, bf16[2048,512]{1,0:T(8,128)(2,1)}, u32[]{:S(2)}, u32[]{:S(2)}) collective-permute-start(bf16[2048,512]{1,0:T(8,128)(2,1)} %broadcast_select_fusion.2), channel_id=1, source_target_pairs={{0,8},{4,12},{8,0},{12,4},{16,24},{20,28},{24,16},{28,20},{1,9},{5... | collective-permute-start | bytes 6291464 | tf_op jit(solution)/shard_map/ppermute | solution.py:169
  1962.6 141.9 %collective-permute-start.117 = (bf16[512,2048]{1,0:T(8,128)(2,1)}, bf16[512,2048]{1,0:T(8,128)(2,1)}, u32[]{:S(2)}, u32[]{:S(2)}) collective-permute-start(bf16[512,2048]{1,0:T(8,128)(2,1)} %broadcast_select_fusion.8), channel_id=1, source_target_pairs={{0,8},{4,12},{8,0},{12,4},{16,24},{20,28},{24,16},{28,20},{1,9},{5... | collective-permute-start | bytes 6291464 | tf_op jit(solution)/shard_map/ppermute | solution.py:169
  2421.4 140.7 %collective-permute-start.89 = (bf16[1280,4096]{1,0:T(8,128)(2,1)}, bf16[1280,4096]{1,0:T(8,128)(2,1)}, u32[]{:S(2)}, u32[]{:S(2)}) collective-permute-start(bf16[1280,4096]{1,0:T(8,128)(2,1)} %convolution_convert_fusion.1), channel_id=1, source_target_pairs={{0,1},{1,0},{2,3},{3,2},{4,5},{5,4},{6,7},{7,6},{8,9},{9,8},{10,11... | collective-permute-start | bytes 31457288 | tf_op jit(solution)/shard_map/ppermute | solution.py:169
  2484.5 138.7 %collective-permute-start.108 = (bf16[1024,1536]{1,0:T(8,128)(2,1)}, bf16[1024,1536]{1,0:T(8,128)(2,1)}, u32[]{:S(2)}, u32[]{:S(2)}) collective-permute-start(bf16[1024,1536]{1,0:T(8,128)(2,1)} %fusion.70), channel_id=1, source_target_pairs={{0,4},{4,0},{8,12},{12,8},{16,20},{20,16},{24,28},{28,24},{1,5},{5... | collective-permute-start | bytes 9437192 | tf_op jit(solution)/shard_map/ppermute | solution.py:169
  2558.8 138.3 %collective-permute-start.107 = (bf16[1024,1536]{1,0:T(8,128)(2,1)}, bf16[1024,1536]{1,0:T(8,128)(2,1)}, u32[]{:S(2)}, u32[]{:S(2)}) collective-permute-start(bf16[1024,1536]{1,0:T(8,128)(2,1)} %add_convert_fusion.12), channel_id=1, source_target_pairs={{0,16},{4,20},{8,24},{12,28},{16,0},{20,4},{24,8},{28,12},{1,17},{... | collective-permute-start | bytes 9437192 | tf_op jit(solution)/shard_map/ppermute | solution.py:169
  (170 other events, 8151.4 us)

commit v2 on v1

v2 whole, which is shorter than its diff:
```python
import functools
import math

import jax
import jax.numpy as jnp
from jax import lax
from jax.experimental import pallas as pl
from jax.experimental.pallas import tpu as pltpu
from jax.sharding import PartitionSpec as P

D = 4096
H = 32
HEAD = D // H
REACH = 640
NORM_EPSILON = 1e-05
SQRT_HALF = 0.7071067811865476
INV_ROOT_TWO_PI = 0.3989422804014327
BF = jnp.bfloat16
F32 = jnp.float32
COVER = 0.05
VMEM = 56 << 20


def norm_forward(values_in):
    row_mean = jnp.mean(values_in, axis=-1, keepdims=True)
    centred = values_in - row_mean
    row_variance = jnp.mean(centred * centred, axis=-1, keepdims=True)
    inverse = lax.rsqrt(row_variance + NORM_EPSILON)
    return centred * inverse, inverse


def norm_backward(grad_out, normed, inverse, gain):
    grad_gain = jnp.sum(grad_out * normed, axis=0)
    scaled = grad_out * gain
    mean_one = jnp.mean(scaled, axis=-1, keepdims=True)
    mean_two = jnp.mean(scaled * normed, axis=-1, keepdims=True)
    return inverse * (scaled - mean_one - normed * mean_two), grad_gain


def gelu_and_slope(pre_act):
    part = 0.5 * (1.0 + lax.erf(pre_act * SQRT_HALF))
    slope = part + pre_act * jnp.exp(-0.5 * pre_act * pre_act) * INV_ROOT_TWO_PI
    return pre_act * part, slope


def dot(left, right, cl, cr):
    return lax.dot_general(left, right, (((cl,), (cr,)), ((), ())), preferred_element_type=F32)


class Steps:
    def __init__(self):
        self.token = jnp.zeros((1,), F32)
        self.pending = []
        self.first = True

    def begin(self, value):
        if self.first:
            return value
        return lax.optimization_barrier((value, self.token))[0]

    def move(self, how, value):
        out = how(self.begin(value))
        self.pending.append(out)
        return out

    def run(self, how, value, *more, **named):
        out = how(self.begin(value), *more, **named)
        self.pending += jax.tree.leaves(out)
        return out

    def close(self):
        self.token = lax.optimization_barrier((self.token, *self.pending))[0]
        self.pending = []
        self.first = False


def params(grid_dims):
    return pltpu.CompilerParams(
        dimension_semantics=("arbitrary",) * grid_dims, vmem_limit_bytes=VMEM
    )


def cost(m, n, k):
    return pl.CostEstimate(
        flops=int(2 * m * n * k * COVER), transcendentals=0, bytes_accessed=2 * (m * k + k * n + m * n)
    )


def tile(size, most):
    if size <= most:
        return size
    while size % most:
        most -= 128
    return most


def stack_rows(*pieces):
    rows = math.gcd(*(v.shape[0] for v in pieces))
    cols = pieces[0].shape[1]
    sizes = [v.shape[0] // rows for v in pieces]
    firsts = [sum(sizes[:i]) for i in range(len(pieces))]

    def body(*refs):
        step = pl.program_id(0)
        for ref, first, size in zip(refs, firsts, sizes):

            @pl.when((step >= first) & (step < first + size))
            def _(ref=ref):
                refs[-1][...] = ref[...]

    def spec(first, size):
        return pl.BlockSpec((rows, cols), lambda g: (jnp.clip(g - first, 0, size - 1), 0))

    return pl.pallas_call(
        body,
        out_shape=jax.ShapeDtypeStruct((sum(sizes) * rows, cols), pieces[0].dtype),
        grid=(sum(sizes),),
        in_specs=[spec(f, s) for f, s in zip(firsts, sizes)],
        out_specs=pl.BlockSpec((rows, cols), lambda g: (g, 0)),
        compiler_params=params(1),
        name="stack_rows",
    )(*pieces)


def gram(a_pair, b_pair, blocks, side):
    rows = a_pair[0].shape[0]
    width = blocks[0][1]
    m = width if side == 0 else a_pair[0].shape[1]
    n = width if side == 1 else b_pair[0].shape[1]
    tm, tn = tile(m, 1024), tile(n, 1024)
    grid_m, grid_n = m // tm, n // tn
    count = len(blocks)
    per = grid_m * grid_n

    def at(g):
        p, r = g // per, g % per
        return p, r // grid_m, r % grid_m

    def body(index_ref, a0, a1, b0, b1, *outs):
        total = (dot(a0[...], b0[...], 0, 0) + dot(a1[...], b1[...], 0, 0)).astype(BF)
        p = pl.program_id(0) // per
        for q in range(count):

            @pl.when(p == q)
            def _(q=q):
                outs[q][...] = total

    def a_map(g, index):
        p, _, i = at(g)
        return 0, (index[p] * grid_m + i if side == 0 else i)

    def b_map(g, index):
        p, j, _ = at(g)
        return 0, (index[p] * grid_n + j if side == 1 else j)

    def out_map(q):
        def at_q(g, index):
            r = jnp.clip(g - q * per, 0, per - 1)
            return r % grid_m, r // grid_m

        return at_q

    return pl.pallas_call(
        body,
        out_shape=[jax.ShapeDtypeStruct((m, n), BF)] * count,
        grid_spec=pltpu.PrefetchScalarGridSpec(
            num_scalar_prefetch=1,
            grid=(count * per,),
            in_specs=[pl.BlockSpec((rows, tm), a_map)] * 2 + [pl.BlockSpec((rows, tn), b_map)] * 2,
            out_specs=[pl.BlockSpec((tm, tn), out_map(q)) for q in range(count)],
        ),
        compiler_params=params(1),
        cost_estimate=cost(m, n * count, 2 * rows),
        name="gram",
    )(jnp.array([b[0] for b in blocks], jnp.int32), *a_pair, *b_pair)


def deep(a, blocks, starts, cr, finish=None, extra=(), outs=1, tm=640, tn=512, parts=1):
    m = a.shape[0]
    n = blocks[0].shape[1 - cr]
    count = len(blocks)
    tm, tn = tile(m, tm), tile(n, tn)
    rows = tm // parts

    def body(starts_ref, a_ref, *rest):
        def part(r):
            total = None
            for p in range(count):
                size = blocks[p].shape[cr]
                at = pl.multiple_of(starts_ref[p] * 128, 128)
                term = dot(a_ref[r * rows : (r + 1) * rows, pl.ds(at, size)], rest[p][...], 1, cr)
                total = term if total is None else total + term
            return total

        def store(r, total):
            at = slice(r * rows, (r + 1) * rows)
            values = (total,) if finish is None else finish(total, *(v[at, :] for v in rest[count:-outs]))
            for ref, value in zip(rest[-outs:], values):
                ref[at, :] = value.astype(BF)

        before = None
        for r in range(parts):
            total = part(r)
            if before is not None:
                store(r - 1, before)
            before = total
        store(parts - 1, before)

    def w_spec(w):
        size = w.shape[cr]
        if cr == 0:
            return pl.BlockSpec((size, tn), lambda j, i, *_: (0, j))
        return pl.BlockSpec((tn, size), lambda j, i, *_: (j, 0))

    out = pl.BlockSpec((tm, tn), lambda j, i, *_: (i, j))
    result = pl.pallas_call(
        body,
        out_shape=[jax.ShapeDtypeStruct((m, n), BF)] * outs,
        grid_spec=pltpu.PrefetchScalarGridSpec(
            num_scalar_prefetch=1,
            grid=(n // tn, m // tm),
            in_specs=[pl.BlockSpec((tm, a.shape[1]), lambda j, i, *_: (i, 0))]
            + [w_spec(w) for w in blocks]
            + [out] * len(extra),
            out_specs=[out] * outs,
        ),
        compiler_params=params(2),
        cost_estimate=cost(m, n, a.shape[1]),
        name="deep",
    )(starts, a, *blocks, *extra)
    return result[0] if outs == 1 else result


def broad(a, blocks, starts, cr, add=None):
    m, k = a.shape
    n = sum(w.shape[1 - cr] for w in blocks)
    count = len(blocks)
    tm = tile(m, 320)

    def body(starts_ref, a_ref, *rest):
        for p in range(count):
            size = blocks[p].shape[1 - cr]
            at = pl.multiple_of(starts_ref[p] * 128, 128)
            part = dot(a_ref[...], rest[p][...], 1, cr)
            if add is not None:
                part = part + rest[count][:, pl.ds(at, size)].astype(F32)
            rest[-1][:, pl.ds(at, size)] = part.astype(BF)

    out = pl.BlockSpec((tm, n), lambda i, *_: (i, 0))
    return pl.pallas_call(
        body,
        out_shape=jax.ShapeDtypeStruct((m, n), BF),
        grid_spec=pltpu.PrefetchScalarGridSpec(
            num_scalar_prefetch=1,
            grid=(m // tm,),
            in_specs=[pl.BlockSpec((tm, k), lambda i, *_: (i, 0))]
            + [pl.BlockSpec(w.shape, lambda i, *_: (0, 0), pipeline_mode=pl.Buffered(1)) for w in blocks]
            + ([out] if add is not None else []),
            out_specs=out,
        ),
        compiler_params=params(1),
        cost_estimate=cost(m, n, k),
        name="broad",
    )(starts, a, *blocks, *(() if add is None else (add,)))


QB = 256


def window(first):
    low = max(0, first - REACH)
    return low, first + QB - low


def masked_scores(q, k, start, slope, first, low, width, scale):
    scores = dot(q, k, 1, 1)
    row = first + lax.broadcasted_iota(jnp.int32, (QB, width), 0)
    col = low + lax.broadcasted_iota(jnp.int32, (QB, width), 1)
    scores = scores * scale - slope * (row - col).astype(F32)
    return jnp.where((col >= start) & (col <= row), scores, -1e30)


def in_order(turn, visit):
    for c in range(2):

        @pl.when(lax.bitwise_and(turn, 1) == c)
        def _(c=c):
            for i in range(4):
                visit(i, (i & 1) ^ c, lax.bitwise_xor(jnp.int32(i >> 1), lax.shift_right_logical(turn, 1)))


def attention_forward(turn_ref, slope_ref, near, far, start_ref, o_near, o_far, lse_ref, q_s, k_s, v_s, o_s):
    turn = turn_ref[0]
    slope = slope_ref[pl.program_id(1)]
    sequence = q_s.shape[0]
    piece = sequence // 4
    scale = 1.0 / math.sqrt(HEAD)

    def load(i, core, x):
        block = (near, far)[core][0, x]
        for j, scratch in enumerate((q_s, k_s, v_s)):
            scratch[i * piece : (i + 1) * piece, :] = block[:, j * HEAD : (j + 1) * HEAD]

    in_order(turn, load)
    for first in range(0, sequence, QB):
        low, width = window(first)
        scores = masked_scores(
            q_s[first : first + QB, :],
            k_s[low : low + width, :],
            start_ref[0, first : first + QB, :],
            slope,
            first,
            low,
            width,
            scale,
        )
        peak = jnp.max(scores, axis=-1, keepdims=True)
        weights = jnp.exp(scores - peak)
        total = jnp.sum(weights, axis=-1, keepdims=True)
        lse_ref[0, 0, first : first + QB, :] = peak + jnp.log(total)
        probs = (weights * (1.0 / total)).astype(BF)
        o_s[first : first + QB, :] = dot(probs, v_s[low : low + width, :], 1, 0).astype(BF)

    def store(i, core, x):
        (o_near, o_far)[core][0, x] = o_s[i * piece : (i + 1) * piece, :]

    in_order(turn, store)


def attention_backward(
    turn_ref,
    slope_ref,
    near,
    far,
    do_near,
    do_far,
    start_ref,
    lse_ref,
    out_near,
    out_far,
    q_s,
    k_s,
    v_s,
    do_s,
    dq_s,
    dk_s,
    dv_s,
):
    turn = turn_ref[0]
    slope = slope_ref[pl.program_id(1)]
    sequence = q_s.shape[0]
    piece = sequence // 4
    scale = 1.0 / math.sqrt(HEAD)

    def load(i, core, x):
        rows = slice(i * piece, (i + 1) * piece)
        block = (near, far)[core][0, x]
        for j, scratch in enumerate((q_s, k_s, v_s)):
            scratch[rows, :] = block[:, j * HEAD : (j + 1) * HEAD]
        do_s[rows, :] = (do_near, do_far)[core][0, x]

    in_order(turn, load)
    dk_s[...] = jnp.zeros_like(dk_s)
    dv_s[...] = jnp.zeros_like(dv_s)
    for first in range(0, sequence, QB):
        low, width = window(first)
        keys = k_s[low : low + width, :]
        query = q_s[first : first + QB, :]
        grad = do_s[first : first + QB, :]
        scores = masked_scores(
            query, keys, start_ref[0, first : first + QB, :], slope, first, low, width, scale
        )
        probs = jnp.exp(scores - lse_ref[0, 0, first : first + QB, :])
        grad_probs = dot(grad, v_s[low : low + width, :], 1, 1)
        delta = jnp.sum(probs * grad_probs, axis=-1, keepdims=True)
        grad_scores = (probs * (grad_probs - delta) * scale).astype(BF)
        dq_s[first : first + QB, :] = dot(grad_scores, keys, 1, 0).astype(BF)
        dk_s[low : low + width, :] += dot(grad_scores, query, 0, 0)
        dv_s[low : low + width, :] += dot(probs.astype(BF), grad, 0, 0)

    def store(i, core, x):
        rows = slice(i * piece, (i + 1) * piece)
        out = (out_near, out_far)[core]
        out[0, x, :, 0:HEAD] = dq_s[rows, :]
        out[0, x, :, HEAD : 2 * HEAD] = dk_s[rows, :].astype(BF)
        out[0, x, :, 2 * HEAD : 3 * HEAD] = dv_s[rows, :].astype(BF)

    in_order(turn, store)


def on_device(
    hidden_in,
    segment_ids,
    qkv_weight,
    out_weight,
    up_weight,
    down_weight,
    norm1_gain,
    norm2_gain,
    out_cotangent,
):
    n = lax.axis_size("fsdp")
    tp = lax.axis_size("tp")
    ring = n // 4
    f = lax.axis_index("fsdp")
    t = lax.axis_index("tp")
    y, zl, zh = f & 1, (f >> 1) & 1, f >> 2
    low_half = zl == 0
    piece = hidden_in.shape[0]
    half = piece // 2
    sequence = piece * tp
    heads = H // tp // 2
    width = heads * HEAD
    unit = D // n
    pairs = [(k, j) for k in range(ring) for j in range(2)]
    far_first = range(ring - 1, -1, -1)
    steps = Steps()
    move, run, close = steps.move, steps.run, steps.close

    def over(axis, to, size):
        return lambda v: lax.ppermute(v, axis, [(i, to(i)) for i in range(size)])

    pp_core = over("tp", lambda i: i ^ 1, tp)
    pp_x = over("tp", lambda i: i ^ 2, tp)
    pp_zl = over("fsdp", lambda i: i ^ 2, n)
    pp_y = over("fsdp", lambda i: i ^ 1, n)
    pp_up = over("fsdp", lambda i: (i + 4) % n, n)
    pp_down = over("fsdp", lambda i: (i - 4) % n, n)

    def to_rel(v):
        cols = [v[..., b * unit : (b + 1) * unit] for b in range(n)]

        def pick(k, j, l):
            chosen = None
            for a in range(ring):
                both = jnp.where(y == j, cols[a * 4 + l * 2], cols[a * 4 + l * 2 + 1])
                chosen = both if chosen is None else jnp.where((zh - k) % ring == a, both, chosen)
            return chosen

        return jnp.concatenate([pick(k, j, l) for k, j in pairs for l in range(2)], axis=-1)

    def from_rel(v):
        cols = [v[..., b * unit : (b + 1) * unit] for b in range(n)]

        def pick(a, l, b):
            chosen = None
            for k in range(ring):
                both = jnp.where(y == b, cols[k * 4 + l], cols[k * 4 + 2 + l])
                chosen = both if chosen is None else jnp.where((zh - k) % ring == a, both, chosen)
            return chosen

        return jnp.concatenate(
            [pick(a, l, b) for a in range(ring) for l in range(2) for b in range(2)], axis=-1
        )

    def mine_of(first, second):
        return jnp.where(low_half, first, second)

    def joined(mine, other, axis):
        return jnp.concatenate(
            [jnp.where(low_half, mine, other), jnp.where(low_half, other, mine)], axis=axis
        )

    def plus(a, b):
        return (a.astype(F32) + b.astype(F32)).astype(BF)

    def ring_up(v):
        chain = [v]
        for _ in range(ring - 1):
            chain.append(pp_up(chain[-1]))
        return chain[1:]

    class Weight:
        def __init__(self):
            self.have = {}

        def zh(self, source, chunk):
            for k, v in enumerate(move(ring_up, self.have[0, 0, source, chunk])):
                self.have[k + 1, 0, source, chunk] = v

        def y(self, source, chunk):
            self.have[0, 1, source, chunk] = move(pp_y, self.have[0, 0, source, chunk])

        def yz(self, source, chunk):
            for k in range(1, ring):
                self.have[k, 1, source, chunk] = move(pp_y, self.have[k, 0, source, chunk])

        def blocks(self, axis):
            found, starts = [], []
            for k, j in pairs:
                for source in range(2):
                    side = zl if source == 0 else 1 - zl
                    base = (2 * (2 * k + j) + side) * unit
                    at = 0
                    for chunk in sorted(c for a, b, s, c in self.have if (a, b, s) == (k, j, source)):
                        v = self.have[k, j, source, chunk]
                        found.append(v)
                        starts.append((base + at) // 128)
                        at += v.shape[axis]
            return found, jnp.stack(starts).astype(jnp.int32)

    gains = jnp.stack([norm1_gain, norm2_gain])
    gain_chain = [joined(gains, pp_zl(gains), 1)]
    gain_chain = jnp.concatenate(gain_chain + ring_up(gain_chain[0]), axis=0)
    gain_other = pp_y(gain_chain)
    gains = jnp.concatenate(
        [(gain_chain, gain_other)[j][2 * k : 2 * k + 2] for k, j in pairs], axis=1
    ).astype(F32)
    gain_one, gain_two = gains[0:1], gains[1:2]
    documents = jnp.concatenate([segment_ids, pp_zl(segment_ids)], axis=0)
    x = to_rel(hidden_in).astype(F32)
    normed_one, inverse_one = norm_forward(x)
    a_one = (normed_one * gain_one).astype(BF)

    qkv_heads = (
        qkv_weight.reshape(unit, 3, 2 * heads, HEAD)
        .transpose(0, 2, 1, 3)
        .reshape(unit, 2 * heads * 3 * HEAD)
    )
    lower, upper = jnp.split(qkv_heads, 2, axis=1)
    mine, other = mine_of(lower, upper), mine_of(upper, lower)
    steps.pending += [a_one, mine, other]
    close()

    def split_rows(v):
        return v[:half], v[half:]

    qkv_w = Weight()
    have = qkv_w.have
    have[0, 0, 0, 0] = mine
    swapped = move(pp_zl, other)
    qkv_w.y(0, 0)
    qkv_w.zh(0, 0)
    ax = move(pp_x, a_one)
    close()
    a_top, a_bottom = split_rows(a_one)
    have[0, 0, 1, 0] = swapped
    swapped_parts = swapped[: unit // 2], swapped[unit // 2 :]

    def qkv_zh(c):
        for k, v in enumerate(move(ring_up, swapped_parts[c])):
            have[k + 1, 0, 1, c] = v

    qkv_zh(0)
    qkv_w.y(1, 0)
    az_top = move(pp_zl, a_top)
    close()
    qkv_zh(1)
    qkv_w.yz(0, 0)
    az_bottom = move(pp_zl, a_bottom)
    ad_top = move(pp_x, az_top)
    close()
    qkv_w.yz(1, 0)
    qkv_w.yz(1, 1)
    ad_bottom = move(pp_x, az_bottom)
    first, second = jnp.split(out_weight, 2, axis=0)
    swap_out = move(pp_zl, mine_of(second, first))
    near_one = stack_rows(a_one, ax, az_top, az_bottom, ad_top, ad_bottom)
    steps.pending.append(near_one)
    close()

    mine_out = joined(mine_of(first, second), swap_out, 1)
    out_w, up_w, down_w = Weight(), Weight(), Weight()
    chunk = unit // 2

    def up_part(side, c):
        rows = up_weight[c * chunk : (c + 1) * chunk]
        lower, upper = jnp.split(rows, 2, axis=1)
        return mine_of(lower, upper) if side == 0 else mine_of(upper, lower)

    def down_part(side, c):
        cols = down_weight[:, c * chunk : (c + 1) * chunk]
        lower, upper = jnp.split(cols, 2, axis=0)
        return mine_of(lower, upper) if side == 0 else mine_of(upper, lower)

    for c in range(2):
        up_w.have[0, 0, 0, c] = up_part(0, c)
        down_w.have[0, 0, 0, c] = down_part(0, c)
    out_w.have[0, 0, 0, 0] = mine_out

    def swap_up(c):
        up_w.have[0, 0, 1, c] = move(pp_zl, up_part(1, c))

    def swap_down(c):
        down_w.have[0, 0, 1, c] = move(pp_zl, down_part(1, c))

    cot = to_rel(out_cotangent)
    cot_top, cot_bottom = split_rows(cot)
    turn = jnp.full((1,), t, jnp.int32)
    head_index = t * 2 * heads + zl * heads + jnp.arange(heads)
    slopes = 2.0 ** (-8.0 * (head_index + 1).astype(F32) / H)
    starts = jnp.sum(
        (documents[:, None, :] < documents[:, :, None]).astype(jnp.int32), axis=-1
    )[:, :, None]

    w_qkv, at_qkv = qkv_w.blocks(0)
    far_one = move(pp_core, near_one)
    out_w.zh(0, 0)
    out_w.y(0, 0)
    swap_up(0)
    qkv = [run(deep, near_one, w_qkv, at_qkv, 0), deep(far_one, w_qkv, at_qkv, 0)]
    qkv = [v.reshape(2, 2, piece, 3 * width) for v in qkv]
    steps.pending += qkv
    close()

    def spec(cols):
        return pl.BlockSpec((1, 2, piece, cols), lambda s, h, *_: (s, 0, 0, h))

    start_spec = pl.BlockSpec((1, sequence, 1), lambda s, h, *_: (s, 0, 0))
    lse_spec = pl.BlockSpec((1, 1, sequence, 1), lambda s, h, *_: (s, h, 0, 0))
    block = pltpu.VMEM((sequence, HEAD), BF)
    wide = pltpu.VMEM((sequence, HEAD), F32)
    halves_shape = jax.ShapeDtypeStruct((2, 2, piece, width), BF)

    def attend(near, far):
        return pl.pallas_call(
            attention_forward,
            out_shape=(halves_shape, halves_shape, jax.ShapeDtypeStruct((2, heads, sequence, 1), F32)),
            grid_spec=pltpu.PrefetchScalarGridSpec(
                num_scalar_prefetch=2,
                grid=(2, heads),
                in_specs=[spec(3 * HEAD), spec(3 * HEAD), start_spec],
                out_specs=[spec(HEAD), spec(HEAD), lse_spec],
                scratch_shapes=[block] * 4,
            ),
            compiler_params=params(2),
            cost_estimate=cost(sequence, sequence, 2 * heads * HEAD * 4),
            name="attention_forward",
        )(turn, slopes, near, far, starts)

    out_w.yz(0, 0)
    up_w.zh(0, 0)
    up_w.y(0, 0)
    swap_up(1)
    cx_top = move(pp_x, cot_top)
    att_near, att_far, lse = run(attend, *qkv)
    att_near, att_far = (v.reshape(4 * piece, width) for v in (att_near, att_far))
    close()

    w_out = [out_w.have[k, j, 0, 0] for k, j in pairs]
    at_out = jnp.arange(len(pairs), dtype=jnp.int32) * (2 * unit // 128)
    far = run(broad, att_far, w_out, at_out, 0)
    got = move(pp_core, far)
    up_w.yz(0, 0)
    cx_bottom = move(pp_x, cot_bottom)
    cz_top = move(pp_zl, cot_top)
    e = run(broad, att_near, w_out, at_out, 0, got)
    close()

    def quarters(v):
        return [v[i * piece : (i + 1) * piece] for i in range(4)]

    e00, ex, ez, ed = quarters(e)
    from_d = move(pp_x, ed)
    up_w.zh(0, 1)
    up_w.y(0, 1)
    swap_down(0)
    close()
    from_x = move(pp_x, ex)
    from_z = move(pp_zl, plus(ez, from_d))
    up_w.zh(1, 0)
    up_w.yz(0, 1)
    up_w.y(1, 0)
    close()
    resid = x + (e00.astype(F32) + from_x.astype(F32) + from_z.astype(F32))
    normed_two, inverse_two = norm_forward(resid)
    a_two = (normed_two * gain_two).astype(BF)
    steps.pending.append(a_two)
    close()

    ax = move(pp_x, a_two)
    az = move(pp_zl, a_two)
    up_w.zh(1, 1)
    up_w.yz(1, 0)
    up_w.y(1, 1)
    close()
    ad = move(pp_x, az)
    up_w.yz(1, 1)
    down_w.zh(0, 0)
    down_w.y(0, 0)
    swap_down(1)
    close()
    near_two = stack_rows(a_two, ax, az, ad)

    w_up, at_up = up_w.blocks(0)

    def lift(rows):
        return deep(
            rows, w_up, at_up, 0, finish=gelu_and_slope, outs=2, tm=1280, parts=5
        )

    far_two = move(pp_core, near_two)
    down_w.zh(0, 1)
    down_w.yz(0, 0)
    down_w.y(0, 1)
    cz_bottom = move(pp_zl, cot_bottom)
    act_near, slope_near = run(lift, near_two)
    close()
    down_w.zh(1, 0)
    down_w.yz(0, 1)
    down_w.y(1, 0)
    cd_top = move(pp_x, cz_top)
    cd_bottom = move(pp_x, cz_bottom)
    act_far, slope_far = run(lift, far_two)
    near_cot = stack_rows(cot, cx_top, cx_bottom, cz_top, cz_bottom, cd_top, cd_bottom)
    steps.pending.append(near_cot)
    close()

    def cuts(j):
        return [((2 * k + j) * 2 + l, unit) for k in far_first for l in range(2)]

    def keys(j):
        return [(k, j, l) for k in far_first for l in range(2)]

    class Sum:
        def __init__(self, axis):
            self.parts = {}
            self.sums = {}
            self.value = {}
            self.axis = axis

        def make(self, j, a_pair, b_pair, first):
            side = self.axis

            def go(v, *_):
                pair = (v, a_pair[1])
                return gram(pair, b_pair, cuts(j), side)

            for key, v in zip(keys(j), run(go, a_pair[0])):
                self.parts[key] = v

        def y_far(self, l):
            for k in range(ring - 1, 0, -1):
                self.sums[k, l] = plus(self.parts[k, 0, l], move(pp_y, self.parts[k, 1, l]))

        def y_own(self, l):
            self.sums[0, l] = plus(self.parts[0, 0, l], move(pp_y, self.parts[0, 1, l]))

        def cut(self, v, r, of):
            size = v.shape[1 - self.axis] // of
            return lax.slice_in_dim(v, r * size, (r + 1) * size, axis=1 - self.axis)

        def zh(self, l, r=0, of=2):
            value = self.cut(self.sums[ring - 1, l], r, of)
            for k in range(ring - 2, 0, -1):
                value = plus(move(pp_down, value), self.cut(self.sums[k, l], r, of))
            self.value[l, r] = move(pp_down, value)

        def zl(self, r=0, of=2):
            first, second = (
                plus(self.value[l, r], self.cut(self.sums[0, l], r, of)) for l in range(2)
            )
            self.value[2, r] = mine_of(first, second)
            self.value[3, r] = move(pp_zl, mine_of(second, first))

        def result(self, of=2):
            mine = [self.value[2, r] for r in range(of)]
            other = [self.value[3, r] for r in range(of)]
            if of == 1:
                return mine[0], other[0]
            return tuple(jnp.concatenate(v, axis=1 - self.axis) for v in (mine, other))

    down_g, up_g, out_g, qkv_g = Sum(1), Sum(0), Sum(1), Sum(0)
    acts = (act_near, act_far)
    far_cot = move(pp_core, near_cot)
    down_w.zh(1, 1)
    down_w.yz(1, 0)
    down_w.y(1, 1)
    down_g.make(1, acts, (near_cot, far_cot), None)
    close()
    down_w.yz(1, 1)
    down_g.make(0, acts, (near_cot, far_cot), None)
    close()

    w_down, at_down = down_w.blocks(1)

    def pull(rows, slope):
        return deep(
            rows, w_down, at_down, 1, finish=lambda total, s: (total * s.astype(F32),), extra=(slope,), tm=640, parts=2
        )

    down_g.y_far(0)
    du_far = run(pull, far_cot, slope_far)
    far = broad(du_far, w_up, at_up, 1)
    steps.pending.append(far)
    close()
    got = move(pp_core, far)
    down_g.y_far(1)
    down_g.zh(0, 0)
    du_near = run(pull, near_cot, slope_near)
    e = broad(du_near, w_up, at_up, 1, got)
    steps.pending.append(e)
    close()

    e00, ex, ez, ed = quarters(e)
    from_d = move(pp_x, ed)
    down_g.y_own(0)
    down_g.zh(0, 1)
    dus = (du_near, du_far)
    up_g.make(1, (near_two, far_two), dus, None)
    up_g.make(0, (near_two, far_two), dus, None)
    close()
    from_x = move(pp_x, ex)
    from_z = move(pp_zl, plus(ez, from_d))
    down_g.y_own(1)
    down_g.zh(1, 0)
    far = run(broad, act_far, w_down, at_down, 0)
    close()
    grad_in_two = e00.astype(F32) + from_x.astype(F32) + from_z.astype(F32)
    grad_part, grad_gain_two = norm_backward(grad_in_two, normed_two, inverse_two, gain_two)
    grad_resid = cot.astype(F32) + grad_part
    grad_rows = grad_resid.astype(BF)
    steps.pending.append(grad_rows)
    close()

    ax = move(pp_x, grad_rows)
    az = move(pp_zl, grad_rows)
    got = move(pp_core, far)
    up_g.y_far(0)
    down_g.zh(1, 1)
    e_out = run(broad, act_near, w_down, at_down, 0, got)
    close()
    ad = move(pp_x, az)
    up_g.y_far(1)
    up_g.zh(0, 0)
    down_g.zl(0)
    close()
    near_grad = stack_rows(grad_rows, ax, az, ad)

    proj_shape = jax.ShapeDtypeStruct((2, 2, piece, 3 * width), BF)

    def attend_back(near, far):
        return pl.pallas_call(
            attention_backward,
            out_shape=(proj_shape, proj_shape),
            grid_spec=pltpu.PrefetchScalarGridSpec(
                num_scalar_prefetch=2,
                grid=(2, heads),
                in_specs=[spec(3 * HEAD), spec(3 * HEAD), spec(HEAD), spec(HEAD), start_spec, lse_spec],
                out_specs=[spec(3 * HEAD), spec(3 * HEAD)],
                scratch_shapes=[block] * 5 + [wide] * 2,
            ),
            compiler_params=params(2),
            cost_estimate=cost(sequence, sequence, 2 * heads * HEAD * 8),
            name="attention_backward",
        )(turn, slopes, *qkv, near, far, starts, lse)

    o00, ox, oz, od = quarters(e_out)
    far_grad = move(pp_core, near_grad)
    from_od = move(pp_x, od)
    up_g.y_own(0)
    up_g.zh(0, 1)
    down_g.zl(1)
    grad_att = [
        v.reshape(2, 2, piece, width)
        for v in (run(deep, near_grad, w_out, at_out, 1), deep(far_grad, w_out, at_out, 1))
    ]
    proj = attend_back(*grad_att)
    proj = tuple(v.reshape(4 * piece, 3 * width) for v in proj)
    steps.pending += proj
    close()

    rows_one = (near_one, far_one)
    up_g.y_own(1)
    up_g.zh(1, 0)
    qkv_g.make(1, rows_one, proj, None)
    qkv_g.make(0, rows_one, proj, None)
    close()

    qkv_g.y_far(0)
    up_g.zh(1, 1)
    from_ox = move(pp_x, ox)
    from_oz = move(pp_zl, plus(oz, from_od))
    far = run(broad, proj[1], w_qkv, at_qkv, 1)
    got = move(pp_core, far)
    e = run(broad, proj[0], w_qkv, at_qkv, 1, got)
    close()
    block_out = from_rel(
        (resid + (o00.astype(F32) + from_ox.astype(F32) + from_oz.astype(F32))).astype(BF)
    )

    e00, ex, ez, ed = quarters(e)
    from_d = move(pp_x, ed)
    qkv_g.y_far(1)
    qkv_g.zh(0, 0, 1)
    up_g.zl(0)
    atts = (att_near, att_far)
    out_g.make(1, atts, (near_grad, far_grad), None)
    out_g.make(0, atts, (near_grad, far_grad), None)
    close()
    from_x = move(pp_x, ex)
    from_z = move(pp_zl, plus(ez, from_d))
    qkv_g.zh(1, 0, 1)
    qkv_g.y_own(0)
    qkv_g.y_own(1)
    close()
    grad_in_one = e00.astype(F32) + from_x.astype(F32) + from_z.astype(F32)
    grad_part, grad_gain_one = norm_backward(grad_in_one, normed_one, inverse_one, gain_one)
    grad_in = from_rel(grad_resid + grad_part)

    out_g.y_far(0)
    out_g.y_far(1)
    up_g.zl(1)
    qkv_g.zl(0, 1)
    close()
    out_g.zh(0, 0, 1)
    out_g.zh(1, 0, 1)
    out_g.y_own(0)
    out_g.y_own(1)
    close()
    out_g.zl(0, 1)

    grad_down = joined(*down_g.result(), 0).astype(F32)
    grad_up = joined(*up_g.result(), 1).astype(F32)
    grad_out = joined(*out_g.result(1), 0).astype(F32)

    def parts_first(v):
        return v.reshape(unit, heads, 3, HEAD).transpose(0, 2, 1, 3).reshape(unit, 3, width)

    mine, other = qkv_g.result(1)
    grad_qkv = joined(parts_first(mine), parts_first(other), 2).astype(F32)

    def total(v):
        v = from_rel(v)
        for step in (pp_core, pp_x, pp_zl, pp_y):
            v = v + step(v)
        moving = v
        for _ in range(ring - 1):
            moving = pp_up(moving)
            v = v + moving
        size = D // (n * tp)
        return lax.dynamic_slice_in_dim(v, (f * tp + t) * size, size)

    return (
        block_out,
        grad_in,
        total(grad_gain_one),
        total(grad_gain_two),
        grad_qkv,
        grad_out,
        grad_up,
        grad_down,
    )


def solution(mesh):
    return jax.shard_map(
        on_device,
        mesh=mesh,
        in_specs=(
            P(("fsdp", "tp"), None),
            P("fsdp", None),
            P("fsdp", None, "tp"),
            P("tp", "fsdp"),
            P("fsdp", "tp"),
            P("tp", "fsdp"),
            P("fsdp"),
            P("fsdp"),
            P(("fsdp", "tp"), None),
        ),
        out_specs=(
            P(("fsdp", "tp"), None),
            P(("fsdp", "tp"), None),
            P(("fsdp", "tp")),
            P(("fsdp", "tp")),
            P("fsdp", None, "tp"),
            P("tp", "fsdp"),
            P("fsdp", "tp"),
            P("tp", "fsdp"),
        ),
        check_vma=False,
    )
```

time: 2840 us -> 1950 us (0.69)
  waiting for transfers between devices: 1780 us -> 863 us
  Pallas kernels: 65.9 us -> 718 us
  matrix products: 552 us -> 0 us
  other arithmetic: 209 us -> 144 us
  local copies, waits for them, and re-layouts: 115 us -> 80.4 us
    ppermute x122 -> x126, waiting for transfers between devices: 1780 us -> 863 us  [over(): return lambda v: lax.ppermute(v, axis, [(i, to(i)) for i in range(size)])]
    pallas_call x2 -> x30, Pallas kernels: 65.9 us -> 718 us  [the longest x8 206 us: gram(): pl.pallas_call(body, out_shape=[jax.ShapeDtypeStruct((m, n), BF)] * count...]
    dot_general x28 -> x0, matrix products: 552 us -> none  [dot(): lax.dot_general(left, right, (((cl,), (cr,)), ((), ())), preferred_elemen...]
    unnamed x88 -> x51, other arithmetic: 95.5 us -> 24 us
    unnamed x176 -> x272, local copies, waits for them, and re-layouts: 72.5 us -> 41.2 us
    ppermute x122 -> x126, starting transfers between devices: 114 us -> 139 us  [over(): return lambda v: lax.ppermute(v, axis, [(i, to(i)) for i in range(size)])]
    convert_element_type x16 -> x24, other arithmetic: 58.4 us -> 60.5 us  [the longest x16 31.3 us: plus(): return (a.astype(F32) + b.astype(F32)).astype(BF)]
  transfers between devices with their start and end apart: 122 -> 126, of which waited for: 54 -> 51; matrix products, arithmetic and copies ran while one was open for 19% -> 9% of each run, Pallas kernels for 1% -> 34%
where the time goes in v2:
time: 1950 us
  waiting for transfers between devices  863 us (44%)
  Pallas kernels  718 us (37%)
  other arithmetic  144 us (7%)
  starting transfers between devices  139 us (7%)
  local copies, waits for them, and re-layouts  80.4 us (4%)
    ppermute x126, waiting for transfers between devices, over(): return lambda v: lax.ppermute(v, axis, [(i, to(i)) for i in range(size)])  863 us
    pallas_call x8, Pallas kernels, gram(): pl.pallas_call(body, out_shape=[jax.ShapeDtypeStruct((m, n), BF)] * count...  206 us
    pallas_call x8, Pallas kernels, deep(): pl.pallas_call(body, out_shape=[jax.ShapeDtypeStruct((m, n), BF)] * outs,...  206 us
    pallas_call x8, Pallas kernels, broad(): pl.pallas_call(body, out_shape=jax.ShapeDtypeStruct((m, n), BF), grid_spe...  204 us
    ppermute x126, starting transfers between devices, over(): return lambda v: lax.ppermute(v, axis, [(i, to(i)) for i in range(size)])  139 us
    unnamed x272, local copies, waits for them, and re-layouts  41.2 us
  transfers between devices with their start and end apart: 126, of which 51 were waited for; matrix products, arithmetic and copies ran while one was open for 9% of the time, Pallas kernels for 34%

profile of v2, /device:TPU:0, one launch (start us, length us, event | category | flops | bytes accessed | tf_op | source)
XLA Modules:
  0.0 1947.6 jit_solution(7353316967490255867)
XLA Ops:
  76.3 35.8 %collective-permute-done.6.rest_4_ = bf16[512,1536]{1,0:T(8,128)(2,1)S(1)} collective-permute-done((bf16[512,1536]{1,0:T(8,128)(2,1)S(1)}, bf16[512,1536]{1,0:T(8,128)(2,1)S(1)}, u32[]{:S(2)}, u32[]{:S(2)}) %collective-permute-start.6) | collective-permute-done | bytes 1572896 | tf_op jit(solution)/shard_map/ppermute | solution.py:421
  118.7 41.8 %collective-permute-done.8.rest_5_ = bf16[256,1536]{1,0:T(8,128)(2,1)S(1)} collective-permute-done((bf16[256,1536]{1,0:T(8,128)(2,1)S(1)}, bf16[256,1536]{1,0:T(8,128)(2,1)S(1)}, u32[]{:S(2)}, u32[]{:S(2)}) %collective-permute-start.8) | collective-permute-done | bytes 786464 | tf_op jit(solution)/shard_map/ppermute | solution.py:421
  166.9 41.5 %collective-permute-done.12.rest_6_ = bf16[256,1536]{1,0:T(8,128)(2,1)S(1)} collective-permute-done((bf16[256,1536]{1,0:T(8,128)(2,1)S(1)}, bf16[256,1536]{1,0:T(8,128)(2,1)S(1)}, u32[]{:S(2)}, u32[]{:S(2)}) %collective-permute-start.12) | collective-permute-done | bytes 786464 | tf_op jit(solution)/shard_map/ppermute | solution.py:421
  426.7 44.6 %collective-permute-done.33.rest_9_ = bf16[256,2048]{1,0:T(8,128)(2,1)S(1)} collective-permute-done((bf16[256,2048]{1,0:T(8,128)(2,1)S(1)}, bf16[256,2048]{1,0:T(8,128)(2,1)S(1)}, u32[]{:S(2)}, u32[]{:S(2)}) %collective-permute-start.33) | collective-permute-done | bytes 1048608 | tf_op jit(solution)/shard_map/ppermute | solution.py:421
  504.5 51.8 %collective-permute-done.38.rest_10_ = bf16[256,2048]{1,0:T(8,128)(2,1)S(1)} collective-permute-done((bf16[256,2048]{1,0:T(8,128)(2,1)S(1)}, bf16[256,2048]{1,0:T(8,128)(2,1)S(1)}, u32[]{:S(2)}, u32[]{:S(2)}) %collective-permute-start.38) | collective-permute-done | bytes 1048608 | tf_op jit(solution)/shard_map/ppermute | solution.py:421
  595.9 50.7 %collective-permute-done.43.rest_11_ = bf16[256,2048]{1,0:T(8,128)(2,1)S(1)} collective-permute-done((bf16[256,2048]{1,0:T(8,128)(2,1)}, bf16[256,2048]{1,0:T(8,128)(2,1)S(1)}, u32[]{:S(2)}, u32[]{:S(2)}) %collective-permute-start.43) | collective-permute-done | bytes 1048608 | tf_op jit(solution)/shard_map/ppermute | solution.py:421
  652.6 42.0 %collective-permute-done.47.rest_15_ = bf16[256,2048]{1,0:T(8,128)(2,1)S(1)} collective-permute-done((bf16[256,2048]{1,0:T(8,128)(2,1)S(1)}, bf16[256,2048]{1,0:T(8,128)(2,1)S(1)}, u32[]{:S(2)}, u32[]{:S(2)}) %collective-permute-start.47) | collective-permute-done | bytes 1048608 | tf_op jit(solution)/shard_map/ppermute | solution.py:421
  717.4 34.1 %deep.10 = (bf16[1280,2048]{1,0:T(8,128)(2,1)}, bf16[1280,2048]{1,0:T(8,128)(2,1)}) custom-call(s32[16]{0:T(128)} %stack.110.starts_ref, bf16[1280,4096]{1,0:T(8,128)(2,1)} %stack_rows.5.a_ref.a0, bf16[256,2048]{1,0:T(8,128)(2,1)} %get-tuple-element.219.rest_0_, bf16[256,2048]{1,0:T(8,128)(2,1)} %get-tuple-element.233.rest_1_, bf16[256,2048]{1,0:T(8,128)(2,1)} %copy-done.20, ...), custom_call_target="tpu_custom_call" | custom-call | flops 1073741824 | bytes 32505856 | tf_op jit(solution)/shard_map/deep/pallas_call | solution.py:216
  773.2 33.8 %deep.11 = (bf16[1280,2048]{1,0:T(8,128)(2,1)}, bf16[1280,2048]{1,0:T(8,128)(2,1)}) custom-call(s32[16]{0:T(128)} %stack.110.starts_ref, bf16[1280,4096]{1,0:T(8,128)(2,1)} %collective-permute-done.51.a_ref.a1, bf16[256,2048]{1,0:T(8,128)(2,1)} %get-tuple-element.219.rest_0_, bf16[256,2048]{1,0:T(8,128)(2,1)} %get-tuple-element.233.rest_1_, ...), custom_call_target="tpu_custom_call" | custom-call | flops 1073741824 | bytes 32505856 | tf_op jit(solution)/shard_map/deep/pallas_call | solution.py:216
  850.8 32.5 %gram.8 = (bf16[2048,512]{1,0:T(8,128)(2,1)}, bf16[2048,512]{1,0:T(8,128)(2,1)}, bf16[2048,512]{1,0:T(8,128)(2,1)}, bf16[2048,512]{1,0:T(8,128)(2,1)}) custom-call(s32[4]{0:T(128)} %constant.339.clone.index_ref, bf16[1280,2048]{1,0:T(8,128)(2,1)} %get-tuple-element.310.a0.a_ref, bf16[1280,2048]{1,0:T(8,128)(2,1)} %get-tuple-element.307.a1.a_ref, ...), custom_call_target="tpu_custom_call" | custom-call | flops 1073741824 | bytes 29360128 | tf_op jit(solution)/shard_map/gram/pallas_call | solution.py:163
  885.0 32.3 %gram.9 = (bf16[2048,512]{1,0:T(8,128)(2,1)}, bf16[2048,512]{1,0:T(8,128)(2,1)}, bf16[2048,512]{1,0:T(8,128)(2,1)}, bf16[2048,512]{1,0:T(8,128)(2,1)}) custom-call(s32[4]{0:T(128)} %constant.340.clone.index_ref, bf16[1280,2048]{1,0:T(8,128)(2,1)} %get-tuple-element.310.a0.a_ref, bf16[1280,2048]{1,0:T(8,128)(2,1)} %get-tuple-element.307.a1.a_ref, ...), custom_call_target="tpu_custom_call" | custom-call | flops 1073741824 | bytes 29360128 | tf_op jit(solution)/shard_map/gram/pallas_call | solution.py:163
  919.0 32.9 %deep.12.a_ref.b1 = bf16[1280,2048]{1,0:T(8,128)(2,1)} custom-call(s32[16]{0:T(128)} %stack.110.starts_ref, bf16[1280,4096]{1,0:T(8,128)(2,1)} %collective-permute-done.61.b1.a_ref, bf16[2048,256]{1,0:T(8,128)(2,1)} %copy-done.10, bf16[2048,256]{1,0:T(8,128)(2,1)} %get-tuple-element.253.rest_1_, bf16[2048,256]{1,0:T(8,128)(2,1)} %copy-done.18, ...), custom_call_target="tpu_custom_call" | custom-call | flops 1073741824 | bytes 32505856 | tf_op jit(solution)/shard_map/deep/pallas_call | solution.py:216
  951.9 32.2 %broad.10 = bf16[1280,4096]{1,0:T(8,128)(2,1)} custom-call(s32[16]{0:T(128)} %stack.110.starts_ref, bf16[1280,2048]{1,0:T(8,128)(2,1)} %deep.12.a_ref.b1, bf16[256,2048]{1,0:T(8,128)(2,1)} %get-tuple-element.219.rest_0_, bf16[256,2048]{1,0:T(8,128)(2,1)} %get-tuple-element.233.rest_1_, bf16[256,2048]{1,0:T(8,128)(2,1)} %copy-done.20, ...), custom_call_target="tpu_custom_call" | custom-call | flops 1073741824 | bytes 32505856 | tf_op jit(solution)/shard_map/broad/pallas_call | solution.py:250
  991.7 32.9 %deep.13.a_ref.b0 = bf16[1280,2048]{1,0:T(8,128)(2,1)} custom-call(s32[16]{0:T(128)} %stack.110.starts_ref, bf16[1280,4096]{1,0:T(8,128)(2,1)} %stack_rows.6.b0.a_ref, bf16[2048,256]{1,0:T(8,128)(2,1)} %copy-done.10, bf16[2048,256]{1,0:T(8,128)(2,1)} %get-tuple-element.253.rest_1_, bf16[2048,256]{1,0:T(8,128)(2,1)} %copy-done.18, ...), custom_call_target="tpu_custom_call" | custom-call | flops 1073741824 | bytes 32505856 | tf_op jit(solution)/shard_map/deep/pallas_call | solution.py:216
  1024.7 32.7 %broad.11 = bf16[1280,4096]{1,0:T(8,128)(2,1)} custom-call(s32[16]{0:T(128)} %stack.110.starts_ref, bf16[1280,2048]{1,0:T(8,128)(2,1)} %deep.13.a_ref.b0, bf16[256,2048]{1,0:T(8,128)(2,1)} %get-tuple-element.219.rest_0_, bf16[256,2048]{1,0:T(8,128)(2,1)} %get-tuple-element.233.rest_1_, bf16[256,2048]{1,0:T(8,128)(2,1)} %copy-done.20, ...), custom_call_target="tpu_custom_call" | custom-call | flops 1073741824 | bytes 32505856 | tf_op jit(solution)/shard_map/broad/pallas_call | solution.py:250
  1066.9 32.5 %gram.11 = (bf16[512,2048]{1,0:T(8,128)(2,1)}, bf16[512,2048]{1,0:T(8,128)(2,1)}, bf16[512,2048]{1,0:T(8,128)(2,1)}, bf16[512,2048]{1,0:T(8,128)(2,1)}) custom-call(s32[4]{0:T(128)} %constant.340.clone.index_ref, bf16[1280,4096]{1,0:T(8,128)(2,1)} %stack_rows.5.a_ref.a0, bf16[1280,4096]{1,0:T(8,128)(2,1)} %collective-permute-done.51.a_ref.a1, ...), custom_call_target="tpu_custom_call" | custom-call | flops 1073741824 | bytes 52953088 | tf_op jit(solution)/shard_map/gram/pallas_call | solution.py:163
  1099.4 32.7 %gram.10 = (bf16[512,2048]{1,0:T(8,128)(2,1)}, bf16[512,2048]{1,0:T(8,128)(2,1)}, bf16[512,2048]{1,0:T(8,128)(2,1)}, bf16[512,2048]{1,0:T(8,128)(2,1)}) custom-call(s32[4]{0:T(128)} %constant.339.clone.index_ref, bf16[1280,4096]{1,0:T(8,128)(2,1)} %stack_rows.5.a_ref.a0, bf16[1280,4096]{1,0:T(8,128)(2,1)} %collective-permute-done.51.a_ref.a1, ...), custom_call_target="tpu_custom_call" | custom-call | flops 1073741824 | bytes 52953088 | tf_op jit(solution)/shard_map/gram/pallas_call | solution.py:163
  1176.6 41.8 %collective-permute-done.74 = bf16[320,4096]{1,0:T(8,128)(2,1)S(1)} collective-permute-done((bf16[320,4096]{1,0:T(8,128)(2,1)}, bf16[320,4096]{1,0:T(8,128)(2,1)S(1)}, u32[]{:S(2)}, u32[]{:S(2)}) %collective-permute-start.74) | collective-permute-done | bytes 2621472 | tf_op jit(solution)/shard_map/ppermute | solution.py:421
  1249.8 32.8 %broad.13 = bf16[1280,4096]{1,0:T(8,128)(2,1)} custom-call(s32[16]{0:T(128)} %stack.110.starts_ref, bf16[1280,2048]{1,0:T(8,128)(2,1)} %get-tuple-element.310.a0.a_ref, bf16[2048,256]{1,0:T(8,128)(2,1)} %copy-done.10, bf16[2048,256]{1,0:T(8,128)(2,1)} %get-tuple-element.253.rest_1_, bf16[2048,256]{1,0:T(8,128)(2,1)} %copy-done.18, ...), custom_call_target="tpu_custom_call" | custom-call | flops 1073741824 | bytes 32505856 | tf_op jit(solution)/shard_map/broad/pallas_call | solution.py:250
  1331.0 43.7 %collective-permute-done.85 = bf16[1024,512]{1,0:T(8,128)(2,1)S(1)} collective-permute-done((bf16[1024,512]{1,0:T(8,128)(2,1)S(1)}, bf16[1024,512]{1,0:T(8,128)(2,1)S(1)}, u32[]{:S(2)}, u32[]{:S(2)}) %collective-permute-start.85) | collective-permute-done | bytes 1048608 | tf_op jit(solution)/shard_map/ppermute | solution.py:421
  1417.5 38.6 %attention_backward.1 = (bf16[2,2,320,1536]{3,2,1,0:T(8,128)(2,1)}, bf16[2,2,320,1536]{3,2,1,0:T(8,128)(2,1)}) custom-call(s32[1]{0:T(128)} %bitcast.turn_ref, f32[4]{0:T(128)} %multiply_power_fusion.slope_ref, bf16[2,2,320,1536]{3,2,1,0:T(8,128)(2,1)} %bitcast.49, bf16[2,2,320,1536]{3,2,1,0:T(8,128)(2,1)} %bitcast.51, bf16[2,2,320,512]{3,2,1,0:T(8,128)(2,1)} %bitcast.74, ...), custom_call_target="tpu_custom_call" | custom-call | flops 1342177280 | bytes 45219840 | tf_op jit(solution)/shard_map/attention_backward/pallas_call | solution.py:833
  1615.3 33.8 %collective-permute-done.97 = bf16[512,1024]{1,0:T(8,128)(2,1)S(1)} collective-permute-done((bf16[512,1024]{1,0:T(8,128)(2,1)}, bf16[512,1024]{1,0:T(8,128)(2,1)S(1)}, u32[]{:S(2)}, u32[]{:S(2)}) %collective-permute-start.97) | collective-permute-done | bytes 1048608 | tf_op jit(solution)/shard_map/ppermute | solution.py:421
  1745.9 69.2 %collective-permute-done.115 = bf16[512,1536]{1,0:T(8,128)(2,1)S(1)} collective-permute-done((bf16[512,1536]{1,0:T(8,128)(2,1)S(1)}, bf16[512,1536]{1,0:T(8,128)(2,1)S(1)}, u32[]{:S(2)}, u32[]{:S(2)}) %collective-permute-start.115) | collective-permute-done | bytes 1572896 | tf_op jit(solution)/shard_map/ppermute | solution.py:421
  1842.5 34.5 %collective-permute-done.106 = f32[4096]{0:T(1024)S(1)} collective-permute-done((f32[4096]{0:T(1024)S(1)}, f32[4096]{0:T(1024)S(1)}, u32[]{:S(2)}, u32[]{:S(2)}) %collective-permute-start.106) | collective-permute-done | bytes 16416 | tf_op jit(solution)/shard_map/ppermute | solution.py:421
  (683 shorter events, 1013.3 us)
Async XLA Ops:
  476.8 79.6 %collective-permute-start.36 = (bf16[320,4096]{1,0:T(8,128)(2,1)S(1)}, bf16[320,4096]{1,0:T(8,128)(2,1)S(1)}, u32[]{:S(2)}, u32[]{:S(2)}) collective-permute-start(bf16[320,4096]{1,0:T(8,128)(2,1)S(1)} %get-tuple-element.236), channel_id=1, source_target_pairs={{0,2},{1,3},{2,0},{3,1},{4,6},{5,7},{6,4},{7,5},{8,10},{9,11},{10,... | collective-permute-start | bytes 7864328 | tf_op jit(solution)/shard_map/ppermute | solution.py:421
  478.2 80.4 %collective-permute-start.37 = (bf16[320,4096]{1,0:T(8,128)(2,1)S(1)}, bf16[320,4096]{1,0:T(8,128)(2,1)}, u32[]{:S(2)}, u32[]{:S(2)}) collective-permute-start(bf16[320,4096]{1,0:T(8,128)(2,1)S(1)} %add_convert_fusion.4), channel_id=1, source_target_pairs={{0,8},{4,12},{8,0},{12,4},{16,24},{20,28},{24,16},{28,20},{1,9},{5... | collective-permute-start | bytes 7864328 | tf_op jit(solution)/shard_map/ppermute | solution.py:421
  480.0 76.4 %collective-permute-start.38 = (bf16[256,2048]{1,0:T(8,128)(2,1)S(1)}, bf16[256,2048]{1,0:T(8,128)(2,1)S(1)}, u32[]{:S(2)}, u32[]{:S(2)}) collective-permute-start(bf16[256,2048]{1,0:T(8,128)(2,1)S(1)} %copy-done.21), channel_id=1, source_target_pairs={{0,16},{4,20},{8,24},{12,28},{16,0},{20,4},{24,8},{28,12},{1,17},{... | collective-permute-start | bytes 3145736 | tf_op jit(solution)/shard_map/ppermute | solution.py:421
  566.0 80.6 %collective-permute-start.41 = (bf16[320,4096]{1,0:T(8,128)(2,1)S(1)}, bf16[320,4096]{1,0:T(8,128)(2,1)S(1)}, u32[]{:S(2)}, u32[]{:S(2)}) collective-permute-start(bf16[320,4096]{1,0:T(8,128)(2,1)S(1)} %multiply_convert_fusion.refs_0_), channel_id=1, source_target_pairs={{0,2},{1,3},{2,0},{3,1},{4,6},{5,7},{6,4},{7,5},{8,10},{9,11},{10,... | collective-permute-start | bytes 7864328 | tf_op jit(solution)/shard_map/ppermute | solution.py:421
  567.6 79.6 %collective-permute-start.42 = (bf16[320,4096]{1,0:T(8,128)(2,1)S(1)}, bf16[320,4096]{1,0:T(8,128)(2,1)S(1)}, u32[]{:S(2)}, u32[]{:S(2)}) collective-permute-start(bf16[320,4096]{1,0:T(8,128)(2,1)S(1)} %multiply_convert_fusion.refs_0_), channel_id=1, source_target_pairs={{0,8},{4,12},{8,0},{12,4},{16,24},{20,28},{24,16},{28,20},{1,9},{5... | collective-permute-start | bytes 7864328 | tf_op jit(solution)/shard_map/ppermute | solution.py:421
  571.3 75.3 %collective-permute-start.43 = (bf16[256,2048]{1,0:T(8,128)(2,1)}, bf16[256,2048]{1,0:T(8,128)(2,1)S(1)}, u32[]{:S(2)}, u32[]{:S(2)}) collective-permute-start(bf16[256,2048]{1,0:T(8,128)(2,1)} %collective-permute-done.26.rest_3_), channel_id=1, source_target_pairs={{0,16},{4,20},{8,24},{12,28},{16,0},{20,4},{24,8},{28,12},{1,17},{... | collective-permute-start | bytes 3145736 | tf_op jit(solution)/shard_map/ppermute | solution.py:421
  572.1 74.5 %collective-permute-start.45 = (bf16[256,2048]{1,0:T(8,128)(2,1)}, bf16[256,2048]{1,0:T(8,128)(2,1)S(1)}, u32[]{:S(2)}, u32[]{:S(2)}) collective-permute-start(bf16[256,2048]{1,0:T(8,128)(2,1)} %collective-permute-done.26.rest_3_), channel_id=1, source_target_pairs={{0,4},{4,0},{8,12},{12,8},{16,20},{20,16},{24,28},{28,24},{1,5},{5... | collective-permute-start | bytes 3145736 | tf_op jit(solution)/shard_map/ppermute | solution.py:421
  985.4 76.6 %collective-permute-start.68 = (bf16[2048,512]{1,0:T(8,128)(2,1)}, bf16[2048,512]{1,0:T(8,128)(2,1)S(1)}, u32[]{:S(2)}, u32[]{:S(2)}) collective-permute-start(bf16[2048,512]{1,0:T(8,128)(2,1)} %get-tuple-element.286), channel_id=1, source_target_pairs={{0,4},{4,0},{8,12},{12,8},{16,20},{20,16},{24,28},{28,24},{1,5},{5... | collective-permute-start | bytes 6291464 | tf_op jit(solution)/shard_map/ppermute | solution.py:421
  1137.8 80.6 %collective-permute-start.74 = (bf16[320,4096]{1,0:T(8,128)(2,1)}, bf16[320,4096]{1,0:T(8,128)(2,1)S(1)}, u32[]{:S(2)}, u32[]{:S(2)}) collective-permute-start(bf16[320,4096]{1,0:T(8,128)(2,1)} %add_convert_fusion.3), channel_id=1, source_target_pairs={{0,8},{4,12},{8,0},{12,4},{16,24},{20,28},{24,16},{28,20},{1,9},{5... | collective-permute-start | bytes 7864328 | tf_op jit(solution)/shard_map/ppermute | solution.py:421
  1139.2 79.2 %collective-permute-start.73 = (bf16[320,4096]{1,0:T(8,128)(2,1)}, bf16[320,4096]{1,0:T(8,128)(2,1)}, u32[]{:S(2)}, u32[]{:S(2)}) collective-permute-start(bf16[320,4096]{1,0:T(8,128)(2,1)} %get-tuple-element.303), channel_id=1, source_target_pairs={{0,2},{1,3},{2,0},{3,1},{4,6},{5,7},{6,4},{7,5},{8,10},{9,11},{10,... | collective-permute-start | bytes 7864328 | tf_op jit(solution)/shard_map/ppermute | solution.py:421
  1140.7 83.0 %collective-permute-start.75 = (bf16[2048,512]{1,0:T(8,128)(2,1)}, bf16[2048,512]{1,0:T(8,128)(2,1)}, u32[]{:S(2)}, u32[]{:S(2)}) collective-permute-start(bf16[2048,512]{1,0:T(8,128)(2,1)} %get-tuple-element.305), channel_id=1, source_target_pairs={{0,4},{4,0},{8,12},{12,8},{16,20},{20,16},{24,28},{28,24},{1,5},{5... | collective-permute-start | bytes 6291464 | tf_op jit(solution)/shard_map/ppermute | solution.py:421
  1143.9 79.8 %collective-permute-start.76 = (bf16[1024,512]{1,0:T(8,128)(2,1)}, bf16[1024,512]{1,0:T(8,128)(2,1)}, u32[]{:S(2)}, u32[]{:S(2)}) collective-permute-start(bf16[1024,512]{1,0:T(8,128)(2,1)} %get-tuple-element.306), channel_id=1, source_target_pairs={{0,16},{4,20},{8,24},{12,28},{16,0},{20,4},{24,8},{28,12},{1,17},{... | collective-permute-start | bytes 3145736 | tf_op jit(solution)/shard_map/ppermute | solution.py:421
  1233.5 80.9 %collective-permute-start.78 = (bf16[320,4096]{1,0:T(8,128)(2,1)S(1)}, bf16[320,4096]{1,0:T(8,128)(2,1)S(1)}, u32[]{:S(2)}, u32[]{:S(2)}) collective-permute-start(bf16[320,4096]{1,0:T(8,128)(2,1)S(1)} %get-tuple-element.312.refs_0_), channel_id=1, source_target_pairs={{0,2},{1,3},{2,0},{3,1},{4,6},{5,7},{6,4},{7,5},{8,10},{9,11},{10,... | collective-permute-start | bytes 7864328 | tf_op jit(solution)/shard_map/ppermute | solution.py:421
  1235.0 81.6 %collective-permute-start.79 = (bf16[320,4096]{1,0:T(8,128)(2,1)S(1)}, bf16[320,4096]{1,0:T(8,128)(2,1)}, u32[]{:S(2)}, u32[]{:S(2)}) collective-permute-start(bf16[320,4096]{1,0:T(8,128)(2,1)S(1)} %get-tuple-element.312.refs_0_), channel_id=1, source_target_pairs={{0,8},{4,12},{8,0},{12,4},{16,24},{20,28},{24,16},{28,20},{1,9},{5... | collective-permute-start | bytes 7864328 | tf_op jit(solution)/shard_map/ppermute | solution.py:421
  1235.0 79.4 %collective-permute-start.80 = (bf16[512,2048]{1,0:T(8,128)(2,1)}, bf16[512,2048]{1,0:T(8,128)(2,1)}, u32[]{:S(2)}, u32[]{:S(2)}) collective-permute-start(bf16[512,2048]{1,0:T(8,128)(2,1)} %get-tuple-element.313), channel_id=1, source_target_pairs={{0,4},{4,0},{8,12},{12,8},{16,20},{20,16},{24,28},{28,24},{1,5},{5... | collective-permute-start | bytes 6291464 | tf_op jit(solution)/shard_map/ppermute | solution.py:421
  1236.0 78.4 %collective-permute-start.81 = (bf16[1024,512]{1,0:T(8,128)(2,1)}, bf16[1024,512]{1,0:T(8,128)(2,1)}, u32[]{:S(2)}, u32[]{:S(2)}) collective-permute-start(bf16[1024,512]{1,0:T(8,128)(2,1)} %get-tuple-element.314), channel_id=1, source_target_pairs={{0,16},{4,20},{8,24},{12,28},{16,0},{20,4},{24,8},{28,12},{1,17},{... | collective-permute-start | bytes 3145736 | tf_op jit(solution)/shard_map/ppermute | solution.py:421
  1571.5 77.6 %collective-permute-start.93 = (bf16[320,4096]{1,0:T(8,128)(2,1)S(1)}, bf16[320,4096]{1,0:T(8,128)(2,1)}, u32[]{:S(2)}, u32[]{:S(2)}) collective-permute-start(bf16[320,4096]{1,0:T(8,128)(2,1)S(1)} %copy-done.55), channel_id=1, source_target_pairs={{0,2},{1,3},{2,0},{3,1},{4,6},{5,7},{6,4},{7,5},{8,10},{9,11},{10,... | collective-permute-start | bytes 7864328 | tf_op jit(solution)/shard_map/ppermute | solution.py:421
  1572.6 77.2 %collective-permute-start.94 = (bf16[320,4096]{1,0:T(8,128)(2,1)}, bf16[320,4096]{1,0:T(8,128)(2,1)}, u32[]{:S(2)}, u32[]{:S(2)}) collective-permute-start(bf16[320,4096]{1,0:T(8,128)(2,1)} %add_convert_fusion.2), channel_id=1, source_target_pairs={{0,8},{4,12},{8,0},{12,4},{16,24},{20,28},{24,16},{28,20},{1,9},{5... | collective-permute-start | bytes 7864328 | tf_op jit(solution)/shard_map/ppermute | solution.py:421
  1650.1 78.3 %collective-permute-start.98 = (bf16[320,4096]{1,0:T(8,128)(2,1)}, bf16[320,4096]{1,0:T(8,128)(2,1)S(1)}, u32[]{:S(2)}, u32[]{:S(2)}) collective-permute-start(bf16[320,4096]{1,0:T(8,128)(2,1)} %get-tuple-element.349), channel_id=1, source_target_pairs={{0,2},{1,3},{2,0},{3,1},{4,6},{5,7},{6,4},{7,5},{8,10},{9,11},{10,... | collective-permute-start | bytes 7864328 | tf_op jit(solution)/shard_map/ppermute | solution.py:421
  1728.5 95.3 %collective-permute-start.102 = (bf16[320,4096]{1,0:T(8,128)(2,1)}, bf16[320,4096]{1,0:T(8,128)(2,1)S(1)}, u32[]{:S(2)}, u32[]{:S(2)}) collective-permute-start(bf16[320,4096]{1,0:T(8,128)(2,1)} %get-tuple-element.363), channel_id=1, source_target_pairs={{0,2},{1,3},{2,0},{3,1},{4,6},{5,7},{6,4},{7,5},{8,10},{9,11},{10,... | collective-permute-start | bytes 7864328 | tf_op jit(solution)/shard_map/ppermute | solution.py:421
  1732.5 91.2 %collective-permute-start.103 = (bf16[320,4096]{1,0:T(8,128)(2,1)S(1)}, bf16[320,4096]{1,0:T(8,128)(2,1)S(1)}, u32[]{:S(2)}, u32[]{:S(2)}) collective-permute-start(bf16[320,4096]{1,0:T(8,128)(2,1)S(1)} %add_convert_fusion), channel_id=1, source_target_pairs={{0,8},{4,12},{8,0},{12,4},{16,24},{20,28},{24,16},{28,20},{1,9},{5... | collective-permute-start | bytes 7864328 | tf_op jit(solution)/shard_map/ppermute | solution.py:421
  1733.0 82.2 %collective-permute-start.115 = (bf16[512,1536]{1,0:T(8,128)(2,1)S(1)}, bf16[512,1536]{1,0:T(8,128)(2,1)S(1)}, u32[]{:S(2)}, u32[]{:S(2)}) collective-permute-start(bf16[512,1536]{1,0:T(8,128)(2,1)S(1)} %add_convert_fusion.15), channel_id=1, source_target_pairs={{0,16},{4,20},{8,24},{12,28},{16,0},{20,4},{24,8},{28,12},{1,17},{... | collective-permute-start | bytes 4718600 | tf_op jit(solution)/shard_map/ppermute | solution.py:421
  1735.4 79.8 %collective-permute-start.116 = (bf16[512,1536]{1,0:T(8,128)(2,1)S(1)}, bf16[512,1536]{1,0:T(8,128)(2,1)S(1)}, u32[]{:S(2)}, u32[]{:S(2)}) collective-permute-start(bf16[512,1536]{1,0:T(8,128)(2,1)S(1)} %copy-done.114), channel_id=1, source_target_pairs={{0,4},{4,0},{8,12},{12,8},{16,20},{20,16},{24,28},{28,24},{1,5},{5... | collective-permute-start | bytes 4718600 | tf_op jit(solution)/shard_map/ppermute | solution.py:421
  1736.3 81.1 %collective-permute-start.114 = (bf16[512,1536]{1,0:T(8,128)(2,1)S(1)}, bf16[512,1536]{1,0:T(8,128)(2,1)}, u32[]{:S(2)}, u32[]{:S(2)}) collective-permute-start(bf16[512,1536]{1,0:T(8,128)(2,1)S(1)} %copy-done.113), channel_id=1, source_target_pairs={{0,4},{4,0},{8,12},{12,8},{16,20},{20,16},{24,28},{28,24},{1,5},{5... | collective-permute-start | bytes 4718600 | tf_op jit(solution)/shard_map/ppermute | solution.py:421
  (234 other events, 8602.4 us)

commit v3 on v2

v3 whole, which is shorter than its diff:
```python
import functools
import math

import jax
import jax.numpy as jnp
from jax import lax
from jax.experimental import pallas as pl
from jax.experimental.pallas import tpu as pltpu
from jax.sharding import PartitionSpec as P

D = 4096
H = 32
HEAD = D // H
REACH = 640
NORM_EPSILON = 1e-05
SQRT_HALF = 0.7071067811865476
INV_ROOT_TWO_PI = 0.3989422804014327
BF = jnp.bfloat16
F32 = jnp.float32
COVER = 0.05
VMEM = 56 << 20


def norm_forward(values_in):
    row_mean = jnp.mean(values_in, axis=-1, keepdims=True)
    centred = values_in - row_mean
    row_variance = jnp.mean(centred * centred, axis=-1, keepdims=True)
    inverse = lax.rsqrt(row_variance + NORM_EPSILON)
    return centred * inverse, inverse


def norm_backward(grad_out, normed, inverse, gain):
    grad_gain = jnp.sum(grad_out * normed, axis=0)
    scaled = grad_out * gain
    mean_one = jnp.mean(scaled, axis=-1, keepdims=True)
    mean_two = jnp.mean(scaled * normed, axis=-1, keepdims=True)
    return inverse * (scaled - mean_one - normed * mean_two), grad_gain


def gelu_and_slope(pre_act):
    part = 0.5 * (1.0 + lax.erf(pre_act * SQRT_HALF))
    slope = part + pre_act * jnp.exp(-0.5 * pre_act * pre_act) * INV_ROOT_TWO_PI
    return pre_act * part, slope


def dot(left, right, cl, cr):
    return lax.dot_general(left, right, (((cl,), (cr,)), ((), ())), preferred_element_type=F32)


class Steps:
    def __init__(self):
        self.token = jnp.zeros((1,), F32)
        self.pending = []
        self.first = True

    def begin(self, value):
        if self.first:
            return value
        return lax.optimization_barrier((value, self.token))[0]

    def move(self, how, value):
        out = how(self.begin(value))
        self.pending.append(out)
        return out

    def run(self, how, value, *more, **named):
        out = how(self.begin(value), *more, **named)
        self.pending += jax.tree.leaves(out)
        return out

    def close(self):
        self.token = lax.optimization_barrier((self.token, *self.pending))[0]
        self.pending = []
        self.first = False


def params(grid_dims):
    return pltpu.CompilerParams(
        dimension_semantics=("arbitrary",) * grid_dims, vmem_limit_bytes=VMEM
    )


def cost(m, n, k):
    return pl.CostEstimate(
        flops=int(2 * m * n * k * COVER), transcendentals=0, bytes_accessed=2 * (m * k + k * n + m * n)
    )


def tile(size, most):
    if size <= most:
        return size
    while size % most:
        most -= 128
    return most


def stack_rows(*pieces):
    rows = math.gcd(*(v.shape[0] for v in pieces))
    cols = pieces[0].shape[1]
    sizes = [v.shape[0] // rows for v in pieces]
    firsts = [sum(sizes[:i]) for i in range(len(pieces))]

    def body(*refs):
        step = pl.program_id(0)
        for ref, first, size in zip(refs, firsts, sizes):

            @pl.when((step >= first) & (step < first + size))
            def _(ref=ref):
                refs[-1][...] = ref[...]

    def spec(first, size):
        return pl.BlockSpec((rows, cols), lambda g: (jnp.clip(g - first, 0, size - 1), 0))

    return pl.pallas_call(
        body,
        out_shape=jax.ShapeDtypeStruct((sum(sizes) * rows, cols), pieces[0].dtype),
        grid=(sum(sizes),),
        in_specs=[spec(f, s) for f, s in zip(firsts, sizes)],
        out_specs=pl.BlockSpec((rows, cols), lambda g: (g, 0)),
        compiler_params=params(1),
        name="stack_rows",
    )(*pieces)


def gram(a_sides, b_sides, blocks, side):
    width = blocks[0][1]
    m = width if side == 0 else a_sides[0][0][0].shape[1]
    n = width if side == 1 else b_sides[0][0][0].shape[1]
    tm, tn = tile(m, 1024), tile(n, 1024)
    grid_m, grid_n = m // tm, n // tn
    count = len(blocks)
    per = grid_m * grid_n

    def at(g):
        p, r = g // per, g % per
        return p, r // grid_m, r % grid_m

    def a_spec(row, rows):
        def index_map(g, index):
            p, _, i = at(g)
            return row, (index[p] * grid_m + i if side == 0 else i)

        return pl.BlockSpec((rows, tm), index_map)

    def b_spec(row, rows):
        def index_map(g, index):
            p, j, _ = at(g)
            return row, (index[p] * grid_n + j if side == 1 else j)

        return pl.BlockSpec((rows, tn), index_map)

    def out_map(q):
        def at_q(g, index):
            r = jnp.clip(g - q * per, 0, per - 1)
            return r % grid_m, r // grid_m

        return at_q

    def body(index_ref, *refs):
        refs = list(refs)

        def take(batch):
            parts = [refs.pop(0)[...] for _ in batch]
            return parts[0] if len(parts) == 1 else jnp.concatenate(parts, axis=0)

        lefts = [take(batch) for batch in a_sides]
        rights = [take(batch) for batch in b_sides]
        total = None
        for left, right in zip(lefts, rights):
            part = dot(left, right, 0, 0)
            total = part if total is None else total + part
        total = total.astype(BF)
        p = pl.program_id(0) // per
        for q in range(count):

            @pl.when(p == q)
            def _(q=q):
                refs[q][...] = total

    flat_a = [piece for batch in a_sides for piece in batch]
    flat_b = [piece for batch in b_sides for piece in batch]
    depth = sum(piece[2] for piece in flat_a)
    return pl.pallas_call(
        body,
        out_shape=[jax.ShapeDtypeStruct((m, n), BF)] * count,
        grid_spec=pltpu.PrefetchScalarGridSpec(
            num_scalar_prefetch=1,
            grid=(count * per,),
            in_specs=[a_spec(row, rows) for _, row, rows in flat_a]
            + [b_spec(row, rows) for _, row, rows in flat_b],
            out_specs=[pl.BlockSpec((tm, tn), out_map(q)) for q in range(count)],
        ),
        compiler_params=params(1),
        cost_estimate=cost(m, n * count, depth),
        name="gram",
    )(
        jnp.array([b[0] for b in blocks], jnp.int32),
        *(piece[0] for piece in flat_a),
        *(piece[0] for piece in flat_b),
    )


def deep(pieces, blocks, starts, cr, finish=None, extra=(), outs=1, tn=512, cuts=1):
    sizes = [rows for _, _, rows in pieces]
    m, k = sum(sizes), pieces[0][0].shape[1]
    n = blocks[0].shape[1 - cr]
    count, heights = len(blocks), len(pieces)
    tn = tile(n, tn)
    work = []
    for i, rows in enumerate(sizes):
        for c in range(cuts):
            height = rows // cuts
            work.append((i, c * height, sum(sizes[:i]) + c * height, height))

    def body(starts_ref, *refs):
        a_refs, rest = refs[:heights], refs[heights:]

        def part(i, first, height):
            total = None
            for p in range(count):
                size = blocks[p].shape[cr]
                at = pl.multiple_of(starts_ref[p] * 128, 128)
                term = dot(a_refs[i][first : first + height, pl.ds(at, size)], rest[p][...], 1, cr)
                total = term if total is None else total + term
            return total

        def store(first, height, total):
            at = slice(first, first + height)
            values = (total,) if finish is None else finish(total, *(v[at, :] for v in rest[count:-outs]))
            for ref, value in zip(rest[-outs:], values):
                ref[at, :] = value.astype(BF)

        before = None
        for i, first, row, height in work:
            total = part(i, first, height)
            if before is not None:
                store(*before)
            before = (row, height, total)
        store(*before)

    def a_spec(row, rows):
        return pl.BlockSpec((rows, k), lambda j, *_: (row, 0), pipeline_mode=pl.Buffered(1))

    def w_spec(w):
        size = w.shape[cr]
        if cr == 0:
            return pl.BlockSpec((size, tn), lambda j, *_: (0, j))
        return pl.BlockSpec((tn, size), lambda j, *_: (j, 0))

    out = pl.BlockSpec((m, tn), lambda j, *_: (0, j))
    result = pl.pallas_call(
        body,
        out_shape=[jax.ShapeDtypeStruct((m, n), BF)] * outs,
        grid_spec=pltpu.PrefetchScalarGridSpec(
            num_scalar_prefetch=1,
            grid=(n // tn,),
            in_specs=[a_spec(row, rows) for _, row, rows in pieces]
            + [w_spec(w) for w in blocks]
            + [out] * len(extra),
            out_specs=[out] * outs,
        ),
        compiler_params=params(1),
        cost_estimate=cost(m, n, k),
        name="deep",
    )(starts, *(piece[0] for piece in pieces), *blocks, *extra)
    return result[0] if outs == 1 else result


def broad(a, blocks, starts, cr):
    m, k = a.shape
    n = sum(w.shape[1 - cr] for w in blocks)
    count = len(blocks)
    tm = tile(m // 2, 320)
    steps = m // 2 // tm

    def body(starts_ref, a_ref, *rest):
        for which in range(2):

            @pl.when(pl.program_id(0) // steps == which)
            def _(out=rest[count + which]):
                for p in range(count):
                    size = blocks[p].shape[1 - cr]
                    at = pl.multiple_of(starts_ref[p] * 128, 128)
                    out[:, pl.ds(at, size)] = dot(a_ref[...], rest[p][...], 1, cr).astype(BF)

    return pl.pallas_call(
        body,
        out_shape=[jax.ShapeDtypeStruct((m // 2, n), BF)] * 2,
        grid_spec=pltpu.PrefetchScalarGridSpec(
            num_scalar_prefetch=1,
            grid=(2 * steps,),
            in_specs=[pl.BlockSpec((tm, k), lambda i, *_: (i, 0))]
            + [pl.BlockSpec(w.shape, lambda i, *_: (0, 0), pipeline_mode=pl.Buffered(1)) for w in blocks],
            out_specs=[
                pl.BlockSpec((tm, n), lambda i, *_: (jnp.minimum(i, steps - 1), 0)),
                pl.BlockSpec((tm, n), lambda i, *_: (jnp.maximum(i - steps, 0), 0)),
            ],
        ),
        compiler_params=params(1),
        cost_estimate=cost(m, n, k),
        name="broad",
    )(starts, a, *blocks)


QB = 256


def window(first):
    low = max(0, first - REACH)
    return low, first + QB - low


def masked_scores(q, k, start, slope, first, low, width, scale):
    scores = dot(q, k, 1, 1)
    row = first + lax.broadcasted_iota(jnp.int32, (QB, width), 0)
    col = low + lax.broadcasted_iota(jnp.int32, (QB, width), 1)
    scores = scores * scale - slope * (row - col).astype(F32)
    return jnp.where((col >= start) & (col <= row), scores, -1e30)


def in_order(turn, visit):
    for i in range(4):
        rel = lax.bitwise_xor(jnp.int32(i), turn)
        visit(i, lax.bitwise_and(rel, 1), lax.shift_right_logical(rel, 1))


def attention_forward(turn_ref, slope_ref, qkv_ref, start_ref, o_ref, lse_ref, q_s, k_s, v_s, o_s):
    turn = turn_ref[0]
    slope = slope_ref[pl.program_id(0)]
    sequence = q_s.shape[0]
    piece = sequence // 4
    scale = 1.0 / math.sqrt(HEAD)

    def load(i, core, x):
        block = qkv_ref[core, x]
        for j, scratch in enumerate((q_s, k_s, v_s)):
            scratch[i * piece : (i + 1) * piece, :] = block[:, j * HEAD : (j + 1) * HEAD]

    in_order(turn, load)
    for first in range(0, sequence, QB):
        low, width = window(first)
        scores = masked_scores(
            q_s[first : first + QB, :],
            k_s[low : low + width, :],
            start_ref[first : first + QB, :],
            slope,
            first,
            low,
            width,
            scale,
        )
        peak = jnp.max(scores, axis=-1, keepdims=True)
        weights = jnp.exp(scores - peak)
        total = jnp.sum(weights, axis=-1, keepdims=True)
        lse_ref[0, first : first + QB, :] = peak + jnp.log(total)
        probs = (weights * (1.0 / total)).astype(BF)
        o_s[first : first + QB, :] = dot(probs, v_s[low : low + width, :], 1, 0).astype(BF)

    def store(i, core, x):
        o_ref[core, x] = o_s[i * piece : (i + 1) * piece, :]

    in_order(turn, store)


def attention_backward(
    turn_ref, slope_ref, qkv_ref, do_ref, start_ref, lse_ref, out_ref, q_s, k_s, v_s, do_s, dq_s, dk_s, dv_s
):
    turn = turn_ref[0]
    slope = slope_ref[pl.program_id(0)]
    sequence = q_s.shape[0]
    piece = sequence // 4
    scale = 1.0 / math.sqrt(HEAD)

    def load(i, core, x):
        rows = slice(i * piece, (i + 1) * piece)
        block = qkv_ref[core, x]
        for j, scratch in enumerate((q_s, k_s, v_s)):
            scratch[rows, :] = block[:, j * HEAD : (j + 1) * HEAD]
        do_s[rows, :] = do_ref[core, x]

    in_order(turn, load)
    dk_s[...] = jnp.zeros_like(dk_s)
    dv_s[...] = jnp.zeros_like(dv_s)
    for first in range(0, sequence, QB):
        low, width = window(first)
        keys = k_s[low : low + width, :]
        query = q_s[first : first + QB, :]
        grad = do_s[first : first + QB, :]
        scores = masked_scores(
            query, keys, start_ref[first : first + QB, :], slope, first, low, width, scale
        )
        probs = jnp.exp(scores - lse_ref[0, first : first + QB, :])
        grad_probs = dot(grad, v_s[low : low + width, :], 1, 1)
        delta = jnp.sum(probs * grad_probs, axis=-1, keepdims=True)
        grad_scores = (probs * (grad_probs - delta) * scale).astype(BF)
        dq_s[first : first + QB, :] = dot(grad_scores, keys, 1, 0).astype(BF)
        dk_s[low : low + width, :] += dot(grad_scores, query, 0, 0)
        dv_s[low : low + width, :] += dot(probs.astype(BF), grad, 0, 0)

    def store(i, core, x):
        rows = slice(i * piece, (i + 1) * piece)
        out_ref[core, x, :, 0:HEAD] = dq_s[rows, :]
        out_ref[core, x, :, HEAD : 2 * HEAD] = dk_s[rows, :].astype(BF)
        out_ref[core, x, :, 2 * HEAD : 3 * HEAD] = dv_s[rows, :].astype(BF)

    in_order(turn, store)


def on_device(
    hidden_in,
    segment_ids,
    qkv_weight,
    out_weight,
    up_weight,
    down_weight,
    norm1_gain,
    norm2_gain,
    out_cotangent,
):
    n = lax.axis_size("fsdp")
    tp = lax.axis_size("tp")
    ring = n // 4
    f = lax.axis_index("fsdp")
    t = lax.axis_index("tp")
    y, zl, zh = f & 1, (f >> 1) & 1, f >> 2
    low_half = zl == 0
    piece = hidden_in.shape[0]
    half = piece // 2
    sequence = piece * tp
    heads = H // tp // 2
    width = heads * HEAD
    unit = D // n
    pairs = [(k, j) for k in range(ring) for j in range(2)]
    far_first = range(ring - 1, -1, -1)
    steps = Steps()
    move, run, close = steps.move, steps.run, steps.close

    def over(axis, to, size):
        return lambda v: lax.ppermute(v, axis, [(i, to(i)) for i in range(size)])

    pp_core = over("tp", lambda i: i ^ 1, tp)
    pp_x = over("tp", lambda i: i ^ 2, tp)
    pp_zl = over("fsdp", lambda i: i ^ 2, n)
    pp_y = over("fsdp", lambda i: i ^ 1, n)
    pp_up = over("fsdp", lambda i: (i + 4) % n, n)
    pp_down = over("fsdp", lambda i: (i - 4) % n, n)

    def to_rel(v):
        cols = [v[..., b * unit : (b + 1) * unit] for b in range(n)]

        def pick(k, j, l):
            chosen = None
            for a in range(ring):
                both = jnp.where(y == j, cols[a * 4 + l * 2], cols[a * 4 + l * 2 + 1])
                chosen = both if chosen is None else jnp.where((zh - k) % ring == a, both, chosen)
            return chosen

        return jnp.concatenate([pick(k, j, l) for k, j in pairs for l in range(2)], axis=-1)

    def from_rel(v):
        cols = [v[..., b * unit : (b + 1) * unit] for b in range(n)]

        def pick(a, l, b):
            chosen = None
            for k in range(ring):
                both = jnp.where(y == b, cols[k * 4 + l], cols[k * 4 + 2 + l])
                chosen = both if chosen is None else jnp.where((zh - k) % ring == a, both, chosen)
            return chosen

        return jnp.concatenate(
            [pick(a, l, b) for a in range(ring) for l in range(2) for b in range(2)], axis=-1
        )

    def mine_of(first, second):
        return jnp.where(low_half, first, second)

    def joined(mine, other, axis):
        return jnp.concatenate(
            [jnp.where(low_half, mine, other), jnp.where(low_half, other, mine)], axis=axis
        )

    def plus(*terms):
        return sum(v.astype(F32) for v in terms).astype(BF)

    def ring_up(v):
        chain = [v]
        for _ in range(ring - 1):
            chain.append(pp_up(chain[-1]))
        return chain[1:]

    def cut_rows(v, c, of=2):
        size = v.shape[0] // of
        return v[c * size : (c + 1) * size]

    class Weight:
        def __init__(self, mine, other):
            self.have = {(0, 0, 0): mine}
            self.other = other
            self.chunks = {}

        def prepare(self, mine=1, other=1):
            first = self.have[0, 0, 0]
            if mine > 1:
                for c in range(mine):
                    self.chunks["mine", c] = run(lambda v, c=c: cut_rows(v, c, mine), first)
            if other > 1:
                for c in range(other):
                    self.chunks["other", c] = run(lambda v, c=c: cut_rows(v, c, other), self.other)

        def get(self, key):
            if isinstance(self.have[key], list):
                first, *rest = self.have[key]
                self.have[key] = stack_rows(steps.begin(first), *rest) if rest else first
            return self.have[key]

        def swap(self, c=0, of=1):
            got = move(pp_zl, self.chunks["other", c] if of > 1 else self.other)
            self.chunks["swap", c] = got
            if c == of - 1:
                self.have[0, 0, 1] = [self.chunks["swap", i] for i in range(of)]

        def zh(self, source, c=0, of=1):
            if source == 1 and of > 1 and ("swap", of - 1) in self.chunks:
                v = self.chunks["swap", c]
            elif source == 0 and of > 1:
                v = self.chunks["mine", c]
            elif of > 1:
                v = cut_rows(self.get((0, 0, source)), c, of)
            else:
                v = self.get((0, 0, source))
            self.chunks[source, c] = move(ring_up, v)
            if c == of - 1:
                for k in range(ring - 1):
                    self.have[k + 1, 0, source] = [self.chunks[source, i][k] for i in range(of)]

        def y(self, source):
            self.have[0, 1, source] = move(pp_y, self.get((0, 0, source)))

        def yz(self, source):
            for k in range(1, ring):
                self.have[k, 1, source] = move(pp_y, self.get((k, 0, source)))

        def blocks(self):
            found, starts = [], []
            for k, j in pairs:
                for source in range(2):
                    found.append(self.get((k, j, source)))
                    starts.append((2 * (2 * k + j) + (zl if source == 0 else 1 - zl)) * (unit // 128))
            return found, jnp.stack(starts).astype(jnp.int32)

    def halves(v, axis):
        lower, upper = jnp.split(v, 2, axis=axis)
        return mine_of(lower, upper), mine_of(upper, lower)

    gains = jnp.stack([norm1_gain, norm2_gain])
    gain_chain = [joined(gains, pp_zl(gains), 1)]
    gain_chain = jnp.concatenate(gain_chain + ring_up(gain_chain[0]), axis=0)
    gain_other = pp_y(gain_chain)
    qkv_heads = (
        qkv_weight.reshape(unit, 3, 2 * heads, HEAD)
        .transpose(0, 2, 1, 3)
        .reshape(unit, 2 * heads * 3 * HEAD)
    )
    qkv_w = Weight(*halves(qkv_heads, 1))
    out_mine, out_other = halves(out_weight, 0)
    other_ids = move(pp_zl, segment_ids)
    steps.pending += [gain_other, gain_chain, qkv_w.have[0, 0, 0], qkv_w.other, out_other]
    close()

    gains = jnp.concatenate(
        [(gain_chain, gain_other)[j][2 * k : 2 * k + 2] for k, j in pairs], axis=1
    ).astype(F32)
    gain_one, gain_two = gains[0:1], gains[1:2]
    qkv_w.swap()
    qkv_w.y(0)
    qkv_w.zh(0)
    out_swapped = move(pp_zl, out_other)
    x = to_rel(steps.begin(hidden_in)).astype(F32)
    normed_one, inverse_one = norm_forward(x)
    a_one = (normed_one * gain_one).astype(BF)
    cot = to_rel(steps.begin(out_cotangent))
    steps.pending += [a_one, cot]
    close()

    qkv_w.zh(1)
    qkv_w.y(1)
    qkv_w.yz(0)
    az = move(pp_zl, a_one)
    ax = move(pp_x, a_one)
    out_block = run(lambda v: joined(v, out_swapped, 1), out_mine)

    def first_of(ids):
        return jnp.sum((ids < ids.reshape(sequence, 1)).astype(jnp.int32), axis=-1, keepdims=True)

    start_a, start_b = run(first_of, segment_ids), run(first_of, other_ids)
    up_w = Weight(*run(lambda v: halves(v, 1), up_weight))
    down_w = Weight(*run(lambda v: halves(v, 0), down_weight))
    up_w.prepare(mine=2, other=2)
    down_w.prepare(mine=2, other=2)
    close()

    def gather(v, *pieces):
        return run(lambda first, *rest: stack_rows(first, *rest), v, *pieces)

    one_a = gather(a_one, ax)
    qkv_w.yz(1)
    ad = move(pp_x, az)
    out_w = Weight(out_block, None)
    out_w.zh(0)
    one_a_far = move(pp_core, one_a)
    up_w.swap(0, 2)
    close()

    turn = jnp.full((1,), t, jnp.int32)
    head_index = t * 2 * heads + zl * heads + jnp.arange(heads)
    slopes = 2.0 ** (-8.0 * (head_index + 1).astype(F32) / H)
    two = 2 * piece

    def batch(near, far):
        return [(near, 0, two), (far, 0, two)]

    w_qkv, at_qkv = qkv_w.blocks()
    one_b = gather(az, ad)
    one_b_far = move(pp_core, one_b)
    up_w.zh(0, 0, 2)
    out_w.y(0)
    out_w.yz(0)
    cx_top = move(pp_x, cot[:half])
    up_w.swap(1, 2)
    one_b_rows = batch(one_b, one_b_far)
    one_a_rows = batch(one_a, one_a_far)
    qkv_a = run(lambda v: deep(batch(v, one_a_far), w_qkv, at_qkv, 0), one_a)
    qkv_b = run(lambda v: deep(batch(one_b, v), w_qkv, at_qkv, 0), one_b_far)
    close()

    def spec(cols):
        return pl.BlockSpec((2, 2, piece, cols), lambda h, *_: (0, 0, 0, h))

    start_spec = pl.BlockSpec((sequence, 1), lambda h, *_: (0, 0))
    lse_spec = pl.BlockSpec((1, sequence, 1), lambda h, *_: (h, 0, 0))
    block = pltpu.VMEM((sequence, HEAD), BF)
    wide = pltpu.VMEM((sequence, HEAD), F32)

    def attend(qkv, start):
        out, lse = pl.pallas_call(
            attention_forward,
            out_shape=(
                jax.ShapeDtypeStruct((2, 2, piece, width), BF),
                jax.ShapeDtypeStruct((heads, sequence, 1), F32),
            ),
            grid_spec=pltpu.PrefetchScalarGridSpec(
                num_scalar_prefetch=2,
                grid=(heads,),
                in_specs=[spec(3 * HEAD), start_spec],
                out_specs=[spec(HEAD), lse_spec],
                scratch_shapes=[block] * 4,
            ),
            compiler_params=params(1),
            cost_estimate=cost(sequence, sequence, 2 * heads * HEAD),
            name="attention_forward",
        )(turn, slopes, qkv.reshape(2, 2, piece, 3 * width), start)
        return out.reshape(sequence, width), lse

    def attend_back(grad, qkv, start, lse):
        out = pl.pallas_call(
            attention_backward,
            out_shape=jax.ShapeDtypeStruct((2, 2, piece, 3 * width), BF),
            grid_spec=pltpu.PrefetchScalarGridSpec(
                num_scalar_prefetch=2,
                grid=(heads,),
                in_specs=[spec(3 * HEAD), spec(HEAD), start_spec, lse_spec],
                out_specs=spec(3 * HEAD),
                scratch_shapes=[block] * 5 + [wide] * 2,
            ),
            compiler_params=params(1),
            cost_estimate=cost(sequence, sequence, 4 * heads * HEAD),
            name="attention_backward",
        )(
            turn,
            slopes,
            qkv.reshape(2, 2, piece, 3 * width),
            grad.reshape(2, 2, piece, width),
            start,
            lse,
        )
        return out.reshape(sequence, 3 * width)

    def core_sum(near, far):
        got = move(pp_core, far)
        near = steps.begin(near)
        return tuple(plus(near[i * piece : (i + 1) * piece], got[i * piece : (i + 1) * piece]) for i in range(2))

    w_out = [out_w.get((k, j, 0)) for k, j in pairs]
    at_out = jnp.arange(len(pairs), dtype=jnp.int32) * (2 * unit // 128)
    att_b, lse_b = run(attend, qkv_b, start_b)
    sums_b = run(broad, att_b, w_out, at_out, 0)
    up_w.zh(0, 1, 2)
    up_w.y(0)
    cz_top = move(pp_zl, cot[:half])
    cx_bottom = move(pp_x, cot[half:])
    close()

    ez, ed = core_sum(*sums_b)
    from_d = pp_x(ed)
    steps.pending += [ez, from_d]
    up_w.zh(1, 0, 2)
    up_w.yz(0)
    cz_bottom = move(pp_zl, cot[half:])
    att_a, lse_a = run(attend, qkv_a, start_a)
    sums_a = run(broad, att_a, w_out, at_out, 0)
    close()

    e00, ex = core_sum(*sums_a)
    from_x = pp_x(ex)
    steps.pending += [e00, from_x]
    from_z = move(pp_zl, plus(steps.begin(ez), from_d))
    up_w.zh(1, 1, 2)
    up_w.y(1)
    cz = gather(cz_top, cz_bottom)
    near_cot_a = gather(cot, cx_top, cx_bottom)
    close()

    resid = x + (steps.begin(e00).astype(F32) + from_x.astype(F32) + from_z.astype(F32))
    normed_two, inverse_two = norm_forward(resid)
    a_two = (normed_two * gain_two).astype(BF)
    far_cot_a = move(pp_core, near_cot_a)
    ax = move(pp_x, a_two)
    az = move(pp_zl, a_two)
    down_w.zh(0, 0, 2)
    up_w.yz(1)
    close()

    w_up, at_up = up_w.blocks()

    def lift(near, far):
        return deep(batch(near, far), w_up, at_up, 0, finish=gelu_and_slope, outs=2, cuts=2)

    two_a = gather(a_two, ax)
    ad = move(pp_x, az)
    two_a_far = move(pp_core, two_a)
    down_w.zh(0, 1, 2)
    down_w.y(0)
    down_w.swap(0, 2)
    act_a, slope_a = run(lambda v: lift(two_a, v), two_a_far)
    close()

    two_b = gather(az, ad)
    two_b_far = move(pp_core, two_b)
    down_w.yz(0)
    down_w.swap(1, 2)
    down_w.zh(1, 0, 2)
    cd = move(pp_x, cz)
    act_b, slope_b = run(lambda v: lift(two_b, v), two_b_far)
    close()

    class Sum:
        def __init__(self, axis, whole=False):
            self.whole = whole
            self.parts = {}
            self.got = {}
            self.sums = {}
            self.value = {}
            self.axis = axis

        def make(self, j, a_sides, b_sides):
            def go(first):
                (head, *others), *sides = a_sides
                head = (first, *head[1:])
                return gram([[head, *others], *sides], b_sides, blocks, self.axis)

            if self.whole:
                keys = [(k, j, 0) for k in far_first]
                blocks = [(2 * k + j, 2 * unit) for k, j, _ in keys]
            else:
                keys = [(k, j, l) for k in far_first for l in range(2)]
                blocks = [((2 * k + j) * 2 + l, unit) for k, j, l in keys]
            for key, v in zip(keys, run(go, a_sides[0][0][0])):
                self.parts[key] = v

        def y_far(self, l):
            for k in range(ring - 1, 0, -1):
                self.sums[k, l] = move(pp_y, self.parts[k, 1, l])

        def y_own(self, l):
            self.got[l] = move(pp_y, self.parts[0, 1, l])

        def cut(self, v, r, of):
            size = v.shape[1 - self.axis] // of
            return lax.slice_in_dim(v, r * size, (r + 1) * size, axis=1 - self.axis)

        def part(self, k, l, r, of):
            mine = steps.begin(self.parts[k, 0, l])
            return self.cut(mine, r, of), self.cut(self.sums[k, l], r, of)

        def zh(self, l, r=0, of=2):
            value = plus(*self.part(ring - 1, l, r, of))
            for k in range(ring - 2, 0, -1):
                value = plus(move(pp_down, value), *self.part(k, l, r, of))
            self.value[l, r] = move(pp_down, value)

        def ready(self, r=0, of=2):
            def go(value):
                if self.whole:
                    total = plus(value, self.parts[0, 0, 0], self.got[0])
                    first, second = jnp.split(total, 2, axis=self.axis)
                else:
                    first, second = (
                        plus(v, self.cut(self.parts[0, 0, l], r, of), self.cut(self.got[l], r, of))
                        for l, v in enumerate((value, self.value[1, r]))
                    )
                return mine_of(first, second), mine_of(second, first)

            self.value[2, r], self.value[3, r] = run(go, self.value[0, r])

        def zl(self, r=0):
            self.value[3, r] = move(pp_zl, self.value[3, r])

        def result(self, of=2):
            mine = [self.value[2, r] for r in range(of)]
            other = [self.value[3, r] for r in range(of)]
            if of == 1:
                return mine[0], other[0]
            return tuple(jnp.concatenate(v, axis=1 - self.axis) for v in (mine, other))

    def finished(make):
        out = make()
        steps.pending.append(out)
        return out

    down_g, up_g, out_g, qkv_g = Sum(1), Sum(0), Sum(1, True), Sum(0)
    near_cot_b = gather(cz, cd)
    far_cot_b = move(pp_core, near_cot_b)
    down_w.zh(1, 1, 2)
    down_w.y(1)
    cot_a, cot_b = batch(near_cot_a, far_cot_a), batch(near_cot_b, far_cot_b)
    acts = [[(act_a, 0, 2 * two)], [(act_b, 0, 2 * two)]]
    down_g.make(1, acts, [cot_a, cot_b])
    close()
    down_w.yz(1)
    down_g.make(0, acts, [cot_a, cot_b])
    close()

    w_down, at_down = down_w.blocks()

    def pull(rows, slope):
        return deep(
            rows,
            w_down,
            at_down,
            1,
            finish=lambda total, s: (total * s.astype(F32),),
            extra=(slope,),
            cuts=1,
        )

    down_g.y_far(0)
    du_b = run(lambda v: pull(cot_b, v), slope_b)
    sums_b = run(broad, du_b, w_up, at_up, 1)
    close()

    ez, ed = core_sum(*sums_b)
    from_d = pp_x(ed)
    steps.pending += [ez, from_d]
    down_g.zh(0, 0)
    down_g.zh(0, 1)
    down_g.y_far(1)
    down_g.y_own(0)
    du_a = run(lambda v: pull(cot_a, v), slope_a)
    sums_a = run(broad, du_a, w_up, at_up, 1)
    close()

    e00, ex = core_sum(*sums_a)
    from_x = pp_x(ex)
    steps.pending += [e00, from_x]
    from_z = move(pp_zl, plus(steps.begin(ez), from_d))
    down_g.zh(1, 0)
    down_g.y_own(1)
    two_rows = [batch(two_a, two_a_far), batch(two_b, two_b_far)]
    dus = [[(du_a, 0, 2 * two)], [(du_b, 0, 2 * two)]]
    up_g.make(1, two_rows, dus)
    up_g.make(0, two_rows, dus)
    close()

    grad_in_two = steps.begin(e00).astype(F32) + from_x.astype(F32) + from_z.astype(F32)
    grad_part, grad_gain_two = norm_backward(grad_in_two, normed_two, inverse_two, gain_two)
    grad_resid = cot.astype(F32) + grad_part
    grad_rows = grad_resid.astype(BF)
    ax = move(pp_x, grad_rows)
    az = move(pp_zl, grad_rows)
    down_g.zh(1, 1)
    up_g.y_far(0)
    out_b = run(broad, act_b, w_down, at_down, 0)
    out_a = run(broad, act_a, w_down, at_down, 0)
    close()

    grad_a = gather(grad_rows, ax)
    grad_a_far = move(pp_core, grad_a)
    ad = move(pp_x, az)
    up_g.zh(0, 0)
    up_g.y_far(1)
    o_b = core_sum(*out_b)
    steps.pending += o_b
    dov_a = run(lambda v: deep(batch(grad_a, v), w_out, at_out, 1), grad_a_far)
    proj_a = attend_back(dov_a, qkv_a, start_a, lse_a)
    steps.pending.append(proj_a)
    close()

    grad_b = gather(az, ad)
    grad_b_far = move(pp_core, grad_b)
    up_g.zh(1, 0)
    up_g.y_own(0)
    oz, od = o_b
    from_od = move(pp_x, od)
    o_a = core_sum(*out_a)
    steps.pending += o_a
    down_g.ready(0)
    down_g.ready(1)
    dov_b = run(lambda v: deep(batch(grad_b, v), w_out, at_out, 1), grad_b_far)
    proj_b = attend_back(dov_b, qkv_b, start_b, lse_b)
    steps.pending.append(proj_b)
    close()

    one_rows = [one_a_rows, one_b_rows]
    projs = [[(proj_a, 0, 2 * two)], [(proj_b, 0, 2 * two)]]
    o00, ox = o_a
    from_ox = move(pp_x, ox)
    from_oz = move(pp_zl, plus(steps.begin(oz), from_od))
    up_g.zh(0, 1)
    up_g.y_own(1)
    qkv_g.make(1, one_rows, projs)
    qkv_g.make(0, one_rows, projs)
    atts = [[(att_a, 0, 2 * two)], [(att_b, 0, 2 * two)]]
    grads = [batch(grad_a, grad_a_far), batch(grad_b, grad_b_far)]
    out_g.make(1, atts, grads)
    close()

    down_g.zl(0)
    down_g.zl(1)
    qkv_g.y_far(0)
    up_g.zh(1, 1)
    sums_b = run(broad, proj_b, w_qkv, at_qkv, 1)
    out_g.y_far(0)
    up_g.ready(0)
    out_g.make(0, atts, grads)
    block_out = run(
        lambda v: from_rel(
            (resid + (v.astype(F32) + from_ox.astype(F32) + from_oz.astype(F32))).astype(BF)
        ),
        o00,
    )
    close()

    ez, ed = core_sum(*sums_b)
    from_d = pp_x(ed)
    steps.pending += [ez, from_d]
    qkv_g.zh(0, 0, 1)
    qkv_g.y_far(1)
    up_g.zl(0)
    up_g.ready(1)
    up_g.zl(1)
    sums_a = run(broad, proj_a, w_qkv, at_qkv, 1)
    grad_down = finished(lambda: joined(steps.begin(down_g.result()[0]), down_g.result()[1], 0).astype(F32))
    close()

    e00, ex = core_sum(*sums_a)
    from_x = pp_x(ex)
    steps.pending += [e00, from_x]
    from_z = move(pp_zl, plus(steps.begin(ez), from_d))
    qkv_g.zh(1, 0, 1)
    qkv_g.y_own(0)
    qkv_g.y_own(1)
    close()

    out_g.y_own(0)
    out_g.zh(0, 0, 1)
    qkv_g.ready(0, 1)
    grad_up = finished(lambda: joined(steps.begin(up_g.result()[0]), up_g.result()[1], 1).astype(F32))
    qkv_g.value[3, 0] = pp_zl(qkv_g.value[3, 0])
    steps.pending.append(qkv_g.value[3, 0])
    grad_in_one = steps.begin(e00).astype(F32) + from_x.astype(F32) + from_z.astype(F32)
    grad_part, grad_gain_one = norm_backward(grad_in_one, normed_one, inverse_one, gain_one)
    grad_in = from_rel(grad_resid + grad_part)
    gain_grads = from_rel(jnp.stack([grad_gain_one, grad_gain_two]))
    for step in (pp_core, pp_x, pp_y):
        gain_grads = gain_grads + step(gain_grads)
    steps.pending += [grad_in, gain_grads]
    close()

    def parts_first(v):
        return v.reshape(unit, heads, 3, HEAD).transpose(0, 2, 1, 3).reshape(unit, 3, width)

    out_g.ready(0, 1)
    out_g.value[3, 0] = pp_zl(out_g.value[3, 0])
    mine, other = qkv_g.result(1)
    grad_qkv = finished(
        lambda: joined(parts_first(steps.begin(mine)), parts_first(other), 2).astype(F32)
    )
    gain_grads = steps.begin(gain_grads)
    gain_grads = gain_grads + pp_zl(gain_grads)
    moving = gain_grads
    for _ in range(ring - 1):
        moving = pp_up(moving)
        gain_grads = gain_grads + moving
    size = D // (n * tp)
    gain_grads = lax.dynamic_slice_in_dim(gain_grads, (f * tp + t) * size, size, axis=1)

    grad_out = joined(*out_g.result(1), 0).astype(F32)

    return (
        block_out,
        grad_in,
        gain_grads[0],
        gain_grads[1],
        grad_qkv,
        grad_out,
        grad_up,
        grad_down,
    )


def solution(mesh):
    return jax.shard_map(
        on_device,
        mesh=mesh,
        in_specs=(
            P(("fsdp", "tp"), None),
            P("fsdp", None),
            P("fsdp", None, "tp"),
            P("tp", "fsdp"),
            P("fsdp", "tp"),
            P("tp", "fsdp"),
            P("fsdp"),
            P("fsdp"),
            P(("fsdp", "tp"), None),
        ),
        out_specs=(
            P(("fsdp", "tp"), None),
            P(("fsdp", "tp"), None),
            P(("fsdp", "tp")),
            P(("fsdp", "tp")),
            P("fsdp", None, "tp"),
            P("tp", "fsdp"),
            P("fsdp", "tp"),
            P("tp", "fsdp"),
        ),
        check_vma=False,
    )
```

time: 1950 us -> 1830 us (0.938)
  waiting for transfers between devices: 863 us -> 701 us
  other arithmetic: 144 us -> 188 us
  Pallas kernels: 718 us -> 748 us
  local copies, waits for them, and re-layouts: 80.4 us -> 55.4 us
    ppermute x126 -> x113, waiting for transfers between devices: 863 us -> 701 us  [over(): return lambda v: lax.ppermute(v, axis, [(i, to(i)) for i in range(size)])]
    convert_element_type x20 -> x27, other arithmetic: 49.1 us -> 98.1 us  [the longest x23 81.3 us: plus(): return sum((v.astype(F32) for v in terms)).astype(BF)]
    pallas_call x4 -> x15, Pallas kernels: 35.1 us -> 62.4 us  [stack_rows(): pl.pallas_call(body, out_shape=jax.ShapeDtypeStruct((sum(sizes) * rows, c...]
    ppermute x126 -> x113, starting transfers between devices: 139 us -> 122 us  [over(): return lambda v: lax.ppermute(v, axis, [(i, to(i)) for i in range(size)])]
    unnamed x272 -> x144, local copies, waits for them, and re-layouts: 41.2 us -> 29.9 us
    pallas_call x10 -> x12, Pallas kernels: 271 us -> 275 us  [the longest x8 203 us: broad(): pl.pallas_call(body, out_shape=[jax.ShapeDtypeStruct((m // 2, n), BF)] *...]
  transfers between devices with their start and end apart: 126 -> 113, of which waited for: 51 -> 53; matrix products, arithmetic and copies ran while one was open for 9% -> 10% of each run, Pallas kernels for 34% -> 39%
where the time goes in v3:
time: 1830 us; the launch traced here: 1820 us
  Pallas kernels  748 us (41%)
  waiting for transfers between devices  701 us (38%)
  other arithmetic  188 us (10%)
  starting transfers between devices  122 us (7%)
  local copies, waits for them, and re-layouts  55.4 us (3%)
    ppermute x113, waiting for transfers between devices, over(): return lambda v: lax.ppermute(v, axis, [(i, to(i)) for i in range(size)])  701 us
    pallas_call x8, Pallas kernels, gram(): pl.pallas_call(body, out_shape=[jax.ShapeDtypeStruct((m, n), BF)] * count...  208 us
    pallas_call x8, Pallas kernels, broad(): pl.pallas_call(body, out_shape=[jax.ShapeDtypeStruct((m // 2, n), BF)] *...  203 us
    pallas_call x8, Pallas kernels, deep(): pl.pallas_call(body, out_shape=[jax.ShapeDtypeStruct((m, n), BF)] * outs,...  203 us
    ppermute x113, starting transfers between devices, over(): return lambda v: lax.ppermute(v, axis, [(i, to(i)) for i in range(size)])  122 us
    convert_element_type x23, other arithmetic, plus(): return sum((v.astype(F32) for v in terms)).astype(BF)  81.3 us
    pallas_call x15, Pallas kernels, stack_rows(): pl.pallas_call(body, out_shape=jax.ShapeDtypeStruct((sum(sizes) * rows, c...  62.4 us
    pallas_call x2, Pallas kernels, attend_back(): pl.pallas_call(attention_backward, out_shape=jax.ShapeDtypeStruct((2, 2,...  41.3 us
  transfers between devices with their start and end apart: 113, of which 53 were waited for; matrix products, arithmetic and copies ran while one was open for 10% of the time, Pallas kernels for 39%

profile of v3, /device:TPU:0, one launch (start us, length us, event | category | flops | bytes accessed | tf_op | source)
XLA Modules:
  0.0 1816.8 jit_solution(2216904857947095644)
XLA Ops:
  41.4 28.8 %collective-permute-done.7 = bf16[512,512]{1,0:T(8,128)(2,1)S(1)} collective-permute-done((bf16[512,512]{1,0:T(8,128)(2,1)}, bf16[512,512]{1,0:T(8,128)(2,1)S(1)}, u32[]{:S(2)}, u32[]{:S(2)}) %collective-permute-start.7) | collective-permute-done | bytes 524320 | tf_op jit(solution)/shard_map/ppermute | solution.py:439
  71.0 31.3 %collective-permute-done.4.refs_3_.rest_1_ = bf16[512,1536]{1,0:T(8,128)(2,1)} collective-permute-done((bf16[512,1536]{1,0:T(8,128)(2,1)}, bf16[512,1536]{1,0:T(8,128)(2,1)}, u32[]{:S(2)}, u32[]{:S(2)}) %collective-permute-start.4) | collective-permute-done | bytes 1572896 | tf_op jit(solution)/shard_map/ppermute | solution.py:439
  140.0 30.0 %collective-permute-done.8.refs_7_.rest_5_ = bf16[512,1536]{1,0:T(8,128)(2,1)} collective-permute-done((bf16[512,1536]{1,0:T(8,128)(2,1)}, bf16[512,1536]{1,0:T(8,128)(2,1)}, u32[]{:S(2)}, u32[]{:S(2)}) %collective-permute-start.8) | collective-permute-done | bytes 1572896 | tf_op jit(solution)/shard_map/ppermute | solution.py:439
  203.8 45.1 %collective-permute-done.15.rest_2_.refs_4_ = bf16[512,1024]{1,0:T(8,128)(2,1)} collective-permute-done((bf16[512,1024]{1,0:T(8,128)(2,1)}, bf16[512,1024]{1,0:T(8,128)(2,1)}, u32[]{:S(2)}, u32[]{:S(2)}) %collective-permute-start.15) | collective-permute-done | bytes 1048608 | tf_op jit(solution)/shard_map/ppermute | solution.py:439
  478.9 58.5 %collective-permute-done.36.refs_1_ = bf16[256,2048]{1,0:T(8,128)(2,1)} collective-permute-done((bf16[256,2048]{1,0:T(8,128)(2,1)}, bf16[256,2048]{1,0:T(8,128)(2,1)}, u32[]{:S(2)}, u32[]{:S(2)}) %collective-permute-start.36) | collective-permute-done | bytes 1048608 | tf_op jit(solution)/shard_map/ppermute | solution.py:439
  555.4 73.8 %collective-permute-done.41.refs_0_ = bf16[1024,512]{1,0:T(8,128)(2,1)} collective-permute-done((bf16[1024,512]{1,0:T(8,128)(2,1)}, bf16[1024,512]{1,0:T(8,128)(2,1)}, u32[]{:S(2)}, u32[]{:S(2)}) %collective-permute-start.41) | collective-permute-done | bytes 1048608 | tf_op jit(solution)/shard_map/ppermute | solution.py:439
  643.9 33.7 %deep.10 = (bf16[1280,2048]{1,0:T(8,128)(2,1)}, bf16[1280,2048]{1,0:T(8,128)(2,1)}) custom-call(s32[8]{0:T(128)} %stack.74.starts_ref, bf16[640,4096]{1,0:T(8,128)(2,1)} %stack_rows.22.refs_0_, bf16[640,4096]{1,0:T(8,128)(2,1)} %collective-permute-done.43.refs_1_, bf16[512,2048]{1,0:T(8,128)(2,1)} %get-tuple-element.305.refs_2_.rest_0_, ...), custom_call_target="tpu_custom_call" | custom-call | flops 1073741824 | bytes 32505856 | tf_op jit(solution)/shard_map/deep/pallas_call | solution.py:251
  708.5 33.9 %deep.11 = (bf16[1280,2048]{1,0:T(8,128)(2,1)}, bf16[1280,2048]{1,0:T(8,128)(2,1)}) custom-call(s32[8]{0:T(128)} %stack.74.starts_ref, bf16[640,4096]{1,0:T(8,128)(2,1)} %stack_rows.23.refs_0_.refs_2_, bf16[640,4096]{1,0:T(8,128)(2,1)} %collective-permute-done.48.refs_1_.refs_3_, bf16[512,2048]{1,0:T(8,128)(2,1)} %get-tuple-element.305.refs_2_.rest_0_, ...), custom_call_target="tpu_custom_call" | custom-call | flops 1073741824 | bytes 32505856 | tf_op jit(solution)/shard_map/deep/pallas_call | solution.py:251
  773.2 32.2 %gram.8 = (bf16[2048,512]{1,0:T(8,128)(2,1)}, bf16[2048,512]{1,0:T(8,128)(2,1)}, bf16[2048,512]{1,0:T(8,128)(2,1)}, bf16[2048,512]{1,0:T(8,128)(2,1)}) custom-call(s32[4]{0:T(128)} %constant.155.clone.index_ref, bf16[1280,2048]{1,0:T(8,128)(2,1)} %get-tuple-element.414.refs_0_.a_ref, bf16[1280,2048]{1,0:T(8,128)(2,1)} %get-tuple-element.421.refs_1_.a_ref, ...), custom_call_target="tpu_custom_call" | custom-call | flops 1073741824 | bytes 29360128 | tf_op jit(solution)/shard_map/gram/pallas_call | solution.py:183
  821.8 32.3 %gram.9 = (bf16[2048,512]{1,0:T(8,128)(2,1)}, bf16[2048,512]{1,0:T(8,128)(2,1)}, bf16[2048,512]{1,0:T(8,128)(2,1)}, bf16[2048,512]{1,0:T(8,128)(2,1)}) custom-call(s32[4]{0:T(128)} %constant.156.clone.index_ref, bf16[1280,2048]{1,0:T(8,128)(2,1)} %get-tuple-element.414.refs_0_.a_ref, bf16[1280,2048]{1,0:T(8,128)(2,1)} %get-tuple-element.421.refs_1_.a_ref, ...), custom_call_target="tpu_custom_call" | custom-call | flops 1073741824 | bytes 29360128 | tf_op jit(solution)/shard_map/gram/pallas_call | solution.py:183
  869.1 30.6 %deep.12.a_ref.refs_5_ = bf16[1280,2048]{1,0:T(8,128)(2,1)} custom-call(s32[8]{0:T(128)} %stack.74.starts_ref, bf16[640,4096]{1,0:T(8,128)(2,1)} %stack_rows.25.refs_4_.refs_0_, bf16[640,4096]{1,0:T(8,128)(2,1)} %collective-permute-done.53.refs_5_.refs_1_, bf16[2048,512]{1,0:T(8,128)(2,1)} %copy-done.3, bf16[2048,512]{1,0:T(8,128)(2,1)} %stack_rows.26.refs_3_.rest_1_, ...), custom_call_target="tpu_custom_call" | custom-call | flops 1073741824 | bytes 32505856 | tf_op jit(solution)/shard_map/deep/pallas_call | solution.py:251
  899.7 32.3 %broad.10 = (bf16[640,4096]{1,0:T(8,128)(2,1)}, bf16[640,4096]{1,0:T(8,128)(2,1)}) custom-call(s32[8]{0:T(128)} %stack.74.starts_ref, bf16[1280,2048]{1,0:T(8,128)(2,1)} %deep.12.a_ref.refs_5_, bf16[512,2048]{1,0:T(8,128)(2,1)} %get-tuple-element.305.refs_2_.rest_0_, bf16[512,2048]{1,0:T(8,128)(2,1)} %stack_rows.18.refs_3_.rest_1_, ...), custom_call_target="tpu_custom_call" | custom-call | flops 1073741824 | bytes 32505856 | tf_op jit(solution)/shard_map/broad/pallas_call | solution.py:286
  953.6 30.8 %deep.13.a_ref.refs_4_ = bf16[1280,2048]{1,0:T(8,128)(2,1)} custom-call(s32[8]{0:T(128)} %stack.74.starts_ref, bf16[640,4096]{1,0:T(8,128)(2,1)} %stack_rows.20.refs_2_.refs_0_, bf16[640,4096]{1,0:T(8,128)(2,1)} %collective-permute-done.38.refs_3_.refs_1_, bf16[2048,512]{1,0:T(8,128)(2,1)} %copy-done.3, bf16[2048,512]{1,0:T(8,128)(2,1)} %stack_rows.26.refs_3_.rest_1_, ...), custom_call_target="tpu_custom_call" | custom-call | flops 1073741824 | bytes 32505856 | tf_op jit(solution)/shard_map/deep/pallas_call | solution.py:251
  984.4 31.9 %broad.11 = (bf16[640,4096]{1,0:T(8,128)(2,1)}, bf16[640,4096]{1,0:T(8,128)(2,1)}) custom-call(s32[8]{0:T(128)} %stack.74.starts_ref, bf16[1280,2048]{1,0:T(8,128)(2,1)} %deep.13.a_ref.refs_4_, bf16[512,2048]{1,0:T(8,128)(2,1)} %get-tuple-element.305.refs_2_.rest_0_, bf16[512,2048]{1,0:T(8,128)(2,1)} %stack_rows.18.refs_3_.rest_1_, ...), custom_call_target="tpu_custom_call" | custom-call | flops 1073741824 | bytes 32505856 | tf_op jit(solution)/shard_map/broad/pallas_call | solution.py:286
  1061.3 32.9 %gram.11 = (bf16[512,2048]{1,0:T(8,128)(2,1)}, bf16[512,2048]{1,0:T(8,128)(2,1)}, bf16[512,2048]{1,0:T(8,128)(2,1)}, bf16[512,2048]{1,0:T(8,128)(2,1)}) custom-call(s32[4]{0:T(128)} %constant.156.clone.index_ref, bf16[640,4096]{1,0:T(8,128)(2,1)} %stack_rows.22.refs_0_, bf16[640,4096]{1,0:T(8,128)(2,1)} %collective-permute-done.43.refs_1_, ...), custom_call_target="tpu_custom_call" | custom-call | flops 1073741824 | bytes 52953088 | tf_op jit(solution)/shard_map/gram/pallas_call | solution.py:183
  1094.1 32.5 %gram.10 = (bf16[512,2048]{1,0:T(8,128)(2,1)}, bf16[512,2048]{1,0:T(8,128)(2,1)}, bf16[512,2048]{1,0:T(8,128)(2,1)}, bf16[512,2048]{1,0:T(8,128)(2,1)}) custom-call(s32[4]{0:T(128)} %constant.155.clone.index_ref, bf16[640,4096]{1,0:T(8,128)(2,1)} %stack_rows.22.refs_0_, bf16[640,4096]{1,0:T(8,128)(2,1)} %collective-permute-done.43.refs_1_, ...), custom_call_target="tpu_custom_call" | custom-call | flops 1073741824 | bytes 52953088 | tf_op jit(solution)/shard_map/gram/pallas_call | solution.py:183
  1148.6 31.7 %broad.12 = (bf16[640,4096]{1,0:T(8,128)(2,1)}, bf16[640,4096]{1,0:T(8,128)(2,1)}) custom-call(s32[8]{0:T(128)} %stack.74.starts_ref, bf16[1280,2048]{1,0:T(8,128)(2,1)} %get-tuple-element.414.refs_0_.a_ref, bf16[2048,512]{1,0:T(8,128)(2,1)} %copy-done.3, bf16[2048,512]{1,0:T(8,128)(2,1)} %stack_rows.26.refs_3_.rest_1_, ...), custom_call_target="tpu_custom_call" | custom-call | flops 1073741824 | bytes 32505856 | tf_op jit(solution)/shard_map/broad/pallas_call | solution.py:286
  1180.3 32.0 %broad.13 = (bf16[640,4096]{1,0:T(8,128)(2,1)}, bf16[640,4096]{1,0:T(8,128)(2,1)}) custom-call(s32[8]{0:T(128)} %stack.74.starts_ref, bf16[1280,2048]{1,0:T(8,128)(2,1)} %get-tuple-element.421.refs_1_.a_ref, bf16[2048,512]{1,0:T(8,128)(2,1)} %copy-done.3, bf16[2048,512]{1,0:T(8,128)(2,1)} %stack_rows.26.refs_3_.rest_1_, ...), custom_call_target="tpu_custom_call" | custom-call | flops 1073741824 | bytes 32505856 | tf_op jit(solution)/shard_map/broad/pallas_call | solution.py:286
  1377.5 27.4 %gram.13 = (bf16[512,1536]{1,0:T(8,128)(2,1)}, bf16[512,1536]{1,0:T(8,128)(2,1)}, bf16[512,1536]{1,0:T(8,128)(2,1)}, bf16[512,1536]{1,0:T(8,128)(2,1)}) custom-call(s32[4]{0:T(128)} %constant.156.clone.index_ref, bf16[640,4096]{1,0:T(8,128)(2,1)} %stack_rows.15.refs_0_, bf16[640,4096]{1,0:T(8,128)(2,1)} %collective-permute-done.16.refs_1_, ...), custom_call_target="tpu_custom_call" | custom-call | flops 805306368 | bytes 40370176 | tf_op jit(solution)/shard_map/gram/pallas_call | solution.py:183
  1404.9 27.2 %gram.12 = (bf16[512,1536]{1,0:T(8,128)(2,1)}, bf16[512,1536]{1,0:T(8,128)(2,1)}, bf16[512,1536]{1,0:T(8,128)(2,1)}, bf16[512,1536]{1,0:T(8,128)(2,1)}) custom-call(s32[4]{0:T(128)} %constant.155.clone.index_ref, bf16[640,4096]{1,0:T(8,128)(2,1)} %stack_rows.15.refs_0_, bf16[640,4096]{1,0:T(8,128)(2,1)} %collective-permute-done.16.refs_1_, ...), custom_call_target="tpu_custom_call" | custom-call | flops 805306368 | bytes 40370176 | tf_op jit(solution)/shard_map/gram/pallas_call | solution.py:183
  1469.3 25.6 %broad.14 = (bf16[640,4096]{1,0:T(8,128)(2,1)}, bf16[640,4096]{1,0:T(8,128)(2,1)}) custom-call(s32[8]{0:T(128)} %stack.74.starts_ref, bf16[1280,1536]{1,0:T(8,128)(2,1)} %bitcast.46, bf16[512,1536]{1,0:T(8,128)(2,1)} %get-tuple-element.264.refs_2_.rest_0_, bf16[512,1536]{1,0:T(8,128)(2,1)} %collective-permute-done.4.refs_3_.rest_1_, ...), custom_call_target="tpu_custom_call" | custom-call | flops 805306368 | bytes 27000832 | tf_op jit(solution)/shard_map/broad/pallas_call | solution.py:286
  1542.1 25.6 %broad.15 = (bf16[640,4096]{1,0:T(8,128)(2,1)}, bf16[640,4096]{1,0:T(8,128)(2,1)}) custom-call(s32[8]{0:T(128)} %stack.74.starts_ref, bf16[1280,1536]{1,0:T(8,128)(2,1)} %bitcast.43, bf16[512,1536]{1,0:T(8,128)(2,1)} %get-tuple-element.264.refs_2_.rest_0_, bf16[512,1536]{1,0:T(8,128)(2,1)} %collective-permute-done.4.refs_3_.rest_1_, ...), custom_call_target="tpu_custom_call" | custom-call | flops 805306368 | bytes 27000832 | tf_op jit(solution)/shard_map/broad/pallas_call | solution.py:286
  1591.8 28.0 %collective-permute-done.97 = bf16[512,1024]{1,0:T(8,128)(2,1)} collective-permute-done((bf16[512,1024]{1,0:T(8,128)(2,1)}, bf16[512,1024]{1,0:T(8,128)(2,1)}, u32[]{:S(2)}, u32[]{:S(2)}) %collective-permute-start.97) | collective-permute-done | bytes 1048608 | tf_op jit(solution)/shard_map/ppermute | solution.py:439
  1642.7 72.5 %collective-permute-done.101 = bf16[512,1536]{1,0:T(8,128)(2,1)} collective-permute-done((bf16[512,1536]{1,0:T(8,128)(2,1)}, bf16[512,1536]{1,0:T(8,128)(2,1)}, u32[]{:S(2)}, u32[]{:S(2)}) %collective-permute-start.101) | collective-permute-done | bytes 1572896 | tf_op jit(solution)/shard_map/ppermute | solution.py:439
  (535 shorter events, 954.3 us)
Async XLA Ops:
  21.1 81.2 %collective-permute-start.6 = (bf16[512,1536]{1,0:T(8,128)(2,1)}, bf16[512,1536]{1,0:T(8,128)(2,1)}, u32[]{:S(2)}, u32[]{:S(2)}) collective-permute-start(bf16[512,1536]{1,0:T(8,128)(2,1)} %get-tuple-element.264.refs_2_.rest_0_), channel_id=1, source_target_pairs={{0,16},{4,20},{8,24},{12,28},{16,0},{20,4},{24,8},{28,12},{1,17},{... | collective-permute-start | bytes 4718600 | tf_op jit(solution)/shard_map/ppermute | solution.py:439
  23.8 78.5 %collective-permute-start.5 = (bf16[512,1536]{1,0:T(8,128)(2,1)}, bf16[512,1536]{1,0:T(8,128)(2,1)}, u32[]{:S(2)}, u32[]{:S(2)}) collective-permute-start(bf16[512,1536]{1,0:T(8,128)(2,1)} %get-tuple-element.264.refs_2_.rest_0_), channel_id=1, source_target_pairs={{0,4},{4,0},{8,12},{12,8},{16,20},{20,16},{24,28},{28,24},{1,5},{5... | collective-permute-start | bytes 4718600 | tf_op jit(solution)/shard_map/ppermute | solution.py:439
  106.1 87.8 %collective-permute-start.11 = (bf16[320,4096]{1,0:T(8,128)(2,1)}, bf16[320,4096]{1,0:T(8,128)(2,1)}, u32[]{:S(2)}, u32[]{:S(2)}) collective-permute-start(bf16[320,4096]{1,0:T(8,128)(2,1)} %fusion.6.refs_0_), channel_id=1, source_target_pairs={{0,8},{4,12},{8,0},{12,4},{16,24},{20,28},{24,16},{28,20},{1,9},{5... | collective-permute-start | bytes 7864328 | tf_op jit(solution)/shard_map/ppermute | solution.py:439
  454.4 83.6 %collective-permute-start.35 = (bf16[320,4096]{1,0:T(8,128)(2,1)}, bf16[320,4096]{1,0:T(8,128)(2,1)S(1)}, u32[]{:S(2)}, u32[]{:S(2)}) collective-permute-start(bf16[320,4096]{1,0:T(8,128)(2,1)} %add_convert_fusion.16), channel_id=1, source_target_pairs={{0,8},{4,12},{8,0},{12,4},{16,24},{20,28},{24,16},{28,20},{1,9},{5... | collective-permute-start | bytes 7864328 | tf_op jit(solution)/shard_map/ppermute | solution.py:439
  539.7 90.2 %collective-permute-start.38 = (bf16[640,4096]{1,0:T(8,128)(2,1)}, bf16[640,4096]{1,0:T(8,128)(2,1)}, u32[]{:S(2)}, u32[]{:S(2)}) collective-permute-start(bf16[640,4096]{1,0:T(8,128)(2,1)} %stack_rows.20.refs_2_.refs_0_), channel_id=1, source_target_pairs={{0,1},{1,0},{2,3},{3,2},{4,5},{5,4},{6,7},{7,6},{8,9},{9,8},{10,11... | collective-permute-start | bytes 15728648 | tf_op jit(solution)/shard_map/ppermute | solution.py:439
  547.7 82.2 %collective-permute-start.40 = (bf16[320,4096]{1,0:T(8,128)(2,1)}, bf16[320,4096]{1,0:T(8,128)(2,1)}, u32[]{:S(2)}, u32[]{:S(2)}) collective-permute-start(bf16[320,4096]{1,0:T(8,128)(2,1)} %multiply_convert_fusion.refs_0_), channel_id=1, source_target_pairs={{0,8},{4,12},{8,0},{12,4},{16,24},{20,28},{24,16},{28,20},{1,9},{5... | collective-permute-start | bytes 7864328 | tf_op jit(solution)/shard_map/ppermute | solution.py:439
  549.6 80.3 %collective-permute-start.39 = (bf16[320,4096]{1,0:T(8,128)(2,1)}, bf16[320,4096]{1,0:T(8,128)(2,1)}, u32[]{:S(2)}, u32[]{:S(2)}) collective-permute-start(bf16[320,4096]{1,0:T(8,128)(2,1)} %multiply_convert_fusion.refs_0_), channel_id=1, source_target_pairs={{0,2},{1,3},{2,0},{3,1},{4,6},{5,7},{6,4},{7,5},{8,10},{9,11},{10,... | collective-permute-start | bytes 7864328 | tf_op jit(solution)/shard_map/ppermute | solution.py:439
  946.1 97.6 %collective-permute-start.59 = (bf16[320,4096]{1,0:T(8,128)(2,1)}, bf16[320,4096]{1,0:T(8,128)(2,1)}, u32[]{:S(2)}, u32[]{:S(2)}) collective-permute-start(bf16[320,4096]{1,0:T(8,128)(2,1)} %get-tuple-element.564), channel_id=1, source_target_pairs={{0,2},{1,3},{2,0},{3,1},{4,6},{5,7},{6,4},{7,5},{8,10},{9,11},{10,... | collective-permute-start | bytes 7864328 | tf_op jit(solution)/shard_map/ppermute | solution.py:439
  946.7 97.0 %collective-permute-start.62 = (bf16[2048,512]{1,0:T(8,128)(2,1)}, bf16[2048,512]{1,0:T(8,128)(2,1)}, u32[]{:S(2)}, u32[]{:S(2)}) collective-permute-start(bf16[2048,512]{1,0:T(8,128)(2,1)} %get-tuple-element.390), channel_id=1, source_target_pairs={{0,4},{4,0},{8,12},{12,8},{16,20},{20,16},{24,28},{28,24},{1,5},{5... | collective-permute-start | bytes 6291464 | tf_op jit(solution)/shard_map/ppermute | solution.py:439
  948.1 95.6 %collective-permute-start.63 = (bf16[2048,512]{1,0:T(8,128)(2,1)}, bf16[2048,512]{1,0:T(8,128)(2,1)}, u32[]{:S(2)}, u32[]{:S(2)}) collective-permute-start(bf16[2048,512]{1,0:T(8,128)(2,1)} %get-tuple-element.391), channel_id=1, source_target_pairs={{0,4},{4,0},{8,12},{12,8},{16,20},{20,16},{24,28},{28,24},{1,5},{5... | collective-permute-start | bytes 6291464 | tf_op jit(solution)/shard_map/ppermute | solution.py:439
  952.3 91.4 %collective-permute-start.61 = (bf16[1024,512]{1,0:T(8,128)(2,1)}, bf16[1024,512]{1,0:T(8,128)(2,1)}, u32[]{:S(2)}, u32[]{:S(2)}) collective-permute-start(bf16[1024,512]{1,0:T(8,128)(2,1)} %get-tuple-element.389), channel_id=1, source_target_pairs={{0,16},{4,20},{8,24},{12,28},{16,0},{20,4},{24,8},{28,12},{1,17},{... | collective-permute-start | bytes 3145736 | tf_op jit(solution)/shard_map/ppermute | solution.py:439
  1048.3 81.9 %collective-permute-start.66 = (bf16[320,4096]{1,0:T(8,128)(2,1)}, bf16[320,4096]{1,0:T(8,128)(2,1)}, u32[]{:S(2)}, u32[]{:S(2)}) collective-permute-start(bf16[320,4096]{1,0:T(8,128)(2,1)} %add_convert_fusion.11), channel_id=1, source_target_pairs={{0,8},{4,12},{8,0},{12,4},{16,24},{20,28},{24,16},{28,20},{1,9},{5... | collective-permute-start | bytes 7864328 | tf_op jit(solution)/shard_map/ppermute | solution.py:439
  1141.7 81.4 %collective-permute-start.70 = (bf16[320,4096]{1,0:T(8,128)(2,1)}, bf16[320,4096]{1,0:T(8,128)(2,1)}, u32[]{:S(2)}, u32[]{:S(2)}) collective-permute-start(bf16[320,4096]{1,0:T(8,128)(2,1)} %get-tuple-element.426.refs_0_), channel_id=1, source_target_pairs={{0,8},{4,12},{8,0},{12,4},{16,24},{20,28},{24,16},{28,20},{1,9},{5... | collective-permute-start | bytes 7864328 | tf_op jit(solution)/shard_map/ppermute | solution.py:439
  1143.3 79.8 %collective-permute-start.69 = (bf16[320,4096]{1,0:T(8,128)(2,1)}, bf16[320,4096]{1,0:T(8,128)(2,1)S(1)}, u32[]{:S(2)}, u32[]{:S(2)}) collective-permute-start(bf16[320,4096]{1,0:T(8,128)(2,1)} %get-tuple-element.426.refs_0_), channel_id=1, source_target_pairs={{0,2},{1,3},{2,0},{3,1},{4,6},{5,7},{6,4},{7,5},{8,10},{9,11},{10,... | collective-permute-start | bytes 7864328 | tf_op jit(solution)/shard_map/ppermute | solution.py:439
  1359.1 81.4 %collective-permute-start.83 = (bf16[320,4096]{1,0:T(8,128)(2,1)}, bf16[320,4096]{1,0:T(8,128)(2,1)S(1)}, u32[]{:S(2)}, u32[]{:S(2)}) collective-permute-start(bf16[320,4096]{1,0:T(8,128)(2,1)} %get-tuple-element.448), channel_id=1, source_target_pairs={{0,2},{1,3},{2,0},{3,1},{4,6},{5,7},{6,4},{7,5},{8,10},{9,11},{10,... | collective-permute-start | bytes 7864328 | tf_op jit(solution)/shard_map/ppermute | solution.py:439
  1360.2 81.0 %collective-permute-start.84 = (bf16[320,4096]{1,0:T(8,128)(2,1)}, bf16[320,4096]{1,0:T(8,128)(2,1)}, u32[]{:S(2)}, u32[]{:S(2)}) collective-permute-start(bf16[320,4096]{1,0:T(8,128)(2,1)} %add_convert_fusion.6), channel_id=1, source_target_pairs={{0,8},{4,12},{8,0},{12,4},{16,24},{20,28},{24,16},{28,20},{1,9},{5... | collective-permute-start | bytes 7864328 | tf_op jit(solution)/shard_map/ppermute | solution.py:439
  1526.7 93.1 %collective-permute-start.93 = (bf16[320,4096]{1,0:T(8,128)(2,1)}, bf16[320,4096]{1,0:T(8,128)(2,1)}, u32[]{:S(2)}, u32[]{:S(2)}) collective-permute-start(bf16[320,4096]{1,0:T(8,128)(2,1)} %get-tuple-element.551), channel_id=1, source_target_pairs={{0,2},{1,3},{2,0},{3,1},{4,6},{5,7},{6,4},{7,5},{8,10},{9,11},{10,... | collective-permute-start | bytes 7864328 | tf_op jit(solution)/shard_map/ppermute | solution.py:439
  1531.8 88.0 %collective-permute-start.94 = (bf16[512,1536]{1,0:T(8,128)(2,1)}, bf16[512,1536]{1,0:T(8,128)(2,1)}, u32[]{:S(2)}, u32[]{:S(2)}) collective-permute-start(bf16[512,1536]{1,0:T(8,128)(2,1)} %add_convert_fusion.24), channel_id=1, source_target_pairs={{0,16},{4,20},{8,24},{12,28},{16,0},{20,4},{24,8},{28,12},{1,17},{... | collective-permute-start | bytes 4718600 | tf_op jit(solution)/shard_map/ppermute | solution.py:439
  1534.4 85.4 %collective-permute-start.95 = (bf16[512,1536]{1,0:T(8,128)(2,1)}, bf16[512,1536]{1,0:T(8,128)(2,1)}, u32[]{:S(2)}, u32[]{:S(2)}) collective-permute-start(bf16[512,1536]{1,0:T(8,128)(2,1)} %get-tuple-element.488), channel_id=1, source_target_pairs={{0,4},{4,0},{8,12},{12,8},{16,20},{20,16},{24,28},{28,24},{1,5},{5... | collective-permute-start | bytes 4718600 | tf_op jit(solution)/shard_map/ppermute | solution.py:439
  1540.0 79.8 %collective-permute-start.97 = (bf16[512,1024]{1,0:T(8,128)(2,1)}, bf16[512,1024]{1,0:T(8,128)(2,1)}, u32[]{:S(2)}, u32[]{:S(2)}) collective-permute-start(bf16[512,1024]{1,0:T(8,128)(2,1)} %get-tuple-element.491), channel_id=1, source_target_pairs={{0,8},{4,12},{8,0},{12,4},{16,24},{20,28},{24,16},{28,20},{1,9},{5... | collective-permute-start | bytes 3145736 | tf_op jit(solution)/shard_map/ppermute | solution.py:439
  1624.2 93.3 %collective-permute-start.100 = (bf16[320,4096]{1,0:T(8,128)(2,1)}, bf16[320,4096]{1,0:T(8,128)(2,1)}, u32[]{:S(2)}, u32[]{:S(2)}) collective-permute-start(bf16[320,4096]{1,0:T(8,128)(2,1)} %add_convert_fusion), channel_id=1, source_target_pairs={{0,8},{4,12},{8,0},{12,4},{16,24},{20,28},{24,16},{28,20},{1,9},{5... | collective-permute-start | bytes 7864328 | tf_op jit(solution)/shard_map/ppermute | solution.py:439
  1631.8 85.7 %collective-permute-start.99 = (bf16[320,4096]{1,0:T(8,128)(2,1)}, bf16[320,4096]{1,0:T(8,128)(2,1)}, u32[]{:S(2)}, u32[]{:S(2)}) collective-permute-start(bf16[320,4096]{1,0:T(8,128)(2,1)} %get-tuple-element.547), channel_id=1, source_target_pairs={{0,2},{1,3},{2,0},{3,1},{4,6},{5,7},{6,4},{7,5},{8,10},{9,11},{10,... | collective-permute-start | bytes 7864328 | tf_op jit(solution)/shard_map/ppermute | solution.py:439
  1636.0 79.3 %collective-permute-start.101 = (bf16[512,1536]{1,0:T(8,128)(2,1)}, bf16[512,1536]{1,0:T(8,128)(2,1)}, u32[]{:S(2)}, u32[]{:S(2)}) collective-permute-start(bf16[512,1536]{1,0:T(8,128)(2,1)} %add_convert_fusion.23), channel_id=1, source_target_pairs={{0,16},{4,20},{8,24},{12,28},{16,0},{20,4},{24,8},{28,12},{1,17},{... | collective-permute-start | bytes 4718600 | tf_op jit(solution)/shard_map/ppermute | solution.py:439
  1636.0 79.3 %collective-permute-start.102 = (bf16[512,1536]{1,0:T(8,128)(2,1)}, bf16[512,1536]{1,0:T(8,128)(2,1)}, u32[]{:S(2)}, u32[]{:S(2)}) collective-permute-start(bf16[512,1536]{1,0:T(8,128)(2,1)} %get-tuple-element.501), channel_id=1, source_target_pairs={{0,4},{4,0},{8,12},{12,8},{16,20},{20,16},{24,28},{28,24},{1,5},{5... | collective-permute-start | bytes 4718600 | tf_op jit(solution)/shard_map/ppermute | solution.py:439
  (157 other events, 6659.4 us)

commit v4 on v3

--- a/solution.py
+++ b/solution.py
@@ -520,7 +520,7 @@
                 self.have[0, 0, 1] = [self.chunks["swap", i] for i in range(of)]
 
         def zh(self, source, c=0, of=1):
-            if source == 1 and of > 1 and ("swap", of - 1) in self.chunks:
+            if source == 1 and of > 1 and ("other", c) in self.chunks:
                 v = self.chunks["swap", c]
             elif source == 0 and of > 1:
                 v = self.chunks["mine", c]
@@ -555,7 +555,6 @@
     gains = jnp.stack([norm1_gain, norm2_gain])
     gain_chain = [joined(gains, pp_zl(gains), 1)]
     gain_chain = jnp.concatenate(gain_chain + ring_up(gain_chain[0]), axis=0)
-    gain_other = pp_y(gain_chain)
     qkv_heads = (
         qkv_weight.reshape(unit, 3, 2 * heads, HEAD)
         .transpose(0, 2, 1, 3)
@@ -564,9 +563,10 @@
     qkv_w = Weight(*halves(qkv_heads, 1))
     out_mine, out_other = halves(out_weight, 0)
     other_ids = move(pp_zl, segment_ids)
-    steps.pending += [gain_other, gain_chain, qkv_w.have[0, 0, 0], qkv_w.other, out_other]
-    close()
-
+    steps.pending += [gain_chain, qkv_w.have[0, 0, 0], qkv_w.other, out_other]
+    close()
+
+    gain_other = move(pp_y, gain_chain)
     gains = jnp.concatenate(
         [(gain_chain, gain_other)[j][2 * k : 2 * k + 2] for k, j in pairs], axis=1
     ).astype(F32)
@@ -616,8 +616,8 @@
     slopes = 2.0 ** (-8.0 * (head_index + 1).astype(F32) / H)
     two = 2 * piece
 
-    def batch(near, far):
-        return [(near, 0, two), (far, 0, two)]
+    def batch(*pieces):
+        return [(v, 0, v.shape[0]) for v in pieces]
 
     w_qkv, at_qkv = qkv_w.blocks()
     one_b = gather(az, ad)
@@ -625,8 +625,8 @@
     up_w.zh(0, 0, 2)
     out_w.y(0)
     out_w.yz(0)
-    cx_top = move(pp_x, cot[:half])
-    up_w.swap(1, 2)
+    cx = move(pp_x, cot)
+    cz_top = move(pp_zl, cot[:half])
     one_b_rows = batch(one_b, one_b_far)
     one_a_rows = batch(one_a, one_a_far)
     qkv_a = run(lambda v: deep(batch(v, one_a_far), w_qkv, at_qkv, 0), one_a)
@@ -696,8 +696,11 @@
     sums_b = run(broad, att_b, w_out, at_out, 0)
     up_w.zh(0, 1, 2)
     up_w.y(0)
-    cz_top = move(pp_zl, cot[:half])
-    cx_bottom = move(pp_x, cot[half:])
+    cz_bottom = move(pp_zl, cot[half:])
+    cd_top = move(pp_x, cz_top)
+    near_cot_a = gather(cot, cx)
+    far_cot_a = pp_core(near_cot_a)
+    steps.pending.append(far_cot_a)
     close()
 
     ez, ed = core_sum(*sums_b)
@@ -705,7 +708,7 @@
     steps.pending += [ez, from_d]
     up_w.zh(1, 0, 2)
     up_w.yz(0)
-    cz_bottom = move(pp_zl, cot[half:])
+    up_w.swap(1, 2)
     att_a, lse_a = run(attend, qkv_a, start_a)
     sums_a = run(broad, att_a, w_out, at_out, 0)
     close()
@@ -716,14 +719,12 @@
     from_z = move(pp_zl, plus(steps.begin(ez), from_d))
     up_w.zh(1, 1, 2)
     up_w.y(1)
-    cz = gather(cz_top, cz_bottom)
-    near_cot_a = gather(cot, cx_top, cx_bottom)
     close()
 
     resid = x + (steps.begin(e00).astype(F32) + from_x.astype(F32) + from_z.astype(F32))
     normed_two, inverse_two = norm_forward(resid)
     a_two = (normed_two * gain_two).astype(BF)
-    far_cot_a = move(pp_core, near_cot_a)
+    a_two_far = move(pp_core, a_two)
     ax = move(pp_x, a_two)
     az = move(pp_zl, a_two)
     down_w.zh(0, 0, 2)
@@ -732,25 +733,25 @@
 
     w_up, at_up = up_w.blocks()
 
-    def lift(near, far):
-        return deep(batch(near, far), w_up, at_up, 0, finish=gelu_and_slope, outs=2, cuts=2)
-
-    two_a = gather(a_two, ax)
+    def lift(*pieces):
+        return deep(batch(*pieces), w_up, at_up, 0, finish=gelu_and_slope, outs=2)
+
+    ax_far = move(pp_core, ax)
     ad = move(pp_x, az)
-    two_a_far = move(pp_core, two_a)
+    two_a = (a_two, ax, a_two_far, ax_far)
     down_w.zh(0, 1, 2)
     down_w.y(0)
     down_w.swap(0, 2)
-    act_a, slope_a = run(lambda v: lift(two_a, v), two_a_far)
-    close()
-
-    two_b = gather(az, ad)
-    two_b_far = move(pp_core, two_b)
+    act_a, slope_a = run(lambda v: lift(a_two, ax, a_two_far, v), ax_far)
+    close()
+
+    az_far, ad_far = move(pp_core, az), move(pp_core, ad)
+    two_b = (az, ad, az_far, ad_far)
     down_w.yz(0)
     down_w.swap(1, 2)
     down_w.zh(1, 0, 2)
-    cd = move(pp_x, cz)
-    act_b, slope_b = run(lambda v: lift(two_b, v), two_b_far)
+    cd_bottom = move(pp_x, cz_bottom)
+    act_b, slope_b = run(lambda v: lift(*two_b[:3], v), ad_far)
     close()
 
     class Sum:
@@ -827,9 +828,9 @@
         steps.pending.append(out)
         return out
 
+    near_cot_b = gather(cz_top, cz_bottom, cd_top, cd_bottom)
+    far_cot_b = move(pp_core, near_cot_b)
     down_g, up_g, out_g, qkv_g = Sum(1), Sum(0), Sum(1, True), Sum(0)
-    near_cot_b = gather(cz, cd)
-    far_cot_b = move(pp_core, near_cot_b)
     down_w.zh(1, 1, 2)
     down_w.y(1)
     cot_a, cot_b = batch(near_cot_a, far_cot_a), batch(near_cot_b, far_cot_b)
@@ -875,7 +876,7 @@
     from_z = move(pp_zl, plus(steps.begin(ez), from_d))
     down_g.zh(1, 0)
     down_g.y_own(1)
-    two_rows = [batch(two_a, two_a_far), batch(two_b, two_b_far)]
+    two_rows = [batch(*two_a), batch(*two_b)]
     dus = [[(du_a, 0, 2 * two)], [(du_b, 0, 2 * two)]]
     up_g.make(1, two_rows, dus)
     up_g.make(0, two_rows, dus)
@@ -885,37 +886,39 @@
     grad_part, grad_gain_two = norm_backward(grad_in_two, normed_two, inverse_two, gain_two)
     grad_resid = cot.astype(F32) + grad_part
     grad_rows = grad_resid.astype(BF)
+    grad_far = move(pp_core, grad_rows)
     ax = move(pp_x, grad_rows)
     az = move(pp_zl, grad_rows)
     down_g.zh(1, 1)
     up_g.y_far(0)
+    down_g.ready(0)
     out_b = run(broad, act_b, w_down, at_down, 0)
     out_a = run(broad, act_a, w_down, at_down, 0)
     close()
 
-    grad_a = gather(grad_rows, ax)
-    grad_a_far = move(pp_core, grad_a)
+    ax_far = move(pp_core, ax)
+    grad_a = (grad_rows, ax, grad_far, ax_far)
     ad = move(pp_x, az)
     up_g.zh(0, 0)
     up_g.y_far(1)
+    down_g.zl(0)
     o_b = core_sum(*out_b)
     steps.pending += o_b
-    dov_a = run(lambda v: deep(batch(grad_a, v), w_out, at_out, 1), grad_a_far)
+    dov_a = run(lambda v: deep(batch(*grad_a[:3], v), w_out, at_out, 1), ax_far)
     proj_a = attend_back(dov_a, qkv_a, start_a, lse_a)
     steps.pending.append(proj_a)
     close()
 
-    grad_b = gather(az, ad)
-    grad_b_far = move(pp_core, grad_b)
+    az_far, ad_far = move(pp_core, az), move(pp_core, ad)
+    grad_b = (az, ad, az_far, ad_far)
     up_g.zh(1, 0)
     up_g.y_own(0)
     oz, od = o_b
     from_od = move(pp_x, od)
     o_a = core_sum(*out_a)
     steps.pending += o_a
-    down_g.ready(0)
     down_g.ready(1)
-    dov_b = run(lambda v: deep(batch(grad_b, v), w_out, at_out, 1), grad_b_far)
+    dov_b = run(lambda v: deep(batch(*grad_b[:3], v), w_out, at_out, 1), ad_far)
     proj_b = attend_back(dov_b, qkv_b, start_b, lse_b)
     steps.pending.append(proj_b)
     close()
@@ -930,11 +933,10 @@
     qkv_g.make(1, one_rows, projs)
     qkv_g.make(0, one_rows, projs)
     atts = [[(att_a, 0, 2 * two)], [(att_b, 0, 2 * two)]]
-    grads = [batch(grad_a, grad_a_far), batch(grad_b, grad_b_far)]
+    grads = [batch(*grad_a), batch(*grad_b)]
     out_g.make(1, atts, grads)
     close()
 
-    down_g.zl(0)
     down_g.zl(1)
     qkv_g.y_far(0)
     up_g.zh(1, 1)
@@ -957,7 +959,6 @@
     qkv_g.y_far(1)
     up_g.zl(0)
     up_g.ready(1)
-    up_g.zl(1)
     sums_a = run(broad, proj_a, w_qkv, at_qkv, 1)
     grad_down = finished(lambda: joined(steps.begin(down_g.result()[0]), down_g.result()[1], 0).astype(F32))
     close()
@@ -973,8 +974,8 @@
 
     out_g.y_own(0)
     out_g.zh(0, 0, 1)
+    up_g.zl(1)
     qkv_g.ready(0, 1)
-    grad_up = finished(lambda: joined(steps.begin(up_g.result()[0]), up_g.result()[1], 1).astype(F32))
     qkv_g.value[3, 0] = pp_zl(qkv_g.value[3, 0])
     steps.pending.append(qkv_g.value[3, 0])
     grad_in_one = steps.begin(e00).astype(F32) + from_x.astype(F32) + from_z.astype(F32)
@@ -991,6 +992,7 @@
 
     out_g.ready(0, 1)
     out_g.value[3, 0] = pp_zl(out_g.value[3, 0])
+    grad_up = joined(steps.begin(up_g.result()[0]), up_g.result()[1], 1).astype(F32)
     mine, other = qkv_g.result(1)
     grad_qkv = finished(
         lambda: joined(parts_first(steps.begin(mine)), parts_first(other), 2).astype(F32)

time: 1830 us -> 1800 us (0.984)
  Pallas kernels: 748 us -> 726 us
    pallas_call x15 -> x10, Pallas kernels: 62.4 us -> 40.2 us  [stack_rows(): pl.pallas_call(body, out_shape=jax.ShapeDtypeStruct((sum(sizes) * rows, c...]
    ppermute x113 -> x117, starting transfers between devices: 122 us -> 104 us  [over(): return lambda v: lax.ppermute(v, axis, [(i, to(i)) for i in range(size)])]
    ppermute x113 -> x117, waiting for transfers between devices: 701 us -> 715 us  [over(): return lambda v: lax.ppermute(v, axis, [(i, to(i)) for i in range(size)])]
  transfers between devices with their start and end apart: 113 -> 117, of which waited for: 53 -> 56; matrix products, arithmetic and copies ran while one was open for 10% -> 10% of each run, Pallas kernels for 39% -> 39%
where the time goes in v4:
time: 1800 us; the launch traced here: 1790 us
  Pallas kernels  726 us (40%)
  waiting for transfers between devices  715 us (40%)
  other arithmetic  198 us (11%)
  starting transfers between devices  104 us (6%)
  local copies, waits for them, and re-layouts  49.8 us (3%)
    ppermute x117, waiting for transfers between devices, over(): return lambda v: lax.ppermute(v, axis, [(i, to(i)) for i in range(size)])  715 us
    pallas_call x8, Pallas kernels, gram(): pl.pallas_call(body, out_shape=[jax.ShapeDtypeStruct((m, n), BF)] * count...  209 us
    pallas_call x8, Pallas kernels, broad(): pl.pallas_call(body, out_shape=[jax.ShapeDtypeStruct((m // 2, n), BF)] *...  203 us
    pallas_call x8, Pallas kernels, deep(): pl.pallas_call(body, out_shape=[jax.ShapeDtypeStruct((m, n), BF)] * outs,...  203 us
    ppermute x117, starting transfers between devices, over(): return lambda v: lax.ppermute(v, axis, [(i, to(i)) for i in range(size)])  104 us
    convert_element_type x23, other arithmetic, plus(): return sum((v.astype(F32) for v in terms)).astype(BF)  79.3 us
    pallas_call x2, Pallas kernels, attend_back(): pl.pallas_call(attention_backward, out_shape=jax.ShapeDtypeStruct((2, 2,...  40.6 us
    pallas_call x10, Pallas kernels, stack_rows(): pl.pallas_call(body, out_shape=jax.ShapeDtypeStruct((sum(sizes) * rows, c...  40.2 us
  transfers between devices with their start and end apart: 117, of which 56 were waited for; matrix products, arithmetic and copies ran while one was open for 10% of the time, Pallas kernels for 39%

profile of v4, /device:TPU:0, one launch (start us, length us, event | category | flops | bytes accessed | tf_op | source)
XLA Modules:
  0.0 1794.5 jit_solution(17699388362120191754)
XLA Ops:
  68.4 33.3 %collective-permute-done.4.refs_3_.rest_1_ = bf16[512,1536]{1,0:T(8,128)(2,1)} collective-permute-done((bf16[512,1536]{1,0:T(8,128)(2,1)}, bf16[512,1536]{1,0:T(8,128)(2,1)}, u32[]{:S(2)}, u32[]{:S(2)}) %collective-permute-start.4) | collective-permute-done | bytes 1572896 | tf_op jit(solution)/shard_map/ppermute | solution.py:439
  139.5 31.3 %collective-permute-done.8.refs_7_.rest_5_ = bf16[512,1536]{1,0:T(8,128)(2,1)} collective-permute-done((bf16[512,1536]{1,0:T(8,128)(2,1)}, bf16[512,1536]{1,0:T(8,128)(2,1)}, u32[]{:S(2)}, u32[]{:S(2)}) %collective-permute-start.8) | collective-permute-done | bytes 1572896 | tf_op jit(solution)/shard_map/ppermute | solution.py:439
  203.0 45.6 %collective-permute-done.15.rest_2_.refs_6_ = bf16[512,1024]{1,0:T(8,128)(2,1)} collective-permute-done((bf16[512,1024]{1,0:T(8,128)(2,1)}, bf16[512,1024]{1,0:T(8,128)(2,1)}, u32[]{:S(2)}, u32[]{:S(2)}) %collective-permute-start.15) | collective-permute-done | bytes 1048608 | tf_op jit(solution)/shard_map/ppermute | solution.py:439
  477.0 64.6 %collective-permute-done.37.refs_1_ = bf16[256,2048]{1,0:T(8,128)(2,1)S(1)} collective-permute-done((bf16[256,2048]{1,0:T(8,128)(2,1)}, bf16[256,2048]{1,0:T(8,128)(2,1)S(1)}, u32[]{:S(2)}, u32[]{:S(2)}) %collective-permute-start.37) | collective-permute-done | bytes 1048608 | tf_op jit(solution)/shard_map/ppermute | solution.py:439
  560.2 73.4 %collective-permute-done.42.refs_0_ = bf16[1024,512]{1,0:T(8,128)(2,1)S(1)} collective-permute-done((bf16[1024,512]{1,0:T(8,128)(2,1)}, bf16[1024,512]{1,0:T(8,128)(2,1)S(1)}, u32[]{:S(2)}, u32[]{:S(2)}) %collective-permute-start.42) | collective-permute-done | bytes 1048608 | tf_op jit(solution)/shard_map/ppermute | solution.py:439
  639.6 33.7 %deep.10 = (bf16[1280,2048]{1,0:T(8,128)(2,1)}, bf16[1280,2048]{1,0:T(8,128)(2,1)}) custom-call(s32[8]{0:T(128)} %stack.74.starts_ref, bf16[320,4096]{1,0:T(8,128)(2,1)} %multiply_convert_fusion.refs_0_, bf16[320,4096]{1,0:T(8,128)(2,1)} %collective-permute-done.39.refs_1_, bf16[320,4096]{1,0:T(8,128)(2,1)} %collective-permute-done.40.refs_2_, ...), custom_call_target="tpu_custom_call" | custom-call | flops 1073741824 | bytes 32505856 | tf_op jit(solution)/shard_map/deep/pallas_call | solution.py:251
  703.0 33.9 %deep.11 = (bf16[1280,2048]{1,0:T(8,128)(2,1)}, bf16[1280,2048]{1,0:T(8,128)(2,1)}) custom-call(s32[8]{0:T(128)} %stack.74.starts_ref, bf16[320,4096]{1,0:T(8,128)(2,1)} %collective-permute-done.41.refs_0_.refs_4_, bf16[320,4096]{1,0:T(8,128)(2,1)} %collective-permute-done.45.refs_1_.refs_5_, bf16[320,4096]{1,0:T(8,128)(2,1)} %collective-permute-done.49.refs_2_.refs_6_, ...), custom_call_target="tpu_custom_call" | custom-call | flops 1073741824 | bytes 32505856 | tf_op jit(solution)/shard_map/deep/pallas_call | solution.py:251
  764.7 32.2 %gram.8 = (bf16[2048,512]{1,0:T(8,128)(2,1)}, bf16[2048,512]{1,0:T(8,128)(2,1)}, bf16[2048,512]{1,0:T(8,128)(2,1)}, bf16[2048,512]{1,0:T(8,128)(2,1)}) custom-call(s32[4]{0:T(128)} %constant.155.clone.index_ref, bf16[1280,2048]{1,0:T(8,128)(2,1)} %get-tuple-element.409.refs_0_.a_ref, bf16[1280,2048]{1,0:T(8,128)(2,1)} %get-tuple-element.417.refs_1_.a_ref, ...), custom_call_target="tpu_custom_call" | custom-call | flops 1073741824 | bytes 29360128 | tf_op jit(solution)/shard_map/gram/pallas_call | solution.py:183
  812.2 32.2 %gram.9 = (bf16[2048,512]{1,0:T(8,128)(2,1)}, bf16[2048,512]{1,0:T(8,128)(2,1)}, bf16[2048,512]{1,0:T(8,128)(2,1)}, bf16[2048,512]{1,0:T(8,128)(2,1)}) custom-call(s32[4]{0:T(128)} %constant.156.clone.index_ref, bf16[1280,2048]{1,0:T(8,128)(2,1)} %get-tuple-element.409.refs_0_.a_ref, bf16[1280,2048]{1,0:T(8,128)(2,1)} %get-tuple-element.417.refs_1_.a_ref, ...), custom_call_target="tpu_custom_call" | custom-call | flops 1073741824 | bytes 29360128 | tf_op jit(solution)/shard_map/gram/pallas_call | solution.py:183
  860.1 30.6 %deep.12.a_ref.refs_9_ = bf16[1280,2048]{1,0:T(8,128)(2,1)} custom-call(s32[8]{0:T(128)} %stack.74.starts_ref, bf16[640,4096]{1,0:T(8,128)(2,1)} %stack_rows.17.refs_4_.refs_0_, bf16[640,4096]{1,0:T(8,128)(2,1)} %collective-permute-done.55.refs_5_.refs_1_, bf16[2048,512]{1,0:T(8,128)(2,1)} %copy-done.3, bf16[2048,512]{1,0:T(8,128)(2,1)} %stack_rows.18.refs_3_.rest_1_, ...), custom_call_target="tpu_custom_call" | custom-call | flops 1073741824 | bytes 32505856 | tf_op jit(solution)/shard_map/deep/pallas_call | solution.py:251
  890.8 32.3 %broad.10 = (bf16[640,4096]{1,0:T(8,128)(2,1)}, bf16[640,4096]{1,0:T(8,128)(2,1)}) custom-call(s32[8]{0:T(128)} %stack.74.starts_ref, bf16[1280,2048]{1,0:T(8,128)(2,1)} %deep.12.a_ref.refs_9_, bf16[512,2048]{1,0:T(8,128)(2,1)} %get-tuple-element.303.refs_4_.rest_0_, bf16[512,2048]{1,0:T(8,128)(2,1)} %stack_rows.14.refs_5_.rest_1_, ...), custom_call_target="tpu_custom_call" | custom-call | flops 1073741824 | bytes 32505856 | tf_op jit(solution)/shard_map/broad/pallas_call | solution.py:286
  945.6 30.8 %deep.13.a_ref.refs_8_ = bf16[1280,2048]{1,0:T(8,128)(2,1)} custom-call(s32[8]{0:T(128)} %stack.74.starts_ref, bf16[640,4096]{1,0:T(8,128)(2,1)} %stack_rows.12.refs_2_.refs_0_, bf16[640,4096]{1,0:T(8,128)(2,1)} %collective-permute-done.28.refs_3_.refs_1_, bf16[2048,512]{1,0:T(8,128)(2,1)} %copy-done.3, bf16[2048,512]{1,0:T(8,128)(2,1)} %stack_rows.18.refs_3_.rest_1_, ...), custom_call_target="tpu_custom_call" | custom-call | flops 1073741824 | bytes 32505856 | tf_op jit(solution)/shard_map/deep/pallas_call | solution.py:251
  976.4 31.9 %broad.11 = (bf16[640,4096]{1,0:T(8,128)(2,1)}, bf16[640,4096]{1,0:T(8,128)(2,1)}) custom-call(s32[8]{0:T(128)} %stack.74.starts_ref, bf16[1280,2048]{1,0:T(8,128)(2,1)} %deep.13.a_ref.refs_8_, bf16[512,2048]{1,0:T(8,128)(2,1)} %get-tuple-element.303.refs_4_.rest_0_, bf16[512,2048]{1,0:T(8,128)(2,1)} %stack_rows.14.refs_5_.rest_1_, ...), custom_call_target="tpu_custom_call" | custom-call | flops 1073741824 | bytes 32505856 | tf_op jit(solution)/shard_map/broad/pallas_call | solution.py:286
  1051.6 32.9 %gram.11 = (bf16[512,2048]{1,0:T(8,128)(2,1)}, bf16[512,2048]{1,0:T(8,128)(2,1)}, bf16[512,2048]{1,0:T(8,128)(2,1)}, bf16[512,2048]{1,0:T(8,128)(2,1)}) custom-call(s32[4]{0:T(128)} %constant.156.clone.index_ref, bf16[320,4096]{1,0:T(8,128)(2,1)} %multiply_convert_fusion.refs_0_, bf16[320,4096]{1,0:T(8,128)(2,1)} %collective-permute-done.39.refs_1_, ...), custom_call_target="tpu_custom_call" | custom-call | flops 1073741824 | bytes 52953088 | tf_op jit(solution)/shard_map/gram/pallas_call | solution.py:183
  1084.5 32.6 %gram.10 = (bf16[512,2048]{1,0:T(8,128)(2,1)}, bf16[512,2048]{1,0:T(8,128)(2,1)}, bf16[512,2048]{1,0:T(8,128)(2,1)}, bf16[512,2048]{1,0:T(8,128)(2,1)}) custom-call(s32[4]{0:T(128)} %constant.155.clone.index_ref, bf16[320,4096]{1,0:T(8,128)(2,1)} %multiply_convert_fusion.refs_0_, bf16[320,4096]{1,0:T(8,128)(2,1)} %collective-permute-done.39.refs_1_, ...), custom_call_target="tpu_custom_call" | custom-call | flops 1073741824 | bytes 52953088 | tf_op jit(solution)/shard_map/gram/pallas_call | solution.py:183
  1139.7 32.4 %broad.12 = (bf16[640,4096]{1,0:T(8,128)(2,1)}, bf16[640,4096]{1,0:T(8,128)(2,1)}) custom-call(s32[8]{0:T(128)} %stack.74.starts_ref, bf16[1280,2048]{1,0:T(8,128)(2,1)} %get-tuple-element.409.refs_0_.a_ref, bf16[2048,512]{1,0:T(8,128)(2,1)} %copy-done.3, bf16[2048,512]{1,0:T(8,128)(2,1)} %stack_rows.18.refs_3_.rest_1_, ...), custom_call_target="tpu_custom_call" | custom-call | flops 1073741824 | bytes 32505856 | tf_op jit(solution)/shard_map/broad/pallas_call | solution.py:286
  1172.0 32.3 %broad.13 = (bf16[640,4096]{1,0:T(8,128)(2,1)}, bf16[640,4096]{1,0:T(8,128)(2,1)}) custom-call(s32[8]{0:T(128)} %stack.74.starts_ref, bf16[1280,2048]{1,0:T(8,128)(2,1)} %get-tuple-element.417.refs_1_.a_ref, bf16[2048,512]{1,0:T(8,128)(2,1)} %copy-done.3, bf16[2048,512]{1,0:T(8,128)(2,1)} %stack_rows.18.refs_3_.rest_1_, ...), custom_call_target="tpu_custom_call" | custom-call | flops 1073741824 | bytes 32505856 | tf_op jit(solution)/shard_map/broad/pallas_call | solution.py:286
  1360.7 27.4 %gram.13 = (bf16[512,1536]{1,0:T(8,128)(2,1)}, bf16[512,1536]{1,0:T(8,128)(2,1)}, bf16[512,1536]{1,0:T(8,128)(2,1)}, bf16[512,1536]{1,0:T(8,128)(2,1)}) custom-call(s32[4]{0:T(128)} %constant.156.clone.index_ref, bf16[640,4096]{1,0:T(8,128)(2,1)} %stack_rows.10.refs_0_, bf16[640,4096]{1,0:T(8,128)(2,1)} %collective-permute-done.16.refs_1_, ...), custom_call_target="tpu_custom_call" | custom-call | flops 805306368 | bytes 40370176 | tf_op jit(solution)/shard_map/gram/pallas_call | solution.py:183
  1388.1 27.0 %gram.12 = (bf16[512,1536]{1,0:T(8,128)(2,1)}, bf16[512,1536]{1,0:T(8,128)(2,1)}, bf16[512,1536]{1,0:T(8,128)(2,1)}, bf16[512,1536]{1,0:T(8,128)(2,1)}) custom-call(s32[4]{0:T(128)} %constant.155.clone.index_ref, bf16[640,4096]{1,0:T(8,128)(2,1)} %stack_rows.10.refs_0_, bf16[640,4096]{1,0:T(8,128)(2,1)} %collective-permute-done.16.refs_1_, ...), custom_call_target="tpu_custom_call" | custom-call | flops 805306368 | bytes 40370176 | tf_op jit(solution)/shard_map/gram/pallas_call | solution.py:183
  1453.0 25.3 %broad.14 = (bf16[640,4096]{1,0:T(8,128)(2,1)}, bf16[640,4096]{1,0:T(8,128)(2,1)}) custom-call(s32[8]{0:T(128)} %stack.74.starts_ref, bf16[1280,1536]{1,0:T(8,128)(2,1)} %bitcast.46, bf16[512,1536]{1,0:T(8,128)(2,1)} %get-tuple-element.262.refs_2_.rest_0_, bf16[512,1536]{1,0:T(8,128)(2,1)} %collective-permute-done.4.refs_3_.rest_1_, ...), custom_call_target="tpu_custom_call" | custom-call | flops 805306368 | bytes 27000832 | tf_op jit(solution)/shard_map/broad/pallas_call | solution.py:286
  1507.5 25.2 %broad.15 = (bf16[640,4096]{1,0:T(8,128)(2,1)}, bf16[640,4096]{1,0:T(8,128)(2,1)}) custom-call(s32[8]{0:T(128)} %stack.74.starts_ref, bf16[1280,1536]{1,0:T(8,128)(2,1)} %bitcast.43, bf16[512,1536]{1,0:T(8,128)(2,1)} %get-tuple-element.262.refs_2_.rest_0_, bf16[512,1536]{1,0:T(8,128)(2,1)} %collective-permute-done.4.refs_3_.rest_1_, ...), custom_call_target="tpu_custom_call" | custom-call | flops 805306368 | bytes 27000832 | tf_op jit(solution)/shard_map/broad/pallas_call | solution.py:286
  1550.2 25.8 %collective-permute-done.98 = bf16[512,1536]{1,0:T(8,128)(2,1)} collective-permute-done((bf16[512,1536]{1,0:T(8,128)(2,1)}, bf16[512,1536]{1,0:T(8,128)(2,1)}, u32[]{:S(2)}, u32[]{:S(2)}) %collective-permute-start.98) | collective-permute-done | bytes 1572896 | tf_op jit(solution)/shard_map/ppermute | solution.py:439
  1598.5 73.0 %collective-permute-done.104 = bf16[512,1536]{1,0:T(8,128)(2,1)} collective-permute-done((bf16[512,1536]{1,0:T(8,128)(2,1)}, bf16[512,1536]{1,0:T(8,128)(2,1)}, u32[]{:S(2)}, u32[]{:S(2)}) %collective-permute-start.104) | collective-permute-done | bytes 1572896 | tf_op jit(solution)/shard_map/ppermute | solution.py:439
  1731.1 32.6 %collective-permute-done.113 = bf16[512,1536]{1,0:T(8,128)(2,1)S(1)} collective-permute-done((bf16[512,1536]{1,0:T(8,128)(2,1)S(1)}, bf16[512,1536]{1,0:T(8,128)(2,1)S(1)}, u32[]{:S(2)}, u32[]{:S(2)}) %collective-permute-start.113) | collective-permute-done | bytes 1572896 | tf_op jit(solution)/shard_map/ppermute | solution.py:439
  (556 shorter events, 920.2 us)
Async XLA Ops:
  19.1 82.7 %collective-permute-start.6 = (bf16[512,1536]{1,0:T(8,128)(2,1)}, bf16[512,1536]{1,0:T(8,128)(2,1)}, u32[]{:S(2)}, u32[]{:S(2)}) collective-permute-start(bf16[512,1536]{1,0:T(8,128)(2,1)} %get-tuple-element.262.refs_2_.rest_0_), channel_id=1, source_target_pairs={{0,16},{4,20},{8,24},{12,28},{16,0},{20,4},{24,8},{28,12},{1,17},{... | collective-permute-start | bytes 4718600 | tf_op jit(solution)/shard_map/ppermute | solution.py:439
  22.0 79.8 %collective-permute-start.5 = (bf16[512,1536]{1,0:T(8,128)(2,1)}, bf16[512,1536]{1,0:T(8,128)(2,1)}, u32[]{:S(2)}, u32[]{:S(2)}) collective-permute-start(bf16[512,1536]{1,0:T(8,128)(2,1)} %get-tuple-element.262.refs_2_.rest_0_), channel_id=1, source_target_pairs={{0,4},{4,0},{8,12},{12,8},{16,20},{20,16},{24,28},{28,24},{1,5},{5... | collective-permute-start | bytes 4718600 | tf_op jit(solution)/shard_map/ppermute | solution.py:439
  105.3 88.8 %collective-permute-start.11 = (bf16[320,4096]{1,0:T(8,128)(2,1)}, bf16[320,4096]{1,0:T(8,128)(2,1)}, u32[]{:S(2)}, u32[]{:S(2)}) collective-permute-start(bf16[320,4096]{1,0:T(8,128)(2,1)} %fusion.6.refs_0_), channel_id=1, source_target_pairs={{0,8},{4,12},{8,0},{12,4},{16,24},{20,28},{24,16},{28,20},{1,9},{5... | collective-permute-start | bytes 7864328 | tf_op jit(solution)/shard_map/ppermute | solution.py:439
  461.0 82.0 %collective-permute-start.36 = (bf16[320,4096]{1,0:T(8,128)(2,1)S(1)}, bf16[320,4096]{1,0:T(8,128)(2,1)S(1)}, u32[]{:S(2)}, u32[]{:S(2)}) collective-permute-start(bf16[320,4096]{1,0:T(8,128)(2,1)S(1)} %add_convert_fusion.16), channel_id=1, source_target_pairs={{0,8},{4,12},{8,0},{12,4},{16,24},{20,28},{24,16},{28,20},{1,9},{5... | collective-permute-start | bytes 7864328 | tf_op jit(solution)/shard_map/ppermute | solution.py:439
  552.5 81.9 %collective-permute-start.41 = (bf16[320,4096]{1,0:T(8,128)(2,1)}, bf16[320,4096]{1,0:T(8,128)(2,1)}, u32[]{:S(2)}, u32[]{:S(2)}) collective-permute-start(bf16[320,4096]{1,0:T(8,128)(2,1)} %multiply_convert_fusion.refs_0_), channel_id=1, source_target_pairs={{0,8},{4,12},{8,0},{12,4},{16,24},{20,28},{24,16},{28,20},{1,9},{5... | collective-permute-start | bytes 7864328 | tf_op jit(solution)/shard_map/ppermute | solution.py:439
  554.7 79.7 %collective-permute-start.40 = (bf16[320,4096]{1,0:T(8,128)(2,1)}, bf16[320,4096]{1,0:T(8,128)(2,1)}, u32[]{:S(2)}, u32[]{:S(2)}) collective-permute-start(bf16[320,4096]{1,0:T(8,128)(2,1)} %multiply_convert_fusion.refs_0_), channel_id=1, source_target_pairs={{0,1},{1,0},{2,3},{3,2},{4,5},{5,4},{6,7},{7,6},{8,9},{9,8},{10,11... | collective-permute-start | bytes 7864328 | tf_op jit(solution)/shard_map/ppermute | solution.py:439
  554.7 79.7 %collective-permute-start.39 = (bf16[320,4096]{1,0:T(8,128)(2,1)}, bf16[320,4096]{1,0:T(8,128)(2,1)}, u32[]{:S(2)}, u32[]{:S(2)}) collective-permute-start(bf16[320,4096]{1,0:T(8,128)(2,1)} %multiply_convert_fusion.refs_0_), channel_id=1, source_target_pairs={{0,2},{1,3},{2,0},{3,1},{4,6},{5,7},{6,4},{7,5},{8,10},{9,11},{10,... | collective-permute-start | bytes 7864328 | tf_op jit(solution)/shard_map/ppermute | solution.py:439
  937.1 98.1 %collective-permute-start.61 = (bf16[320,4096]{1,0:T(8,128)(2,1)}, bf16[320,4096]{1,0:T(8,128)(2,1)}, u32[]{:S(2)}, u32[]{:S(2)}) collective-permute-start(bf16[320,4096]{1,0:T(8,128)(2,1)} %get-tuple-element.558), channel_id=1, source_target_pairs={{0,2},{1,3},{2,0},{3,1},{4,6},{5,7},{6,4},{7,5},{8,10},{9,11},{10,... | collective-permute-start | bytes 7864328 | tf_op jit(solution)/shard_map/ppermute | solution.py:439
  938.6 96.6 %collective-permute-start.64 = (bf16[2048,512]{1,0:T(8,128)(2,1)}, bf16[2048,512]{1,0:T(8,128)(2,1)}, u32[]{:S(2)}, u32[]{:S(2)}) collective-permute-start(bf16[2048,512]{1,0:T(8,128)(2,1)} %get-tuple-element.385), channel_id=1, source_target_pairs={{0,4},{4,0},{8,12},{12,8},{16,20},{20,16},{24,28},{28,24},{1,5},{5... | collective-permute-start | bytes 6291464 | tf_op jit(solution)/shard_map/ppermute | solution.py:439
  939.5 95.8 %collective-permute-start.65 = (bf16[2048,512]{1,0:T(8,128)(2,1)}, bf16[2048,512]{1,0:T(8,128)(2,1)}, u32[]{:S(2)}, u32[]{:S(2)}) collective-permute-start(bf16[2048,512]{1,0:T(8,128)(2,1)} %get-tuple-element.386), channel_id=1, source_target_pairs={{0,4},{4,0},{8,12},{12,8},{16,20},{20,16},{24,28},{28,24},{1,5},{5... | collective-permute-start | bytes 6291464 | tf_op jit(solution)/shard_map/ppermute | solution.py:439
  942.7 92.5 %collective-permute-start.63 = (bf16[1024,512]{1,0:T(8,128)(2,1)}, bf16[1024,512]{1,0:T(8,128)(2,1)}, u32[]{:S(2)}, u32[]{:S(2)}) collective-permute-start(bf16[1024,512]{1,0:T(8,128)(2,1)} %get-tuple-element.384), channel_id=1, source_target_pairs={{0,16},{4,20},{8,24},{12,28},{16,0},{20,4},{24,8},{28,12},{1,17},{... | collective-permute-start | bytes 3145736 | tf_op jit(solution)/shard_map/ppermute | solution.py:439
  1039.8 82.2 %collective-permute-start.68 = (bf16[320,4096]{1,0:T(8,128)(2,1)}, bf16[320,4096]{1,0:T(8,128)(2,1)}, u32[]{:S(2)}, u32[]{:S(2)}) collective-permute-start(bf16[320,4096]{1,0:T(8,128)(2,1)} %add_convert_fusion.11), channel_id=1, source_target_pairs={{0,8},{4,12},{8,0},{12,4},{16,24},{20,28},{24,16},{28,20},{1,9},{5... | collective-permute-start | bytes 7864328 | tf_op jit(solution)/shard_map/ppermute | solution.py:439
  1133.6 81.1 %collective-permute-start.73 = (bf16[320,4096]{1,0:T(8,128)(2,1)S(1)}, bf16[320,4096]{1,0:T(8,128)(2,1)S(1)}, u32[]{:S(2)}, u32[]{:S(2)}) collective-permute-start(bf16[320,4096]{1,0:T(8,128)(2,1)S(1)} %get-tuple-element.412.refs_0_.refs_2_), channel_id=1, source_target_pairs={{0,8},{4,12},{8,0},{12,4},{16,24},{20,28},{24,16},{28,20},{1,9},{5... | collective-permute-start | bytes 7864328 | tf_op jit(solution)/shard_map/ppermute | solution.py:439
  1134.1 80.6 %collective-permute-start.72 = (bf16[320,4096]{1,0:T(8,128)(2,1)S(1)}, bf16[320,4096]{1,0:T(8,128)(2,1)S(1)}, u32[]{:S(2)}, u32[]{:S(2)}) collective-permute-start(bf16[320,4096]{1,0:T(8,128)(2,1)S(1)} %get-tuple-element.412.refs_0_.refs_2_), channel_id=1, source_target_pairs={{0,2},{1,3},{2,0},{3,1},{4,6},{5,7},{6,4},{7,5},{8,10},{9,11},{10,... | collective-permute-start | bytes 7864328 | tf_op jit(solution)/shard_map/ppermute | solution.py:439
  1134.6 80.1 %collective-permute-start.71 = (bf16[320,4096]{1,0:T(8,128)(2,1)S(1)}, bf16[320,4096]{1,0:T(8,128)(2,1)}, u32[]{:S(2)}, u32[]{:S(2)}) collective-permute-start(bf16[320,4096]{1,0:T(8,128)(2,1)S(1)} %get-tuple-element.412.refs_0_.refs_2_), channel_id=1, source_target_pairs={{0,1},{1,0},{2,3},{3,2},{4,5},{5,4},{6,7},{7,6},{8,9},{9,8},{10,11... | collective-permute-start | bytes 7864328 | tf_op jit(solution)/shard_map/ppermute | solution.py:439
  1134.6 78.4 %collective-permute-start.75 = (bf16[512,2048]{1,0:T(8,128)(2,1)}, bf16[512,2048]{1,0:T(8,128)(2,1)}, u32[]{:S(2)}, u32[]{:S(2)}) collective-permute-start(bf16[512,2048]{1,0:T(8,128)(2,1)} %get-tuple-element.415), channel_id=1, source_target_pairs={{0,4},{4,0},{8,12},{12,8},{16,20},{20,16},{24,28},{28,24},{1,5},{5... | collective-permute-start | bytes 6291464 | tf_op jit(solution)/shard_map/ppermute | solution.py:439
  1342.3 79.1 %collective-permute-start.88 = (bf16[320,4096]{1,0:T(8,128)(2,1)}, bf16[320,4096]{1,0:T(8,128)(2,1)}, u32[]{:S(2)}, u32[]{:S(2)}) collective-permute-start(bf16[320,4096]{1,0:T(8,128)(2,1)} %get-tuple-element.443), channel_id=1, source_target_pairs={{0,2},{1,3},{2,0},{3,1},{4,6},{5,7},{6,4},{7,5},{8,10},{9,11},{10,... | collective-permute-start | bytes 7864328 | tf_op jit(solution)/shard_map/ppermute | solution.py:439
  1343.0 80.6 %collective-permute-start.89 = (bf16[320,4096]{1,0:T(8,128)(2,1)S(1)}, bf16[320,4096]{1,0:T(8,128)(2,1)}, u32[]{:S(2)}, u32[]{:S(2)}) collective-permute-start(bf16[320,4096]{1,0:T(8,128)(2,1)S(1)} %add_convert_fusion.6), channel_id=1, source_target_pairs={{0,8},{4,12},{8,0},{12,4},{16,24},{20,28},{24,16},{28,20},{1,9},{5... | collective-permute-start | bytes 7864328 | tf_op jit(solution)/shard_map/ppermute | solution.py:439
  1343.0 78.4 %collective-permute-start.91 = (bf16[512,2048]{1,0:T(8,128)(2,1)}, bf16[512,2048]{1,0:T(8,128)(2,1)}, u32[]{:S(2)}, u32[]{:S(2)}) collective-permute-start(bf16[512,2048]{1,0:T(8,128)(2,1)} %get-tuple-element.448), channel_id=1, source_target_pairs={{0,4},{4,0},{8,12},{12,8},{16,20},{20,16},{24,28},{28,24},{1,5},{5... | collective-permute-start | bytes 6291464 | tf_op jit(solution)/shard_map/ppermute | solution.py:439
  1580.4 93.3 %collective-permute-start.103 = (bf16[320,4096]{1,0:T(8,128)(2,1)}, bf16[320,4096]{1,0:T(8,128)(2,1)}, u32[]{:S(2)}, u32[]{:S(2)}) collective-permute-start(bf16[320,4096]{1,0:T(8,128)(2,1)} %add_convert_fusion), channel_id=1, source_target_pairs={{0,8},{4,12},{8,0},{12,4},{16,24},{20,28},{24,16},{28,20},{1,9},{5... | collective-permute-start | bytes 7864328 | tf_op jit(solution)/shard_map/ppermute | solution.py:439
  1588.1 85.5 %collective-permute-start.102 = (bf16[320,4096]{1,0:T(8,128)(2,1)}, bf16[320,4096]{1,0:T(8,128)(2,1)}, u32[]{:S(2)}, u32[]{:S(2)}) collective-permute-start(bf16[320,4096]{1,0:T(8,128)(2,1)} %get-tuple-element.541), channel_id=1, source_target_pairs={{0,2},{1,3},{2,0},{3,1},{4,6},{5,7},{6,4},{7,5},{8,10},{9,11},{10,... | collective-permute-start | bytes 7864328 | tf_op jit(solution)/shard_map/ppermute | solution.py:439
  1591.8 79.6 %collective-permute-start.104 = (bf16[512,1536]{1,0:T(8,128)(2,1)}, bf16[512,1536]{1,0:T(8,128)(2,1)}, u32[]{:S(2)}, u32[]{:S(2)}) collective-permute-start(bf16[512,1536]{1,0:T(8,128)(2,1)} %add_convert_fusion.23), channel_id=1, source_target_pairs={{0,16},{4,20},{8,24},{12,28},{16,0},{20,4},{24,8},{28,12},{1,17},{... | collective-permute-start | bytes 4718600 | tf_op jit(solution)/shard_map/ppermute | solution.py:439
  1591.8 79.6 %collective-permute-start.105 = (bf16[512,1536]{1,0:T(8,128)(2,1)}, bf16[512,1536]{1,0:T(8,128)(2,1)}, u32[]{:S(2)}, u32[]{:S(2)}) collective-permute-start(bf16[512,1536]{1,0:T(8,128)(2,1)} %get-tuple-element.494), channel_id=1, source_target_pairs={{0,4},{4,0},{8,12},{12,8},{16,20},{20,16},{24,28},{28,24},{1,5},{5... | collective-permute-start | bytes 4718600 | tf_op jit(solution)/shard_map/ppermute | solution.py:439
  1592.7 78.8 %collective-permute-start.106 = (bf16[512,1536]{1,0:T(8,128)(2,1)}, bf16[512,1536]{1,0:T(8,128)(2,1)}, u32[]{:S(2)}, u32[]{:S(2)}) collective-permute-start(bf16[512,1536]{1,0:T(8,128)(2,1)} %get-tuple-element.495), channel_id=1, source_target_pairs={{0,4},{4,0},{8,12},{12,8},{16,20},{20,16},{24,28},{28,24},{1,5},{5... | collective-permute-start | bytes 4718600 | tf_op jit(solution)/shard_map/ppermute | solution.py:439
  (170 other events, 6867.8 us)

commit v5 on v4

--- a/solution.py
+++ b/solution.py
@@ -620,17 +620,16 @@
         return [(v, 0, v.shape[0]) for v in pieces]
 
     w_qkv, at_qkv = qkv_w.blocks()
-    one_b = gather(az, ad)
-    one_b_far = move(pp_core, one_b)
+    one_b = (az, ad, move(pp_core, az), move(pp_core, ad))
     up_w.zh(0, 0, 2)
     out_w.y(0)
     out_w.yz(0)
     cx = move(pp_x, cot)
     cz_top = move(pp_zl, cot[:half])
-    one_b_rows = batch(one_b, one_b_far)
+    one_b_rows = batch(*one_b)
     one_a_rows = batch(one_a, one_a_far)
     qkv_a = run(lambda v: deep(batch(v, one_a_far), w_qkv, at_qkv, 0), one_a)
-    qkv_b = run(lambda v: deep(batch(one_b, v), w_qkv, at_qkv, 0), one_b_far)
+    qkv_b = run(lambda v: deep(batch(*one_b[:3], v), w_qkv, at_qkv, 0), one_b[3])
     close()
 
     def spec(cols):
@@ -751,6 +750,7 @@
     down_w.swap(1, 2)
     down_w.zh(1, 0, 2)
     cd_bottom = move(pp_x, cz_bottom)
+    cot_b_most = gather(cz_top, cz_bottom, cd_top)
     act_b, slope_b = run(lambda v: lift(*two_b[:3], v), ad_far)
     close()
 
@@ -828,17 +828,18 @@
         steps.pending.append(out)
         return out
 
-    near_cot_b = gather(cz_top, cz_bottom, cd_top, cd_bottom)
-    far_cot_b = move(pp_core, near_cot_b)
+    cot_b_parts = (cot_b_most, cd_bottom, move(pp_core, cot_b_most), move(pp_core, cd_bottom))
     down_g, up_g, out_g, qkv_g = Sum(1), Sum(0), Sum(1, True), Sum(0)
     down_w.zh(1, 1, 2)
     down_w.y(1)
-    cot_a, cot_b = batch(near_cot_a, far_cot_a), batch(near_cot_b, far_cot_b)
+    cot_a, cot_b = batch(near_cot_a, far_cot_a), batch(*cot_b_parts)
     acts = [[(act_a, 0, 2 * two)], [(act_b, 0, 2 * two)]]
     down_g.make(1, acts, [cot_a, cot_b])
     close()
     down_w.yz(1)
     down_g.make(0, acts, [cot_a, cot_b])
+    cot_b_near = gather(cot_b_parts[0], cot_b_parts[1])
+    cot_b_far = gather(cot_b_parts[2], cot_b_parts[3])
     close()
 
     w_down, at_down = down_w.blocks()
@@ -855,7 +856,7 @@
         )
 
     down_g.y_far(0)
-    du_b = run(lambda v: pull(cot_b, v), slope_b)
+    du_b = run(lambda v: pull(batch(cot_b_near, cot_b_far), v), slope_b)
     sums_b = run(broad, du_b, w_up, at_up, 1)
     close()
 

time: 1800 us -> 1800 us (level)
    ppermute x117 -> x119, waiting for transfers between devices: 715 us -> 702 us  [over(): return lambda v: lax.ppermute(v, axis, [(i, to(i)) for i in range(size)])]
    pallas_call x10 -> x11, Pallas kernels: 40.2 us -> 45 us  [stack_rows(): pl.pallas_call(body, out_shape=jax.ShapeDtypeStruct((sum(sizes) * rows, c...]
    ppermute x117 -> x119, starting transfers between devices: 104 us -> 102 us  [over(): return lambda v: lax.ppermute(v, axis, [(i, to(i)) for i in range(size)])]
  transfers between devices with their start and end apart: 117 -> 119, of which waited for: 56 -> 54; matrix products, arithmetic and copies ran while one was open for 10% -> 10% of each run, Pallas kernels for 39% -> 40%
where the time goes in v5:
time: 1800 us; the launch traced here: 1790 us
  Pallas kernels  731 us (41%)
  waiting for transfers between devices  702 us (39%)
  other arithmetic  199 us (11%)
  starting transfers between devices  102 us (6%)
  local copies, waits for them, and re-layouts  50.5 us (3%)
    ppermute x119, waiting for transfers between devices, over(): return lambda v: lax.ppermute(v, axis, [(i, to(i)) for i in range(size)])  702 us
    pallas_call x8, Pallas kernels, gram(): pl.pallas_call(body, out_shape=[jax.ShapeDtypeStruct((m, n), BF)] * count...  209 us
    pallas_call x8, Pallas kernels, deep(): pl.pallas_call(body, out_shape=[jax.ShapeDtypeStruct((m, n), BF)] * outs,...  203 us
    pallas_call x8, Pallas kernels, broad(): pl.pallas_call(body, out_shape=[jax.ShapeDtypeStruct((m // 2, n), BF)] *...  202 us
    ppermute x119, starting transfers between devices, over(): return lambda v: lax.ppermute(v, axis, [(i, to(i)) for i in range(size)])  102 us
    convert_element_type x23, other arithmetic, plus(): return sum((v.astype(F32) for v in terms)).astype(BF)  80.6 us
    pallas_call x11, Pallas kernels, stack_rows(): pl.pallas_call(body, out_shape=jax.ShapeDtypeStruct((sum(sizes) * rows, c...  45 us
    pallas_call x2, Pallas kernels, attend_back(): pl.pallas_call(attention_backward, out_shape=jax.ShapeDtypeStruct((2, 2,...  40.6 us
  transfers between devices with their start and end apart: 119, of which 54 were waited for; matrix products, arithmetic and copies ran while one was open for 10% of the time, Pallas kernels for 40%

profile of v5, /device:TPU:0, one launch (start us, length us, event | category | flops | bytes accessed | tf_op | source)
XLA Modules:
  0.0 1786.1 jit_solution(16220272893351577502)
XLA Ops:
  68.4 33.3 %collective-permute-done.4.refs_3_.refs_5_.rest_1_ = bf16[512,1536]{1,0:T(8,128)(2,1)} collective-permute-done((bf16[512,1536]{1,0:T(8,128)(2,1)}, bf16[512,1536]{1,0:T(8,128)(2,1)}, u32[]{:S(2)}, u32[]{:S(2)}) %collective-permute-start.4) | collective-permute-done | bytes 1572896 | tf_op jit(solution)/shard_map/ppermute | solution.py:439
  139.4 31.3 %collective-permute-done.8.refs_7_.refs_9_.rest_5_ = bf16[512,1536]{1,0:T(8,128)(2,1)} collective-permute-done((bf16[512,1536]{1,0:T(8,128)(2,1)}, bf16[512,1536]{1,0:T(8,128)(2,1)}, u32[]{:S(2)}, u32[]{:S(2)}) %collective-permute-start.8) | collective-permute-done | bytes 1572896 | tf_op jit(solution)/shard_map/ppermute | solution.py:439
  203.3 45.5 %collective-permute-done.15.rest_2_.refs_6_ = bf16[512,1024]{1,0:T(8,128)(2,1)} collective-permute-done((bf16[512,1024]{1,0:T(8,128)(2,1)}, bf16[512,1024]{1,0:T(8,128)(2,1)}, u32[]{:S(2)}, u32[]{:S(2)}) %collective-permute-start.15) | collective-permute-done | bytes 1048608 | tf_op jit(solution)/shard_map/ppermute | solution.py:439
  472.4 65.1 %collective-permute-done.38.refs_1_ = bf16[256,2048]{1,0:T(8,128)(2,1)S(1)} collective-permute-done((bf16[256,2048]{1,0:T(8,128)(2,1)}, bf16[256,2048]{1,0:T(8,128)(2,1)S(1)}, u32[]{:S(2)}, u32[]{:S(2)}) %collective-permute-start.38) | collective-permute-done | bytes 1048608 | tf_op jit(solution)/shard_map/ppermute | solution.py:439
  555.4 74.0 %collective-permute-done.43.refs_0_ = bf16[1024,512]{1,0:T(8,128)(2,1)S(1)} collective-permute-done((bf16[1024,512]{1,0:T(8,128)(2,1)}, bf16[1024,512]{1,0:T(8,128)(2,1)S(1)}, u32[]{:S(2)}, u32[]{:S(2)}) %collective-permute-start.43) | collective-permute-done | bytes 1048608 | tf_op jit(solution)/shard_map/ppermute | solution.py:439
  635.4 33.7 %deep.10 = (bf16[1280,2048]{1,0:T(8,128)(2,1)}, bf16[1280,2048]{1,0:T(8,128)(2,1)}) custom-call(s32[8]{0:T(128)} %stack.74.starts_ref, bf16[320,4096]{1,0:T(8,128)(2,1)} %multiply_convert_fusion.refs_0_, bf16[320,4096]{1,0:T(8,128)(2,1)} %collective-permute-done.40.refs_1_, bf16[320,4096]{1,0:T(8,128)(2,1)} %collective-permute-done.41.refs_2_, ...), custom_call_target="tpu_custom_call" | custom-call | flops 1073741824 | bytes 32505856 | tf_op jit(solution)/shard_map/deep/pallas_call | solution.py:251
  702.1 33.8 %deep.11 = (bf16[1280,2048]{1,0:T(8,128)(2,1)}, bf16[1280,2048]{1,0:T(8,128)(2,1)}) custom-call(s32[8]{0:T(128)} %stack.74.starts_ref, bf16[320,4096]{1,0:T(8,128)(2,1)} %collective-permute-done.42.refs_0_.refs_4_, bf16[320,4096]{1,0:T(8,128)(2,1)} %collective-permute-done.46.refs_1_.refs_5_, bf16[320,4096]{1,0:T(8,128)(2,1)} %collective-permute-done.50.refs_2_.refs_6_, ...), custom_call_target="tpu_custom_call" | custom-call | flops 1073741824 | bytes 32505856 | tf_op jit(solution)/shard_map/deep/pallas_call | solution.py:251
  753.9 32.2 %gram.8 = (bf16[2048,512]{1,0:T(8,128)(2,1)}, bf16[2048,512]{1,0:T(8,128)(2,1)}, bf16[2048,512]{1,0:T(8,128)(2,1)}, bf16[2048,512]{1,0:T(8,128)(2,1)}) custom-call(s32[4]{0:T(128)} %constant.155.clone.index_ref, bf16[1280,2048]{1,0:T(8,128)(2,1)} %get-tuple-element.415.refs_0_.a_ref, bf16[1280,2048]{1,0:T(8,128)(2,1)} %get-tuple-element.423.refs_1_.a_ref, ...), custom_call_target="tpu_custom_call" | custom-call | flops 1073741824 | bytes 29360128 | tf_op jit(solution)/shard_map/gram/pallas_call | solution.py:183
  813.3 32.2 %gram.9 = (bf16[2048,512]{1,0:T(8,128)(2,1)}, bf16[2048,512]{1,0:T(8,128)(2,1)}, bf16[2048,512]{1,0:T(8,128)(2,1)}, bf16[2048,512]{1,0:T(8,128)(2,1)}) custom-call(s32[4]{0:T(128)} %constant.156.clone.index_ref, bf16[1280,2048]{1,0:T(8,128)(2,1)} %get-tuple-element.415.refs_0_.a_ref, bf16[1280,2048]{1,0:T(8,128)(2,1)} %get-tuple-element.423.refs_1_.a_ref, ...), custom_call_target="tpu_custom_call" | custom-call | flops 1073741824 | bytes 29360128 | tf_op jit(solution)/shard_map/gram/pallas_call | solution.py:183
  850.5 31.0 %deep.12.a_ref.refs_9_ = bf16[1280,2048]{1,0:T(8,128)(2,1)} custom-call(s32[8]{0:T(128)} %stack.74.starts_ref, bf16[640,4096]{1,0:T(8,128)(2,1)} %stack_rows.20.refs_0_, bf16[640,4096]{1,0:T(8,128)(2,1)} %stack_rows.21.refs_1_, bf16[2048,512]{1,0:T(8,128)(2,1)} %copy-done.3, bf16[2048,512]{1,0:T(8,128)(2,1)} %stack_rows.18.refs_3_.rest_1_, ...), custom_call_target="tpu_custom_call" | custom-call | flops 1073741824 | bytes 32505856 | tf_op jit(solution)/shard_map/deep/pallas_call | solution.py:251
  881.6 31.9 %broad.10 = (bf16[640,4096]{1,0:T(8,128)(2,1)}, bf16[640,4096]{1,0:T(8,128)(2,1)}) custom-call(s32[8]{0:T(128)} %stack.74.starts_ref, bf16[1280,2048]{1,0:T(8,128)(2,1)} %deep.12.a_ref.refs_9_, bf16[512,2048]{1,0:T(8,128)(2,1)} %get-tuple-element.306.refs_4_.rest_0_, bf16[512,2048]{1,0:T(8,128)(2,1)} %stack_rows.14.refs_5_.rest_1_, ...), custom_call_target="tpu_custom_call" | custom-call | flops 1073741824 | bytes 32505856 | tf_op jit(solution)/shard_map/broad/pallas_call | solution.py:286
  937.2 30.7 %deep.13.a_ref.refs_8_ = bf16[1280,2048]{1,0:T(8,128)(2,1)} custom-call(s32[8]{0:T(128)} %stack.74.starts_ref, bf16[640,4096]{1,0:T(8,128)(2,1)} %stack_rows.12.refs_2_.refs_0_, bf16[640,4096]{1,0:T(8,128)(2,1)} %collective-permute-done.29.refs_3_.refs_1_, bf16[2048,512]{1,0:T(8,128)(2,1)} %copy-done.3, bf16[2048,512]{1,0:T(8,128)(2,1)} %stack_rows.18.refs_3_.rest_1_, ...), custom_call_target="tpu_custom_call" | custom-call | flops 1073741824 | bytes 32505856 | tf_op jit(solution)/shard_map/deep/pallas_call | solution.py:251
  968.0 31.9 %broad.11 = (bf16[640,4096]{1,0:T(8,128)(2,1)}, bf16[640,4096]{1,0:T(8,128)(2,1)}) custom-call(s32[8]{0:T(128)} %stack.74.starts_ref, bf16[1280,2048]{1,0:T(8,128)(2,1)} %deep.13.a_ref.refs_8_, bf16[512,2048]{1,0:T(8,128)(2,1)} %get-tuple-element.306.refs_4_.rest_0_, bf16[512,2048]{1,0:T(8,128)(2,1)} %stack_rows.14.refs_5_.rest_1_, ...), custom_call_target="tpu_custom_call" | custom-call | flops 1073741824 | bytes 32505856 | tf_op jit(solution)/shard_map/broad/pallas_call | solution.py:286
  1042.9 32.8 %gram.11 = (bf16[512,2048]{1,0:T(8,128)(2,1)}, bf16[512,2048]{1,0:T(8,128)(2,1)}, bf16[512,2048]{1,0:T(8,128)(2,1)}, bf16[512,2048]{1,0:T(8,128)(2,1)}) custom-call(s32[4]{0:T(128)} %constant.156.clone.index_ref, bf16[320,4096]{1,0:T(8,128)(2,1)} %multiply_convert_fusion.refs_0_, bf16[320,4096]{1,0:T(8,128)(2,1)} %collective-permute-done.40.refs_1_, ...), custom_call_target="tpu_custom_call" | custom-call | flops 1073741824 | bytes 52953088 | tf_op jit(solution)/shard_map/gram/pallas_call | solution.py:183
  1075.8 32.6 %gram.10 = (bf16[512,2048]{1,0:T(8,128)(2,1)}, bf16[512,2048]{1,0:T(8,128)(2,1)}, bf16[512,2048]{1,0:T(8,128)(2,1)}, bf16[512,2048]{1,0:T(8,128)(2,1)}) custom-call(s32[4]{0:T(128)} %constant.155.clone.index_ref, bf16[320,4096]{1,0:T(8,128)(2,1)} %multiply_convert_fusion.refs_0_, bf16[320,4096]{1,0:T(8,128)(2,1)} %collective-permute-done.40.refs_1_, ...), custom_call_target="tpu_custom_call" | custom-call | flops 1073741824 | bytes 52953088 | tf_op jit(solution)/shard_map/gram/pallas_call | solution.py:183
  1131.4 32.2 %broad.12 = (bf16[640,4096]{1,0:T(8,128)(2,1)}, bf16[640,4096]{1,0:T(8,128)(2,1)}) custom-call(s32[8]{0:T(128)} %stack.74.starts_ref, bf16[1280,2048]{1,0:T(8,128)(2,1)} %get-tuple-element.415.refs_0_.a_ref, bf16[2048,512]{1,0:T(8,128)(2,1)} %copy-done.3, bf16[2048,512]{1,0:T(8,128)(2,1)} %stack_rows.18.refs_3_.rest_1_, ...), custom_call_target="tpu_custom_call" | custom-call | flops 1073741824 | bytes 32505856 | tf_op jit(solution)/shard_map/broad/pallas_call | solution.py:286
  1163.6 32.2 %broad.13 = (bf16[640,4096]{1,0:T(8,128)(2,1)}, bf16[640,4096]{1,0:T(8,128)(2,1)}) custom-call(s32[8]{0:T(128)} %stack.74.starts_ref, bf16[1280,2048]{1,0:T(8,128)(2,1)} %get-tuple-element.423.refs_1_.a_ref, bf16[2048,512]{1,0:T(8,128)(2,1)} %copy-done.3, bf16[2048,512]{1,0:T(8,128)(2,1)} %stack_rows.18.refs_3_.rest_1_, ...), custom_call_target="tpu_custom_call" | custom-call | flops 1073741824 | bytes 32505856 | tf_op jit(solution)/shard_map/broad/pallas_call | solution.py:286
  1352.5 27.4 %gram.13 = (bf16[512,1536]{1,0:T(8,128)(2,1)}, bf16[512,1536]{1,0:T(8,128)(2,1)}, bf16[512,1536]{1,0:T(8,128)(2,1)}, bf16[512,1536]{1,0:T(8,128)(2,1)}) custom-call(s32[4]{0:T(128)} %constant.156.clone.index_ref, bf16[640,4096]{1,0:T(8,128)(2,1)} %stack_rows.11.refs_0_, bf16[640,4096]{1,0:T(8,128)(2,1)} %collective-permute-done.16.refs_1_, ...), custom_call_target="tpu_custom_call" | custom-call | flops 805306368 | bytes 40370176 | tf_op jit(solution)/shard_map/gram/pallas_call | solution.py:183
  1379.9 27.0 %gram.12 = (bf16[512,1536]{1,0:T(8,128)(2,1)}, bf16[512,1536]{1,0:T(8,128)(2,1)}, bf16[512,1536]{1,0:T(8,128)(2,1)}, bf16[512,1536]{1,0:T(8,128)(2,1)}) custom-call(s32[4]{0:T(128)} %constant.155.clone.index_ref, bf16[640,4096]{1,0:T(8,128)(2,1)} %stack_rows.11.refs_0_, bf16[640,4096]{1,0:T(8,128)(2,1)} %collective-permute-done.16.refs_1_, ...), custom_call_target="tpu_custom_call" | custom-call | flops 805306368 | bytes 40370176 | tf_op jit(solution)/shard_map/gram/pallas_call | solution.py:183
  1444.9 25.3 %broad.14 = (bf16[640,4096]{1,0:T(8,128)(2,1)}, bf16[640,4096]{1,0:T(8,128)(2,1)}) custom-call(s32[8]{0:T(128)} %stack.74.starts_ref, bf16[1280,1536]{1,0:T(8,128)(2,1)} %bitcast.46, bf16[512,1536]{1,0:T(8,128)(2,1)} %get-tuple-element.265.refs_2_.refs_4_.rest_0_, bf16[512,1536]{1,0:T(8,128)(2,1)} %collective-permute-done.4.refs_3_.refs_5_.rest_1_, ...), custom_call_target="tpu_custom_call" | custom-call | flops 805306368 | bytes 27000832 | tf_op jit(solution)/shard_map/broad/pallas_call | solution.py:286
  1499.1 25.2 %broad.15 = (bf16[640,4096]{1,0:T(8,128)(2,1)}, bf16[640,4096]{1,0:T(8,128)(2,1)}) custom-call(s32[8]{0:T(128)} %stack.74.starts_ref, bf16[1280,1536]{1,0:T(8,128)(2,1)} %bitcast.43, bf16[512,1536]{1,0:T(8,128)(2,1)} %get-tuple-element.265.refs_2_.refs_4_.rest_0_, bf16[512,1536]{1,0:T(8,128)(2,1)} %collective-permute-done.4.refs_3_.refs_5_.rest_1_, ...), custom_call_target="tpu_custom_call" | custom-call | flops 805306368 | bytes 27000832 | tf_op jit(solution)/shard_map/broad/pallas_call | solution.py:286
  1542.0 25.8 %collective-permute-done.100 = bf16[512,1536]{1,0:T(8,128)(2,1)} collective-permute-done((bf16[512,1536]{1,0:T(8,128)(2,1)}, bf16[512,1536]{1,0:T(8,128)(2,1)}, u32[]{:S(2)}, u32[]{:S(2)}) %collective-permute-start.100) | collective-permute-done | bytes 1572896 | tf_op jit(solution)/shard_map/ppermute | solution.py:439
  1590.3 73.0 %collective-permute-done.106 = bf16[512,1536]{1,0:T(8,128)(2,1)} collective-permute-done((bf16[512,1536]{1,0:T(8,128)(2,1)}, bf16[512,1536]{1,0:T(8,128)(2,1)}, u32[]{:S(2)}, u32[]{:S(2)}) %collective-permute-start.106) | collective-permute-done | bytes 1572896 | tf_op jit(solution)/shard_map/ppermute | solution.py:439
  1722.7 32.6 %collective-permute-done.115 = bf16[512,1536]{1,0:T(8,128)(2,1)S(1)} collective-permute-done((bf16[512,1536]{1,0:T(8,128)(2,1)S(1)}, bf16[512,1536]{1,0:T(8,128)(2,1)S(1)}, u32[]{:S(2)}, u32[]{:S(2)}) %collective-permute-start.115) | collective-permute-done | bytes 1572896 | tf_op jit(solution)/shard_map/ppermute | solution.py:439
  (561 shorter events, 911.1 us)
Async XLA Ops:
  19.0 82.7 %collective-permute-start.6 = (bf16[512,1536]{1,0:T(8,128)(2,1)}, bf16[512,1536]{1,0:T(8,128)(2,1)}, u32[]{:S(2)}, u32[]{:S(2)}) collective-permute-start(bf16[512,1536]{1,0:T(8,128)(2,1)} %get-tuple-element.265.refs_2_.refs_4_.rest_0_), channel_id=1, source_target_pairs={{0,16},{4,20},{8,24},{12,28},{16,0},{20,4},{24,8},{28,12},{1,17},{... | collective-permute-start | bytes 4718600 | tf_op jit(solution)/shard_map/ppermute | solution.py:439
  22.0 79.8 %collective-permute-start.5 = (bf16[512,1536]{1,0:T(8,128)(2,1)}, bf16[512,1536]{1,0:T(8,128)(2,1)}, u32[]{:S(2)}, u32[]{:S(2)}) collective-permute-start(bf16[512,1536]{1,0:T(8,128)(2,1)} %get-tuple-element.265.refs_2_.refs_4_.rest_0_), channel_id=1, source_target_pairs={{0,4},{4,0},{8,12},{12,8},{16,20},{20,16},{24,28},{28,24},{1,5},{5... | collective-permute-start | bytes 4718600 | tf_op jit(solution)/shard_map/ppermute | solution.py:439
  105.3 88.8 %collective-permute-start.11 = (bf16[320,4096]{1,0:T(8,128)(2,1)}, bf16[320,4096]{1,0:T(8,128)(2,1)}, u32[]{:S(2)}, u32[]{:S(2)}) collective-permute-start(bf16[320,4096]{1,0:T(8,128)(2,1)} %fusion.6.refs_0_), channel_id=1, source_target_pairs={{0,8},{4,12},{8,0},{12,4},{16,24},{20,28},{24,16},{28,20},{1,9},{5... | collective-permute-start | bytes 7864328 | tf_op jit(solution)/shard_map/ppermute | solution.py:439
  456.8 82.0 %collective-permute-start.37 = (bf16[320,4096]{1,0:T(8,128)(2,1)S(1)}, bf16[320,4096]{1,0:T(8,128)(2,1)S(1)}, u32[]{:S(2)}, u32[]{:S(2)}) collective-permute-start(bf16[320,4096]{1,0:T(8,128)(2,1)S(1)} %add_convert_fusion.16), channel_id=1, source_target_pairs={{0,8},{4,12},{8,0},{12,4},{16,24},{20,28},{24,16},{28,20},{1,9},{5... | collective-permute-start | bytes 7864328 | tf_op jit(solution)/shard_map/ppermute | solution.py:439
  548.3 81.9 %collective-permute-start.42 = (bf16[320,4096]{1,0:T(8,128)(2,1)}, bf16[320,4096]{1,0:T(8,128)(2,1)}, u32[]{:S(2)}, u32[]{:S(2)}) collective-permute-start(bf16[320,4096]{1,0:T(8,128)(2,1)} %multiply_convert_fusion.refs_0_), channel_id=1, source_target_pairs={{0,8},{4,12},{8,0},{12,4},{16,24},{20,28},{24,16},{28,20},{1,9},{5... | collective-permute-start | bytes 7864328 | tf_op jit(solution)/shard_map/ppermute | solution.py:439
  550.5 79.7 %collective-permute-start.41 = (bf16[320,4096]{1,0:T(8,128)(2,1)}, bf16[320,4096]{1,0:T(8,128)(2,1)}, u32[]{:S(2)}, u32[]{:S(2)}) collective-permute-start(bf16[320,4096]{1,0:T(8,128)(2,1)} %multiply_convert_fusion.refs_0_), channel_id=1, source_target_pairs={{0,1},{1,0},{2,3},{3,2},{4,5},{5,4},{6,7},{7,6},{8,9},{9,8},{10,11... | collective-permute-start | bytes 7864328 | tf_op jit(solution)/shard_map/ppermute | solution.py:439
  550.5 79.7 %collective-permute-start.40 = (bf16[320,4096]{1,0:T(8,128)(2,1)}, bf16[320,4096]{1,0:T(8,128)(2,1)}, u32[]{:S(2)}, u32[]{:S(2)}) collective-permute-start(bf16[320,4096]{1,0:T(8,128)(2,1)} %multiply_convert_fusion.refs_0_), channel_id=1, source_target_pairs={{0,2},{1,3},{2,0},{3,1},{4,6},{5,7},{6,4},{7,5},{8,10},{9,11},{10,... | collective-permute-start | bytes 7864328 | tf_op jit(solution)/shard_map/ppermute | solution.py:439
  927.4 99.5 %collective-permute-start.63 = (bf16[320,4096]{1,0:T(8,128)(2,1)}, bf16[320,4096]{1,0:T(8,128)(2,1)}, u32[]{:S(2)}, u32[]{:S(2)}) collective-permute-start(bf16[320,4096]{1,0:T(8,128)(2,1)} %get-tuple-element.564), channel_id=1, source_target_pairs={{0,2},{1,3},{2,0},{3,1},{4,6},{5,7},{6,4},{7,5},{8,10},{9,11},{10,... | collective-permute-start | bytes 7864328 | tf_op jit(solution)/shard_map/ppermute | solution.py:439
  928.8 98.1 %collective-permute-start.66 = (bf16[2048,512]{1,0:T(8,128)(2,1)}, bf16[2048,512]{1,0:T(8,128)(2,1)}, u32[]{:S(2)}, u32[]{:S(2)}) collective-permute-start(bf16[2048,512]{1,0:T(8,128)(2,1)} %get-tuple-element.391), channel_id=1, source_target_pairs={{0,4},{4,0},{8,12},{12,8},{16,20},{20,16},{24,28},{28,24},{1,5},{5... | collective-permute-start | bytes 6291464 | tf_op jit(solution)/shard_map/ppermute | solution.py:439
  929.4 97.4 %collective-permute-start.67 = (bf16[2048,512]{1,0:T(8,128)(2,1)}, bf16[2048,512]{1,0:T(8,128)(2,1)}, u32[]{:S(2)}, u32[]{:S(2)}) collective-permute-start(bf16[2048,512]{1,0:T(8,128)(2,1)} %get-tuple-element.392), channel_id=1, source_target_pairs={{0,4},{4,0},{8,12},{12,8},{16,20},{20,16},{24,28},{28,24},{1,5},{5... | collective-permute-start | bytes 6291464 | tf_op jit(solution)/shard_map/ppermute | solution.py:439
  934.3 92.5 %collective-permute-start.65 = (bf16[1024,512]{1,0:T(8,128)(2,1)}, bf16[1024,512]{1,0:T(8,128)(2,1)}, u32[]{:S(2)}, u32[]{:S(2)}) collective-permute-start(bf16[1024,512]{1,0:T(8,128)(2,1)} %get-tuple-element.390), channel_id=1, source_target_pairs={{0,16},{4,20},{8,24},{12,28},{16,0},{20,4},{24,8},{28,12},{1,17},{... | collective-permute-start | bytes 3145736 | tf_op jit(solution)/shard_map/ppermute | solution.py:439
  1031.5 82.2 %collective-permute-start.70 = (bf16[320,4096]{1,0:T(8,128)(2,1)}, bf16[320,4096]{1,0:T(8,128)(2,1)}, u32[]{:S(2)}, u32[]{:S(2)}) collective-permute-start(bf16[320,4096]{1,0:T(8,128)(2,1)} %add_convert_fusion.11), channel_id=1, source_target_pairs={{0,8},{4,12},{8,0},{12,4},{16,24},{20,28},{24,16},{28,20},{1,9},{5... | collective-permute-start | bytes 7864328 | tf_op jit(solution)/shard_map/ppermute | solution.py:439
  1125.4 81.1 %collective-permute-start.75 = (bf16[320,4096]{1,0:T(8,128)(2,1)S(1)}, bf16[320,4096]{1,0:T(8,128)(2,1)S(1)}, u32[]{:S(2)}, u32[]{:S(2)}) collective-permute-start(bf16[320,4096]{1,0:T(8,128)(2,1)S(1)} %get-tuple-element.418.refs_0_.refs_2_), channel_id=1, source_target_pairs={{0,8},{4,12},{8,0},{12,4},{16,24},{20,28},{24,16},{28,20},{1,9},{5... | collective-permute-start | bytes 7864328 | tf_op jit(solution)/shard_map/ppermute | solution.py:439
  1125.9 80.6 %collective-permute-start.74 = (bf16[320,4096]{1,0:T(8,128)(2,1)S(1)}, bf16[320,4096]{1,0:T(8,128)(2,1)S(1)}, u32[]{:S(2)}, u32[]{:S(2)}) collective-permute-start(bf16[320,4096]{1,0:T(8,128)(2,1)S(1)} %get-tuple-element.418.refs_0_.refs_2_), channel_id=1, source_target_pairs={{0,2},{1,3},{2,0},{3,1},{4,6},{5,7},{6,4},{7,5},{8,10},{9,11},{10,... | collective-permute-start | bytes 7864328 | tf_op jit(solution)/shard_map/ppermute | solution.py:439
  1126.5 80.0 %collective-permute-start.73 = (bf16[320,4096]{1,0:T(8,128)(2,1)S(1)}, bf16[320,4096]{1,0:T(8,128)(2,1)}, u32[]{:S(2)}, u32[]{:S(2)}) collective-permute-start(bf16[320,4096]{1,0:T(8,128)(2,1)S(1)} %get-tuple-element.418.refs_0_.refs_2_), channel_id=1, source_target_pairs={{0,1},{1,0},{2,3},{3,2},{4,5},{5,4},{6,7},{7,6},{8,9},{9,8},{10,11... | collective-permute-start | bytes 7864328 | tf_op jit(solution)/shard_map/ppermute | solution.py:439
  1126.5 78.3 %collective-permute-start.77 = (bf16[512,2048]{1,0:T(8,128)(2,1)}, bf16[512,2048]{1,0:T(8,128)(2,1)}, u32[]{:S(2)}, u32[]{:S(2)}) collective-permute-start(bf16[512,2048]{1,0:T(8,128)(2,1)} %get-tuple-element.421), channel_id=1, source_target_pairs={{0,4},{4,0},{8,12},{12,8},{16,20},{20,16},{24,28},{28,24},{1,5},{5... | collective-permute-start | bytes 6291464 | tf_op jit(solution)/shard_map/ppermute | solution.py:439
  1334.1 79.1 %collective-permute-start.90 = (bf16[320,4096]{1,0:T(8,128)(2,1)}, bf16[320,4096]{1,0:T(8,128)(2,1)}, u32[]{:S(2)}, u32[]{:S(2)}) collective-permute-start(bf16[320,4096]{1,0:T(8,128)(2,1)} %get-tuple-element.449), channel_id=1, source_target_pairs={{0,2},{1,3},{2,0},{3,1},{4,6},{5,7},{6,4},{7,5},{8,10},{9,11},{10,... | collective-permute-start | bytes 7864328 | tf_op jit(solution)/shard_map/ppermute | solution.py:439
  1334.8 80.6 %collective-permute-start.91 = (bf16[320,4096]{1,0:T(8,128)(2,1)S(1)}, bf16[320,4096]{1,0:T(8,128)(2,1)}, u32[]{:S(2)}, u32[]{:S(2)}) collective-permute-start(bf16[320,4096]{1,0:T(8,128)(2,1)S(1)} %add_convert_fusion.6), channel_id=1, source_target_pairs={{0,8},{4,12},{8,0},{12,4},{16,24},{20,28},{24,16},{28,20},{1,9},{5... | collective-permute-start | bytes 7864328 | tf_op jit(solution)/shard_map/ppermute | solution.py:439
  1334.8 78.4 %collective-permute-start.93 = (bf16[512,2048]{1,0:T(8,128)(2,1)}, bf16[512,2048]{1,0:T(8,128)(2,1)}, u32[]{:S(2)}, u32[]{:S(2)}) collective-permute-start(bf16[512,2048]{1,0:T(8,128)(2,1)} %get-tuple-element.454), channel_id=1, source_target_pairs={{0,4},{4,0},{8,12},{12,8},{16,20},{20,16},{24,28},{28,24},{1,5},{5... | collective-permute-start | bytes 6291464 | tf_op jit(solution)/shard_map/ppermute | solution.py:439
  1572.1 93.3 %collective-permute-start.105 = (bf16[320,4096]{1,0:T(8,128)(2,1)}, bf16[320,4096]{1,0:T(8,128)(2,1)}, u32[]{:S(2)}, u32[]{:S(2)}) collective-permute-start(bf16[320,4096]{1,0:T(8,128)(2,1)} %add_convert_fusion), channel_id=1, source_target_pairs={{0,8},{4,12},{8,0},{12,4},{16,24},{20,28},{24,16},{28,20},{1,9},{5... | collective-permute-start | bytes 7864328 | tf_op jit(solution)/shard_map/ppermute | solution.py:439
  1579.9 85.5 %collective-permute-start.104 = (bf16[320,4096]{1,0:T(8,128)(2,1)}, bf16[320,4096]{1,0:T(8,128)(2,1)}, u32[]{:S(2)}, u32[]{:S(2)}) collective-permute-start(bf16[320,4096]{1,0:T(8,128)(2,1)} %get-tuple-element.547), channel_id=1, source_target_pairs={{0,2},{1,3},{2,0},{3,1},{4,6},{5,7},{6,4},{7,5},{8,10},{9,11},{10,... | collective-permute-start | bytes 7864328 | tf_op jit(solution)/shard_map/ppermute | solution.py:439
  1583.6 79.6 %collective-permute-start.106 = (bf16[512,1536]{1,0:T(8,128)(2,1)}, bf16[512,1536]{1,0:T(8,128)(2,1)}, u32[]{:S(2)}, u32[]{:S(2)}) collective-permute-start(bf16[512,1536]{1,0:T(8,128)(2,1)} %add_convert_fusion.23), channel_id=1, source_target_pairs={{0,16},{4,20},{8,24},{12,28},{16,0},{20,4},{24,8},{28,12},{1,17},{... | collective-permute-start | bytes 4718600 | tf_op jit(solution)/shard_map/ppermute | solution.py:439
  1583.6 79.6 %collective-permute-start.107 = (bf16[512,1536]{1,0:T(8,128)(2,1)}, bf16[512,1536]{1,0:T(8,128)(2,1)}, u32[]{:S(2)}, u32[]{:S(2)}) collective-permute-start(bf16[512,1536]{1,0:T(8,128)(2,1)} %get-tuple-element.500), channel_id=1, source_target_pairs={{0,4},{4,0},{8,12},{12,8},{16,20},{20,16},{24,28},{28,24},{1,5},{5... | collective-permute-start | bytes 4718600 | tf_op jit(solution)/shard_map/ppermute | solution.py:439
  1584.3 79.0 %collective-permute-start.108 = (bf16[512,1536]{1,0:T(8,128)(2,1)}, bf16[512,1536]{1,0:T(8,128)(2,1)}, u32[]{:S(2)}, u32[]{:S(2)}) collective-permute-start(bf16[512,1536]{1,0:T(8,128)(2,1)} %get-tuple-element.501), channel_id=1, source_target_pairs={{0,4},{4,0},{8,12},{12,8},{16,20},{20,16},{24,28},{28,24},{1,5},{5... | collective-permute-start | bytes 4718600 | tf_op jit(solution)/shard_map/ppermute | solution.py:439
  (172 other events, 6875.6 us)

commit v6 on v5

--- a/solution.py
+++ b/solution.py
@@ -697,9 +697,6 @@
     up_w.y(0)
     cz_bottom = move(pp_zl, cot[half:])
     cd_top = move(pp_x, cz_top)
-    near_cot_a = gather(cot, cx)
-    far_cot_a = pp_core(near_cot_a)
-    steps.pending.append(far_cot_a)
     close()
 
     ez, ed = core_sum(*sums_b)
@@ -718,6 +715,7 @@
     from_z = move(pp_zl, plus(steps.begin(ez), from_d))
     up_w.zh(1, 1, 2)
     up_w.y(1)
+    near_cot_a = gather(cot, cx)
     close()
 
     resid = x + (steps.begin(e00).astype(F32) + from_x.astype(F32) + from_z.astype(F32))
@@ -741,6 +739,7 @@
     down_w.zh(0, 1, 2)
     down_w.y(0)
     down_w.swap(0, 2)
+    far_cot_a = move(pp_core, near_cot_a)
     act_a, slope_a = run(lambda v: lift(a_two, ax, a_two_far, v), ax_far)
     close()
 

time: 1800 us -> 1790 us (level)
  transfers between devices with their start and end apart: 119 -> 119, of which waited for: 54 -> 55; matrix products, arithmetic and copies ran while one was open for 10% -> 10% of each run, Pallas kernels for 40% -> 41%
where the time goes in v6:
time: 1790 us; the launch traced here: 1780 us
  Pallas kernels  730 us (41%)
  waiting for transfers between devices  695 us (39%)
  other arithmetic  201 us (11%)
  starting transfers between devices  103 us (6%)
  local copies, waits for them, and re-layouts  50.7 us (3%)
    ppermute x119, waiting for transfers between devices, over(): return lambda v: lax.ppermute(v, axis, [(i, to(i)) for i in range(size)])  695 us
    pallas_call x8, Pallas kernels, gram(): pl.pallas_call(body, out_shape=[jax.ShapeDtypeStruct((m, n), BF)] * count...  208 us
    pallas_call x8, Pallas kernels, deep(): pl.pallas_call(body, out_shape=[jax.ShapeDtypeStruct((m, n), BF)] * outs,...  203 us
    pallas_call x8, Pallas kernels, broad(): pl.pallas_call(body, out_shape=[jax.ShapeDtypeStruct((m // 2, n), BF)] *...  203 us
    ppermute x119, starting transfers between devices, over(): return lambda v: lax.ppermute(v, axis, [(i, to(i)) for i in range(size)])  103 us
    convert_element_type x23, other arithmetic, plus(): return sum((v.astype(F32) for v in terms)).astype(BF)  82.2 us
    pallas_call x11, Pallas kernels, stack_rows(): pl.pallas_call(body, out_shape=jax.ShapeDtypeStruct((sum(sizes) * rows, c...  44.8 us
    pallas_call x2, Pallas kernels, attend_back(): pl.pallas_call(attention_backward, out_shape=jax.ShapeDtypeStruct((2, 2,...  40.6 us
  transfers between devices with their start and end apart: 119, of which 55 were waited for; matrix products, arithmetic and copies ran while one was open for 10% of the time, Pallas kernels for 41%

profile of v6, /device:TPU:0, one launch (start us, length us, event | category | flops | bytes accessed | tf_op | source)
XLA Modules:
  0.0 1782.0 jit_solution(18208345297057355216)
XLA Ops:
  68.4 33.3 %collective-permute-done.4.refs_3_.refs_5_.rest_1_ = bf16[512,1536]{1,0:T(8,128)(2,1)} collective-permute-done((bf16[512,1536]{1,0:T(8,128)(2,1)}, bf16[512,1536]{1,0:T(8,128)(2,1)}, u32[]{:S(2)}, u32[]{:S(2)}) %collective-permute-start.4) | collective-permute-done | bytes 1572896 | tf_op jit(solution)/shard_map/ppermute | solution.py:439
  139.4 31.3 %collective-permute-done.8.refs_7_.refs_9_.rest_5_ = bf16[512,1536]{1,0:T(8,128)(2,1)} collective-permute-done((bf16[512,1536]{1,0:T(8,128)(2,1)}, bf16[512,1536]{1,0:T(8,128)(2,1)}, u32[]{:S(2)}, u32[]{:S(2)}) %collective-permute-start.8) | collective-permute-done | bytes 1572896 | tf_op jit(solution)/shard_map/ppermute | solution.py:439
  203.3 45.5 %collective-permute-done.15.rest_2_.refs_6_ = bf16[512,1024]{1,0:T(8,128)(2,1)} collective-permute-done((bf16[512,1024]{1,0:T(8,128)(2,1)}, bf16[512,1024]{1,0:T(8,128)(2,1)}, u32[]{:S(2)}, u32[]{:S(2)}) %collective-permute-start.15) | collective-permute-done | bytes 1048608 | tf_op jit(solution)/shard_map/ppermute | solution.py:439
  471.4 62.0 %collective-permute-done.37.refs_1_ = bf16[256,2048]{1,0:T(8,128)(2,1)} collective-permute-done((bf16[256,2048]{1,0:T(8,128)(2,1)}, bf16[256,2048]{1,0:T(8,128)(2,1)}, u32[]{:S(2)}, u32[]{:S(2)}) %collective-permute-start.37) | collective-permute-done | bytes 1048608 | tf_op jit(solution)/shard_map/ppermute | solution.py:439
  551.1 74.1 %collective-permute-done.42.refs_0_ = bf16[1024,512]{1,0:T(8,128)(2,1)S(1)} collective-permute-done((bf16[1024,512]{1,0:T(8,128)(2,1)}, bf16[1024,512]{1,0:T(8,128)(2,1)S(1)}, u32[]{:S(2)}, u32[]{:S(2)}) %collective-permute-start.42) | collective-permute-done | bytes 1048608 | tf_op jit(solution)/shard_map/ppermute | solution.py:439
  641.1 33.7 %deep.10 = (bf16[1280,2048]{1,0:T(8,128)(2,1)}, bf16[1280,2048]{1,0:T(8,128)(2,1)}) custom-call(s32[8]{0:T(128)} %stack.74.starts_ref, bf16[320,4096]{1,0:T(8,128)(2,1)} %multiply_convert_fusion.refs_0_, bf16[320,4096]{1,0:T(8,128)(2,1)} %collective-permute-done.39.refs_1_, bf16[320,4096]{1,0:T(8,128)(2,1)} %collective-permute-done.40.refs_2_, ...), custom_call_target="tpu_custom_call" | custom-call | flops 1073741824 | bytes 32505856 | tf_op jit(solution)/shard_map/deep/pallas_call | solution.py:251
  697.9 33.8 %deep.11 = (bf16[1280,2048]{1,0:T(8,128)(2,1)}, bf16[1280,2048]{1,0:T(8,128)(2,1)}) custom-call(s32[8]{0:T(128)} %stack.74.starts_ref, bf16[320,4096]{1,0:T(8,128)(2,1)} %collective-permute-done.41.refs_0_.refs_4_, bf16[320,4096]{1,0:T(8,128)(2,1)} %collective-permute-done.45.refs_1_.refs_5_, bf16[320,4096]{1,0:T(8,128)(2,1)} %collective-permute-done.50.refs_2_.refs_6_, ...), custom_call_target="tpu_custom_call" | custom-call | flops 1073741824 | bytes 32505856 | tf_op jit(solution)/shard_map/deep/pallas_call | solution.py:251
  749.7 32.1 %gram.8 = (bf16[2048,512]{1,0:T(8,128)(2,1)}, bf16[2048,512]{1,0:T(8,128)(2,1)}, bf16[2048,512]{1,0:T(8,128)(2,1)}, bf16[2048,512]{1,0:T(8,128)(2,1)}) custom-call(s32[4]{0:T(128)} %constant.155.clone.index_ref, bf16[1280,2048]{1,0:T(8,128)(2,1)} %get-tuple-element.417.refs_0_.a_ref, bf16[1280,2048]{1,0:T(8,128)(2,1)} %get-tuple-element.425.refs_1_.a_ref, ...), custom_call_target="tpu_custom_call" | custom-call | flops 1073741824 | bytes 29360128 | tf_op jit(solution)/shard_map/gram/pallas_call | solution.py:183
  809.0 32.1 %gram.9 = (bf16[2048,512]{1,0:T(8,128)(2,1)}, bf16[2048,512]{1,0:T(8,128)(2,1)}, bf16[2048,512]{1,0:T(8,128)(2,1)}, bf16[2048,512]{1,0:T(8,128)(2,1)}) custom-call(s32[4]{0:T(128)} %constant.156.clone.index_ref, bf16[1280,2048]{1,0:T(8,128)(2,1)} %get-tuple-element.417.refs_0_.a_ref, bf16[1280,2048]{1,0:T(8,128)(2,1)} %get-tuple-element.425.refs_1_.a_ref, ...), custom_call_target="tpu_custom_call" | custom-call | flops 1073741824 | bytes 29360128 | tf_op jit(solution)/shard_map/gram/pallas_call | solution.py:183
  846.2 31.1 %deep.12.a_ref.refs_9_ = bf16[1280,2048]{1,0:T(8,128)(2,1)} custom-call(s32[8]{0:T(128)} %stack.74.starts_ref, bf16[640,4096]{1,0:T(8,128)(2,1)} %stack_rows.20.refs_0_, bf16[640,4096]{1,0:T(8,128)(2,1)} %stack_rows.21.refs_1_, bf16[2048,512]{1,0:T(8,128)(2,1)} %copy-done.3, bf16[2048,512]{1,0:T(8,128)(2,1)} %stack_rows.18.refs_3_.rest_1_, ...), custom_call_target="tpu_custom_call" | custom-call | flops 1073741824 | bytes 32505856 | tf_op jit(solution)/shard_map/deep/pallas_call | solution.py:251
  877.4 31.9 %broad.10 = (bf16[640,4096]{1,0:T(8,128)(2,1)}, bf16[640,4096]{1,0:T(8,128)(2,1)}) custom-call(s32[8]{0:T(128)} %stack.74.starts_ref, bf16[1280,2048]{1,0:T(8,128)(2,1)} %deep.12.a_ref.refs_9_, bf16[512,2048]{1,0:T(8,128)(2,1)} %get-tuple-element.307.refs_4_.rest_0_, bf16[512,2048]{1,0:T(8,128)(2,1)} %stack_rows.13.refs_5_.rest_1_, ...), custom_call_target="tpu_custom_call" | custom-call | flops 1073741824 | bytes 32505856 | tf_op jit(solution)/shard_map/broad/pallas_call | solution.py:286
  933.1 30.7 %deep.13.a_ref.refs_8_ = bf16[1280,2048]{1,0:T(8,128)(2,1)} custom-call(s32[8]{0:T(128)} %stack.74.starts_ref, bf16[640,4096]{1,0:T(8,128)(2,1)} %stack_rows.14.refs_2_.refs_0_, bf16[640,4096]{1,0:T(8,128)(2,1)} %collective-permute-done.49.refs_3_.refs_1_, bf16[2048,512]{1,0:T(8,128)(2,1)} %copy-done.3, bf16[2048,512]{1,0:T(8,128)(2,1)} %stack_rows.18.refs_3_.rest_1_, ...), custom_call_target="tpu_custom_call" | custom-call | flops 1073741824 | bytes 32505856 | tf_op jit(solution)/shard_map/deep/pallas_call | solution.py:251
  963.9 31.9 %broad.11 = (bf16[640,4096]{1,0:T(8,128)(2,1)}, bf16[640,4096]{1,0:T(8,128)(2,1)}) custom-call(s32[8]{0:T(128)} %stack.74.starts_ref, bf16[1280,2048]{1,0:T(8,128)(2,1)} %deep.13.a_ref.refs_8_, bf16[512,2048]{1,0:T(8,128)(2,1)} %get-tuple-element.307.refs_4_.rest_0_, bf16[512,2048]{1,0:T(8,128)(2,1)} %stack_rows.13.refs_5_.rest_1_, ...), custom_call_target="tpu_custom_call" | custom-call | flops 1073741824 | bytes 32505856 | tf_op jit(solution)/shard_map/broad/pallas_call | solution.py:286
  1038.8 32.7 %gram.11 = (bf16[512,2048]{1,0:T(8,128)(2,1)}, bf16[512,2048]{1,0:T(8,128)(2,1)}, bf16[512,2048]{1,0:T(8,128)(2,1)}, bf16[512,2048]{1,0:T(8,128)(2,1)}) custom-call(s32[4]{0:T(128)} %constant.156.clone.index_ref, bf16[320,4096]{1,0:T(8,128)(2,1)} %multiply_convert_fusion.refs_0_, bf16[320,4096]{1,0:T(8,128)(2,1)} %collective-permute-done.39.refs_1_, ...), custom_call_target="tpu_custom_call" | custom-call | flops 1073741824 | bytes 52953088 | tf_op jit(solution)/shard_map/gram/pallas_call | solution.py:183
  1071.6 32.6 %gram.10 = (bf16[512,2048]{1,0:T(8,128)(2,1)}, bf16[512,2048]{1,0:T(8,128)(2,1)}, bf16[512,2048]{1,0:T(8,128)(2,1)}, bf16[512,2048]{1,0:T(8,128)(2,1)}) custom-call(s32[4]{0:T(128)} %constant.155.clone.index_ref, bf16[320,4096]{1,0:T(8,128)(2,1)} %multiply_convert_fusion.refs_0_, bf16[320,4096]{1,0:T(8,128)(2,1)} %collective-permute-done.39.refs_1_, ...), custom_call_target="tpu_custom_call" | custom-call | flops 1073741824 | bytes 52953088 | tf_op jit(solution)/shard_map/gram/pallas_call | solution.py:183
  1127.2 32.2 %broad.12 = (bf16[640,4096]{1,0:T(8,128)(2,1)}, bf16[640,4096]{1,0:T(8,128)(2,1)}) custom-call(s32[8]{0:T(128)} %stack.74.starts_ref, bf16[1280,2048]{1,0:T(8,128)(2,1)} %get-tuple-element.417.refs_0_.a_ref, bf16[2048,512]{1,0:T(8,128)(2,1)} %copy-done.3, bf16[2048,512]{1,0:T(8,128)(2,1)} %stack_rows.18.refs_3_.rest_1_, ...), custom_call_target="tpu_custom_call" | custom-call | flops 1073741824 | bytes 32505856 | tf_op jit(solution)/shard_map/broad/pallas_call | solution.py:286
  1159.4 32.2 %broad.13 = (bf16[640,4096]{1,0:T(8,128)(2,1)}, bf16[640,4096]{1,0:T(8,128)(2,1)}) custom-call(s32[8]{0:T(128)} %stack.74.starts_ref, bf16[1280,2048]{1,0:T(8,128)(2,1)} %get-tuple-element.425.refs_1_.a_ref, bf16[2048,512]{1,0:T(8,128)(2,1)} %copy-done.3, bf16[2048,512]{1,0:T(8,128)(2,1)} %stack_rows.18.refs_3_.rest_1_, ...), custom_call_target="tpu_custom_call" | custom-call | flops 1073741824 | bytes 32505856 | tf_op jit(solution)/shard_map/broad/pallas_call | solution.py:286
  1348.3 27.4 %gram.13 = (bf16[512,1536]{1,0:T(8,128)(2,1)}, bf16[512,1536]{1,0:T(8,128)(2,1)}, bf16[512,1536]{1,0:T(8,128)(2,1)}, bf16[512,1536]{1,0:T(8,128)(2,1)}) custom-call(s32[4]{0:T(128)} %constant.156.clone.index_ref, bf16[640,4096]{1,0:T(8,128)(2,1)} %stack_rows.11.refs_0_, bf16[640,4096]{1,0:T(8,128)(2,1)} %collective-permute-done.16.refs_1_, ...), custom_call_target="tpu_custom_call" | custom-call | flops 805306368 | bytes 40370176 | tf_op jit(solution)/shard_map/gram/pallas_call | solution.py:183
  1375.7 27.0 %gram.12 = (bf16[512,1536]{1,0:T(8,128)(2,1)}, bf16[512,1536]{1,0:T(8,128)(2,1)}, bf16[512,1536]{1,0:T(8,128)(2,1)}, bf16[512,1536]{1,0:T(8,128)(2,1)}) custom-call(s32[4]{0:T(128)} %constant.155.clone.index_ref, bf16[640,4096]{1,0:T(8,128)(2,1)} %stack_rows.11.refs_0_, bf16[640,4096]{1,0:T(8,128)(2,1)} %collective-permute-done.16.refs_1_, ...), custom_call_target="tpu_custom_call" | custom-call | flops 805306368 | bytes 40370176 | tf_op jit(solution)/shard_map/gram/pallas_call | solution.py:183
  1440.7 25.3 %broad.14 = (bf16[640,4096]{1,0:T(8,128)(2,1)}, bf16[640,4096]{1,0:T(8,128)(2,1)}) custom-call(s32[8]{0:T(128)} %stack.74.starts_ref, bf16[1280,1536]{1,0:T(8,128)(2,1)} %bitcast.46, bf16[512,1536]{1,0:T(8,128)(2,1)} %get-tuple-element.266.refs_2_.refs_4_.rest_0_, bf16[512,1536]{1,0:T(8,128)(2,1)} %collective-permute-done.4.refs_3_.refs_5_.rest_1_, ...), custom_call_target="tpu_custom_call" | custom-call | flops 805306368 | bytes 27000832 | tf_op jit(solution)/shard_map/broad/pallas_call | solution.py:286
  1495.0 25.2 %broad.15 = (bf16[640,4096]{1,0:T(8,128)(2,1)}, bf16[640,4096]{1,0:T(8,128)(2,1)}) custom-call(s32[8]{0:T(128)} %stack.74.starts_ref, bf16[1280,1536]{1,0:T(8,128)(2,1)} %bitcast.43, bf16[512,1536]{1,0:T(8,128)(2,1)} %get-tuple-element.266.refs_2_.refs_4_.rest_0_, bf16[512,1536]{1,0:T(8,128)(2,1)} %collective-permute-done.4.refs_3_.refs_5_.rest_1_, ...), custom_call_target="tpu_custom_call" | custom-call | flops 805306368 | bytes 27000832 | tf_op jit(solution)/shard_map/broad/pallas_call | solution.py:286
  1537.9 25.8 %collective-permute-done.100 = bf16[512,1536]{1,0:T(8,128)(2,1)} collective-permute-done((bf16[512,1536]{1,0:T(8,128)(2,1)}, bf16[512,1536]{1,0:T(8,128)(2,1)}, u32[]{:S(2)}, u32[]{:S(2)}) %collective-permute-start.100) | collective-permute-done | bytes 1572896 | tf_op jit(solution)/shard_map/ppermute | solution.py:439
  1586.2 73.0 %collective-permute-done.106 = bf16[512,1536]{1,0:T(8,128)(2,1)} collective-permute-done((bf16[512,1536]{1,0:T(8,128)(2,1)}, bf16[512,1536]{1,0:T(8,128)(2,1)}, u32[]{:S(2)}, u32[]{:S(2)}) %collective-permute-start.106) | collective-permute-done | bytes 1572896 | tf_op jit(solution)/shard_map/ppermute | solution.py:439
  1718.6 32.6 %collective-permute-done.115 = bf16[512,1536]{1,0:T(8,128)(2,1)S(1)} collective-permute-done((bf16[512,1536]{1,0:T(8,128)(2,1)S(1)}, bf16[512,1536]{1,0:T(8,128)(2,1)S(1)}, u32[]{:S(2)}, u32[]{:S(2)}) %collective-permute-start.115) | collective-permute-done | bytes 1572896 | tf_op jit(solution)/shard_map/ppermute | solution.py:439
  (559 shorter events, 910.3 us)
Async XLA Ops:
  19.0 82.7 %collective-permute-start.6 = (bf16[512,1536]{1,0:T(8,128)(2,1)}, bf16[512,1536]{1,0:T(8,128)(2,1)}, u32[]{:S(2)}, u32[]{:S(2)}) collective-permute-start(bf16[512,1536]{1,0:T(8,128)(2,1)} %get-tuple-element.266.refs_2_.refs_4_.rest_0_), channel_id=1, source_target_pairs={{0,16},{4,20},{8,24},{12,28},{16,0},{20,4},{24,8},{28,12},{1,17},{... | collective-permute-start | bytes 4718600 | tf_op jit(solution)/shard_map/ppermute | solution.py:439
  22.0 79.8 %collective-permute-start.5 = (bf16[512,1536]{1,0:T(8,128)(2,1)}, bf16[512,1536]{1,0:T(8,128)(2,1)}, u32[]{:S(2)}, u32[]{:S(2)}) collective-permute-start(bf16[512,1536]{1,0:T(8,128)(2,1)} %get-tuple-element.266.refs_2_.refs_4_.rest_0_), channel_id=1, source_target_pairs={{0,4},{4,0},{8,12},{12,8},{16,20},{20,16},{24,28},{28,24},{1,5},{5... | collective-permute-start | bytes 4718600 | tf_op jit(solution)/shard_map/ppermute | solution.py:439
  105.3 88.8 %collective-permute-start.11 = (bf16[320,4096]{1,0:T(8,128)(2,1)}, bf16[320,4096]{1,0:T(8,128)(2,1)}, u32[]{:S(2)}, u32[]{:S(2)}) collective-permute-start(bf16[320,4096]{1,0:T(8,128)(2,1)} %fusion.6.refs_0_), channel_id=1, source_target_pairs={{0,8},{4,12},{8,0},{12,4},{16,24},{20,28},{24,16},{28,20},{1,9},{5... | collective-permute-start | bytes 7864328 | tf_op jit(solution)/shard_map/ppermute | solution.py:439
  452.6 82.1 %collective-permute-start.36 = (bf16[320,4096]{1,0:T(8,128)(2,1)}, bf16[320,4096]{1,0:T(8,128)(2,1)S(1)}, u32[]{:S(2)}, u32[]{:S(2)}) collective-permute-start(bf16[320,4096]{1,0:T(8,128)(2,1)} %add_convert_fusion.16), channel_id=1, source_target_pairs={{0,8},{4,12},{8,0},{12,4},{16,24},{20,28},{24,16},{28,20},{1,9},{5... | collective-permute-start | bytes 7864328 | tf_op jit(solution)/shard_map/ppermute | solution.py:439
  544.2 81.7 %collective-permute-start.41 = (bf16[320,4096]{1,0:T(8,128)(2,1)}, bf16[320,4096]{1,0:T(8,128)(2,1)}, u32[]{:S(2)}, u32[]{:S(2)}) collective-permute-start(bf16[320,4096]{1,0:T(8,128)(2,1)} %multiply_convert_fusion.refs_0_), channel_id=1, source_target_pairs={{0,8},{4,12},{8,0},{12,4},{16,24},{20,28},{24,16},{28,20},{1,9},{5... | collective-permute-start | bytes 7864328 | tf_op jit(solution)/shard_map/ppermute | solution.py:439
  546.2 79.7 %collective-permute-start.40 = (bf16[320,4096]{1,0:T(8,128)(2,1)}, bf16[320,4096]{1,0:T(8,128)(2,1)}, u32[]{:S(2)}, u32[]{:S(2)}) collective-permute-start(bf16[320,4096]{1,0:T(8,128)(2,1)} %multiply_convert_fusion.refs_0_), channel_id=1, source_target_pairs={{0,1},{1,0},{2,3},{3,2},{4,5},{5,4},{6,7},{7,6},{8,9},{9,8},{10,11... | collective-permute-start | bytes 7864328 | tf_op jit(solution)/shard_map/ppermute | solution.py:439
  546.3 79.7 %collective-permute-start.39 = (bf16[320,4096]{1,0:T(8,128)(2,1)}, bf16[320,4096]{1,0:T(8,128)(2,1)}, u32[]{:S(2)}, u32[]{:S(2)}) collective-permute-start(bf16[320,4096]{1,0:T(8,128)(2,1)} %multiply_convert_fusion.refs_0_), channel_id=1, source_target_pairs={{0,2},{1,3},{2,0},{3,1},{4,6},{5,7},{6,4},{7,5},{8,10},{9,11},{10,... | collective-permute-start | bytes 7864328 | tf_op jit(solution)/shard_map/ppermute | solution.py:439
  923.2 99.6 %collective-permute-start.63 = (bf16[320,4096]{1,0:T(8,128)(2,1)}, bf16[320,4096]{1,0:T(8,128)(2,1)}, u32[]{:S(2)}, u32[]{:S(2)}) collective-permute-start(bf16[320,4096]{1,0:T(8,128)(2,1)} %get-tuple-element.566), channel_id=1, source_target_pairs={{0,2},{1,3},{2,0},{3,1},{4,6},{5,7},{6,4},{7,5},{8,10},{9,11},{10,... | collective-permute-start | bytes 7864328 | tf_op jit(solution)/shard_map/ppermute | solution.py:439
  924.7 98.1 %collective-permute-start.66 = (bf16[2048,512]{1,0:T(8,128)(2,1)}, bf16[2048,512]{1,0:T(8,128)(2,1)}, u32[]{:S(2)}, u32[]{:S(2)}) collective-permute-start(bf16[2048,512]{1,0:T(8,128)(2,1)} %get-tuple-element.393), channel_id=1, source_target_pairs={{0,4},{4,0},{8,12},{12,8},{16,20},{20,16},{24,28},{28,24},{1,5},{5... | collective-permute-start | bytes 6291464 | tf_op jit(solution)/shard_map/ppermute | solution.py:439
  925.3 97.4 %collective-permute-start.67 = (bf16[2048,512]{1,0:T(8,128)(2,1)}, bf16[2048,512]{1,0:T(8,128)(2,1)}, u32[]{:S(2)}, u32[]{:S(2)}) collective-permute-start(bf16[2048,512]{1,0:T(8,128)(2,1)} %get-tuple-element.394), channel_id=1, source_target_pairs={{0,4},{4,0},{8,12},{12,8},{16,20},{20,16},{24,28},{28,24},{1,5},{5... | collective-permute-start | bytes 6291464 | tf_op jit(solution)/shard_map/ppermute | solution.py:439
  930.2 92.5 %collective-permute-start.65 = (bf16[1024,512]{1,0:T(8,128)(2,1)}, bf16[1024,512]{1,0:T(8,128)(2,1)}, u32[]{:S(2)}, u32[]{:S(2)}) collective-permute-start(bf16[1024,512]{1,0:T(8,128)(2,1)} %get-tuple-element.392), channel_id=1, source_target_pairs={{0,16},{4,20},{8,24},{12,28},{16,0},{20,4},{24,8},{28,12},{1,17},{... | collective-permute-start | bytes 3145736 | tf_op jit(solution)/shard_map/ppermute | solution.py:439
  1027.4 82.2 %collective-permute-start.70 = (bf16[320,4096]{1,0:T(8,128)(2,1)}, bf16[320,4096]{1,0:T(8,128)(2,1)}, u32[]{:S(2)}, u32[]{:S(2)}) collective-permute-start(bf16[320,4096]{1,0:T(8,128)(2,1)} %add_convert_fusion.11), channel_id=1, source_target_pairs={{0,8},{4,12},{8,0},{12,4},{16,24},{20,28},{24,16},{28,20},{1,9},{5... | collective-permute-start | bytes 7864328 | tf_op jit(solution)/shard_map/ppermute | solution.py:439
  1121.3 81.1 %collective-permute-start.75 = (bf16[320,4096]{1,0:T(8,128)(2,1)S(1)}, bf16[320,4096]{1,0:T(8,128)(2,1)S(1)}, u32[]{:S(2)}, u32[]{:S(2)}) collective-permute-start(bf16[320,4096]{1,0:T(8,128)(2,1)S(1)} %get-tuple-element.420.refs_0_.refs_2_), channel_id=1, source_target_pairs={{0,8},{4,12},{8,0},{12,4},{16,24},{20,28},{24,16},{28,20},{1,9},{5... | collective-permute-start | bytes 7864328 | tf_op jit(solution)/shard_map/ppermute | solution.py:439
  1121.8 80.6 %collective-permute-start.74 = (bf16[320,4096]{1,0:T(8,128)(2,1)S(1)}, bf16[320,4096]{1,0:T(8,128)(2,1)S(1)}, u32[]{:S(2)}, u32[]{:S(2)}) collective-permute-start(bf16[320,4096]{1,0:T(8,128)(2,1)S(1)} %get-tuple-element.420.refs_0_.refs_2_), channel_id=1, source_target_pairs={{0,2},{1,3},{2,0},{3,1},{4,6},{5,7},{6,4},{7,5},{8,10},{9,11},{10,... | collective-permute-start | bytes 7864328 | tf_op jit(solution)/shard_map/ppermute | solution.py:439
  1122.3 80.1 %collective-permute-start.73 = (bf16[320,4096]{1,0:T(8,128)(2,1)S(1)}, bf16[320,4096]{1,0:T(8,128)(2,1)}, u32[]{:S(2)}, u32[]{:S(2)}) collective-permute-start(bf16[320,4096]{1,0:T(8,128)(2,1)S(1)} %get-tuple-element.420.refs_0_.refs_2_), channel_id=1, source_target_pairs={{0,1},{1,0},{2,3},{3,2},{4,5},{5,4},{6,7},{7,6},{8,9},{9,8},{10,11... | collective-permute-start | bytes 7864328 | tf_op jit(solution)/shard_map/ppermute | solution.py:439
  1122.3 78.4 %collective-permute-start.77 = (bf16[512,2048]{1,0:T(8,128)(2,1)}, bf16[512,2048]{1,0:T(8,128)(2,1)}, u32[]{:S(2)}, u32[]{:S(2)}) collective-permute-start(bf16[512,2048]{1,0:T(8,128)(2,1)} %get-tuple-element.423), channel_id=1, source_target_pairs={{0,4},{4,0},{8,12},{12,8},{16,20},{20,16},{24,28},{28,24},{1,5},{5... | collective-permute-start | bytes 6291464 | tf_op jit(solution)/shard_map/ppermute | solution.py:439
  1330.1 79.1 %collective-permute-start.90 = (bf16[320,4096]{1,0:T(8,128)(2,1)}, bf16[320,4096]{1,0:T(8,128)(2,1)}, u32[]{:S(2)}, u32[]{:S(2)}) collective-permute-start(bf16[320,4096]{1,0:T(8,128)(2,1)} %get-tuple-element.451), channel_id=1, source_target_pairs={{0,2},{1,3},{2,0},{3,1},{4,6},{5,7},{6,4},{7,5},{8,10},{9,11},{10,... | collective-permute-start | bytes 7864328 | tf_op jit(solution)/shard_map/ppermute | solution.py:439
  1330.7 80.6 %collective-permute-start.91 = (bf16[320,4096]{1,0:T(8,128)(2,1)S(1)}, bf16[320,4096]{1,0:T(8,128)(2,1)}, u32[]{:S(2)}, u32[]{:S(2)}) collective-permute-start(bf16[320,4096]{1,0:T(8,128)(2,1)S(1)} %add_convert_fusion.6), channel_id=1, source_target_pairs={{0,8},{4,12},{8,0},{12,4},{16,24},{20,28},{24,16},{28,20},{1,9},{5... | collective-permute-start | bytes 7864328 | tf_op jit(solution)/shard_map/ppermute | solution.py:439
  1330.7 78.4 %collective-permute-start.93 = (bf16[512,2048]{1,0:T(8,128)(2,1)}, bf16[512,2048]{1,0:T(8,128)(2,1)}, u32[]{:S(2)}, u32[]{:S(2)}) collective-permute-start(bf16[512,2048]{1,0:T(8,128)(2,1)} %get-tuple-element.456), channel_id=1, source_target_pairs={{0,4},{4,0},{8,12},{12,8},{16,20},{20,16},{24,28},{28,24},{1,5},{5... | collective-permute-start | bytes 6291464 | tf_op jit(solution)/shard_map/ppermute | solution.py:439
  1568.1 93.3 %collective-permute-start.105 = (bf16[320,4096]{1,0:T(8,128)(2,1)}, bf16[320,4096]{1,0:T(8,128)(2,1)}, u32[]{:S(2)}, u32[]{:S(2)}) collective-permute-start(bf16[320,4096]{1,0:T(8,128)(2,1)} %add_convert_fusion), channel_id=1, source_target_pairs={{0,8},{4,12},{8,0},{12,4},{16,24},{20,28},{24,16},{28,20},{1,9},{5... | collective-permute-start | bytes 7864328 | tf_op jit(solution)/shard_map/ppermute | solution.py:439
  1575.8 85.5 %collective-permute-start.104 = (bf16[320,4096]{1,0:T(8,128)(2,1)}, bf16[320,4096]{1,0:T(8,128)(2,1)}, u32[]{:S(2)}, u32[]{:S(2)}) collective-permute-start(bf16[320,4096]{1,0:T(8,128)(2,1)} %get-tuple-element.549), channel_id=1, source_target_pairs={{0,2},{1,3},{2,0},{3,1},{4,6},{5,7},{6,4},{7,5},{8,10},{9,11},{10,... | collective-permute-start | bytes 7864328 | tf_op jit(solution)/shard_map/ppermute | solution.py:439
  1579.5 79.6 %collective-permute-start.106 = (bf16[512,1536]{1,0:T(8,128)(2,1)}, bf16[512,1536]{1,0:T(8,128)(2,1)}, u32[]{:S(2)}, u32[]{:S(2)}) collective-permute-start(bf16[512,1536]{1,0:T(8,128)(2,1)} %add_convert_fusion.23), channel_id=1, source_target_pairs={{0,16},{4,20},{8,24},{12,28},{16,0},{20,4},{24,8},{28,12},{1,17},{... | collective-permute-start | bytes 4718600 | tf_op jit(solution)/shard_map/ppermute | solution.py:439
  1579.5 79.6 %collective-permute-start.107 = (bf16[512,1536]{1,0:T(8,128)(2,1)}, bf16[512,1536]{1,0:T(8,128)(2,1)}, u32[]{:S(2)}, u32[]{:S(2)}) collective-permute-start(bf16[512,1536]{1,0:T(8,128)(2,1)} %get-tuple-element.502), channel_id=1, source_target_pairs={{0,4},{4,0},{8,12},{12,8},{16,20},{20,16},{24,28},{28,24},{1,5},{5... | collective-permute-start | bytes 4718600 | tf_op jit(solution)/shard_map/ppermute | solution.py:439
  1580.2 79.0 %collective-permute-start.108 = (bf16[512,1536]{1,0:T(8,128)(2,1)}, bf16[512,1536]{1,0:T(8,128)(2,1)}, u32[]{:S(2)}, u32[]{:S(2)}) collective-permute-start(bf16[512,1536]{1,0:T(8,128)(2,1)} %get-tuple-element.503), channel_id=1, source_target_pairs={{0,4},{4,0},{8,12},{12,8},{16,20},{20,16},{24,28},{28,24},{1,5},{5... | collective-permute-start | bytes 4718600 | tf_op jit(solution)/shard_map/ppermute | solution.py:439
  (171 other events, 6895.0 us)
